TPU v7x, 128 devices: a whole 4x4x4 slice. The times are simulated.
128 devices in a mesh: dp: 4 (over x), expert: 32 (over z, y, core).
Axes of the slice: x: 4, y: 4, z: 4, core: 2. Of those that a mesh axis runs over, the one named last changes fastest.
Arguments:
- tokens: bfloat16 [10240, 7168], P('expert', 'dp'), may hold values from -6 to 6
- route_ids: int32 [10240, 8], P('expert'), may hold values from 0 to 255, as said below
- route_scores: float32 [10240, 8], P('expert'), may hold values from 0.05 to 1
- partner: int32 [32], replicated, may hold values from 0 to 31, as said below
- w_gate: bfloat16 [32, 7168, 1024], P('expert', None, 'dp'), may hold values from -0.0625 to 0.0625
- w_up: bfloat16 [32, 7168, 1024], P('expert', None, 'dp'), may hold values from -0.0625 to 0.0625
- w_down: bfloat16 [32, 1024, 7168], P('expert', 'dp'), may hold values from -0.5 to 0.5
Outputs:
- mixed: bfloat16 [10240, 7168], P('expert', 'dp')
- placed_gate: bfloat16 [32, 7168, 1024], P('expert', None, 'dp')
- placed_up: bfloat16 [32, 7168, 1024], P('expert', None, 'dp')
- placed_down: bfloat16 [32, 1024, 7168], P('expert', 'dp')
Inputs may be any that keep to these rules, and one draw needn't show every extreme that they name: `route_ids`: each token names 8 different experts, exactly one of them below 32. The 320 tokens of one index of expert name each expert below 32 at most 20 times, and one expert below 32 is named exactly 20 times by the tokens of every index. partner[e] is e or e xor 1, and partner[partner[e]] = e.
All inputs are finite; a program needn't handle non-finite values.
Results may differ from a plain program's by a relative error of at most 0.017.
Values may be sent and summed in bfloat16 or wider, within the bound.
No kernel may reach another device: no remote copies, remote signals or barrier semaphores. Data moves between devices by JAX's collectives and lax.ppermute only.
A program may use at most 192 MiB of HBM per device.

v0:
```python
import jax
import jax.numpy as jnp
from jax import lax
from jax.sharding import PartitionSpec as P


def swapped_2(value, axis, apart):
    return lax.ppermute(value, axis, [(i, i ^ 1 << apart) for i in range(lax.axis_size(axis))])


def body(tokens, route_ids, route_scores, partner, w_gate, w_up, w_down):
    expert_count = lax.axis_size("expert")
    token_rows = tokens.shape[0]
    capacity = 2 * token_rows // expert_count
    slot_count = expert_count * capacity
    own_index = lax.axis_index("expert")
    in_window = route_ids < expert_count
    expert_pick = jnp.sum(jnp.where(in_window, route_ids, 0), axis=1)
    window_score = jnp.sum(jnp.where(in_window, route_scores, jnp.zeros_like(route_scores)), axis=1)
    gate_weight = 2.5 * window_score / jnp.sum(route_scores, axis=1)
    swapped = swapped_2((w_gate, w_up, w_down), "expert", 0)
    is_moved = partner[own_index] != own_index
    placed_gate = jnp.where(is_moved, swapped[0], w_gate)
    placed_up = jnp.where(is_moved, swapped[1], w_up)
    placed_down = jnp.where(is_moved, swapped[2], w_down)
    target = partner[expert_pick]
    gate_matrix, up_matrix, down_matrix = (placed_gate[0], placed_up[0], placed_down[0])
    columns = jnp.arange(expert_count, dtype=jnp.int32)
    one_hot = (target[:, None] == columns[None, :]).astype(jnp.int32)
    slot_rank = jnp.sum((jnp.cumsum(one_hot, axis=0) - 1) * one_hot, axis=1)
    slot_index = target * capacity + slot_rank
    gathered = lax.all_gather(tokens, "dp", axis=1, tiled=True)
    send_buffer = (
        jnp.zeros((slot_count, gathered.shape[1]), jnp.bfloat16).at[slot_index].set(gathered)
    )
    arrived = lax.all_to_all(
        send_buffer.reshape(expert_count, capacity, gathered.shape[1]),
        "expert",
        split_axis=0,
        concat_axis=0,
        tiled=True,
    )
    flat_rows = arrived.reshape(slot_count, gathered.shape[1])
    gate_proj = jnp.dot(flat_rows, gate_matrix, preferred_element_type=jnp.float32)
    up_proj = jnp.dot(flat_rows, up_matrix, preferred_element_type=jnp.float32)
    hidden = (jax.nn.silu(gate_proj) * up_proj).astype(jnp.bfloat16)
    partial_value = jnp.dot(hidden, down_matrix, preferred_element_type=jnp.float32).astype(
        jnp.bfloat16
    )
    returned = lax.all_to_all(
        partial_value.reshape(expert_count, capacity, partial_value.shape[1]),
        "expert",
        split_axis=0,
        concat_axis=0,
        tiled=True,
    )
    own_rows = returned.reshape(slot_count, partial_value.shape[1])[slot_index].astype(jnp.float32)
    term_rows = gate_weight[:, None] * own_rows
    summed = lax.psum_scatter(term_rows.astype(jnp.bfloat16), "dp", scatter_dimension=1, tiled=True)
    return (summed, placed_gate, placed_up, placed_down)


def solution(mesh):
    return jax.shard_map(
        body,
        mesh=mesh,
        in_specs=(
            P("expert", "dp"),
            P("expert", None),
            P("expert", None),
            P(),
            P("expert", None, "dp"),
            P("expert", None, "dp"),
            P("expert", "dp", None),
        ),
        out_specs=(
            P("expert", "dp"),
            P("expert", None, "dp"),
            P("expert", None, "dp"),
            P("expert", "dp", None),
        ),
        check_vma=False,
    )
```

profile of v0, /device:TPU:1, one launch (start us, length us, event | category | flops | bytes accessed | tf_op | source)
XLA Modules:
  0.0 525.6 jit_solution(10358214112548858214)
XLA Ops:
  7.2 0.0 all-gather.2.cloned.1.call-start
  7.2 0.7 all-gather.2.cloned.1.call-update
  7.9 1.5 collective-permute-start.1
  9.4 0.7 fusion.15
  10.1 1.8 fusion.20
  12.0 4.1 fusion.16
  16.0 2.1 fusion.19
  18.1 0.1 compare_reduce_fusion.24
  18.2 15.4 %select_select_fusion = s32[320]{0:T(512)S(1)} fusion(pred[320]{0:T(512)(128)(4,1)S(1)} %get-tuple-element.30, pred[320]{0:T(512)(128)(4,1)S(1)} %get-tuple-element.29, pred[320]{0:T(512)(128)(4,1)S(1)} %get-tuple-element.28, pred[320]{0:T(512)(128)(4,1)S(1)} %get-tuple-element.27, pred[320]{0:T(512)(128)(4,1)S(1)} %get-tuple-element.26, ...), kind=kLoop, calls=%fused_computation.64 | loop fusion | flops 8000 | bytes 10660 | tf_op jit(solution)/shard_map/gather | solution.py:26
  33.7 0.9 reduce-window.6
  34.6 0.2 slice_reduce_fusion
  34.8 0.1 bitcast_bitcast_fusion
  35.0 29.4 %all-gather.2.cloned.1.call-done = bf16[320,7168]{1,0:T(8,128)(2,1)} async-done(((bf16[320,1792]{1,0:T(8,128)(2,1)}), bf16[320,7168]{1,0:T(8,128)(2,1)}) %all-gather.2.cloned.1.call-update) | async-done | bytes 4587536 | tf_op jit(solution)/shard_map/all_gather | solution.py:32
  64.4 13.4 %scatter_custom_fusion = bf16[640,7168]{1,0:T(8,128)(2,1)} fusion(s32[320]{0:T(512)S(1)} %fusion.17, bf16[320,7168]{1,0:T(8,128)(2,1)} %all-gather.2.cloned.1.call-done, bf16[]{:T(256)} %constant.14.clone.1), kind=kCustom, calls=%fused_computation.4 | custom fusion | bytes 9175552 | tf_op jit(solution)/shard_map/scatter | solution.py:34
  77.7 13.2 %reshape.79 = bf16[32,20,7168]{2,1,0:T(8,128)(2,1)} reshape(bf16[640,7168]{1,0:T(8,128)(2,1)} %scatter_custom_fusion) | data formatting | bytes 18350080 | tf_op jit(solution)/shard_map/reshape | solution.py:37
  91.0 7.8 %all-to-all-start = ((bf16[32,20,7168]{2,1,0:T(8,128)(2,1)}), bf16[32,20,7168]{2,1,0:T(8,128)(2,1)}, u32[]{:S(2)}, u32[]{:S(2)}) async-start(bf16[32,20,7168]{2,1,0:T(8,128)(2,1)} %reshape.79), calls=%async_computation | async-start | bytes 22020096 | tf_op jit(solution)/shard_map/all_to_all | solution.py:36
  98.7 0.4 collective-permute-start
  99.1 0.2 collective-permute-start.2
  99.9 0.0 copy-start
  99.9 0.0 collective-permute-done.1
  99.9 4.4 broadcast_select_fusion.1
  104.3 0.0 copy-start.1
  104.3 1.2 collective-permute-done
  105.6 0.0 copy-done
  105.6 4.3 broadcast_select_fusion.2
  109.8 1.0 collective-permute-done.2
  110.8 0.0 copy-done.1
  110.8 4.3 broadcast_select_fusion
  115.1 116.1 %all-to-all-done = bf16[32,20,7168]{2,1,0:T(8,128)(2,1)} async-done(((bf16[32,20,7168]{2,1,0:T(8,128)(2,1)}), bf16[32,20,7168]{2,1,0:T(8,128)(2,1)}, u32[]{:S(2)}, u32[]{:S(2)}) %all-to-all-start) | async-done | bytes 9175072 | tf_op jit(solution)/shard_map/all_to_all | solution.py:36
  231.2 13.3 %reshape.80 = bf16[640,7168]{1,0:T(8,128)(2,1)} reshape(bf16[32,20,7168]{2,1,0:T(8,128)(2,1)} %all-to-all-done) | data formatting | bytes 18350080 | tf_op jit(solution)/shard_map/reshape | solution.py:43
  244.6 7.2 %fusion.3 = f32[640,256]{1,0:T(8,128)S(1)} fusion(bf16[640,7168]{1,0:T(8,128)(2,1)} %reshape.80, bf16[1,7168,256]{2,1,0:T(8,128)(2,1)} %broadcast_select_fusion.1), kind=kOutput, calls=%fused_computation.7 | convolution fusion | flops 2348810240 | bytes 13500416 | tf_op jit(solution)/shard_map/dot_general | solution.py:45
  251.7 18.9 %convolution_convert_fusion = bf16[640,7168]{1,0:T(8,128)(2,1)} fusion(bf16[1,256,7168]{2,1,0:T(8,128)(2,1)} %broadcast_select_fusion, f32[640,256]{1,0:T(8,128)S(1)} %fusion.3, bf16[640,7168]{1,0:T(8,128)(2,1)} %reshape.80, bf16[1,7168,256]{2,1,0:T(8,128)(2,1)} %broadcast_select_fusion.2), kind=kOutput, calls=%fused_computation.2 | convolution fusion | flops 4703191040 | bytes 26345472 | tf_op jit(solution)/shard_map/dot_general | solution.py:47
  270.7 13.2 %reshape.81 = bf16[32,20,7168]{2,1,0:T(8,128)(2,1)} reshape(bf16[640,7168]{1,0:T(8,128)(2,1)} %convolution_convert_fusion) | data formatting | bytes 18350080 | tf_op jit(solution)/shard_map/reshape | solution.py:51
  283.9 0.0 copy-start.2
  283.9 0.0 copy-start.3
  283.9 12.6 %all-to-all-start.1 = ((bf16[32,20,7168]{2,1,0:T(8,128)(2,1)}), bf16[32,20,7168]{2,1,0:T(8,128)(2,1)}, u32[]{:S(2)}, u32[]{:S(2)}) async-start(bf16[32,20,7168]{2,1,0:T(8,128)(2,1)} %reshape.81), calls=%async_computation.1 | async-start | bytes 22020096 | tf_op jit(solution)/shard_map/all_to_all | solution.py:50
  296.5 0.0 reduce-scatter.2.cloned.1.call-start
  296.6 0.0 copy-done.2
  296.6 0.0 copy-done.3
  296.6 131.9 %all-to-all-done.1 = bf16[32,20,7168]{2,1,0:T(8,128)(2,1)} async-done(((bf16[32,20,7168]{2,1,0:T(8,128)(2,1)}), bf16[32,20,7168]{2,1,0:T(8,128)(2,1)}, u32[]{:S(2)}, u32[]{:S(2)}) %all-to-all-start.1) | async-done | bytes 9175072 | tf_op jit(solution)/shard_map/all_to_all | solution.py:50
  428.5 13.3 %reshape.82 = bf16[640,7168]{1,0:T(8,128)(2,1)} reshape(bf16[32,20,7168]{2,1,0:T(8,128)(2,1)} %all-to-all-done.1) | data formatting | bytes 18350080 | tf_op jit(solution)/shard_map/reshape | solution.py:57
  441.9 17.7 %gather_fusion = bf16[320,7168]{1,0:T(8,128)(2,1)} fusion(bf16[640,7168]{1,0:T(8,128)(2,1)} %reshape.82, s32[1024]{0:T(1024)S(1)} %pad_clamp_fusion), kind=kCustom, calls=%fused_computation | custom fusion | bytes 9176320 | tf_op jit(solution)/shard_map/gather | solution.py:57
  459.6 5.6 %multiply_convert_fusion = bf16[320,7168]{1,0:T(8,128)(2,1)} fusion(bf16[320,7168]{1,0:T(8,128)(2,1)} %gather_fusion, f32[320]{0:T(512)S(1)} %multiply_divide_fusion), kind=kLoop, calls=%fused_computation.3 | loop fusion | flops 6881280 | bytes 9176320 | tf_op jit(solution)/shard_map/convert_element_type | solution.py:59
  465.1 0.0 reduce-scatter.2.cloned.1.call-update
  465.2 53.5 %reduce-scatter.2.cloned.1.call-done = bf16[320,1792]{1,0:T(8,128)(2,1)} async-done(((bf16[320,7168]{1,0:T(8,128)(2,1)}), bf16[320,1792]{1,0:T(8,128)(2,1)}) %reduce-scatter.2.cloned.1.call-update) | async-done | bytes 1146896 | tf_op jit(solution)/shard_map/reduce_scatter | solution.py:59
  (9 shorter events, 0.1 us)
Async XLA Ops:
  7.2 57.2 %all-gather.2.cloned.1.call-start = ((), (), s32[]{:S(2)}) async-start(), calls=%async_computation.3 | async-start | bytes 5734400 | tf_op jit(solution)/shard_map/all_gather | solution.py:32
  7.9 92.0 %collective-permute-start.1 = (bf16[1,7168,256]{2,1,0:T(8,128)(2,1)}, bf16[1,7168,256]{2,1,0:T(8,128)(2,1)}, u32[]{:S(2)}, u32[]{:S(2)}) collective-permute-start(bf16[1,7168,256]{2,1,0:T(8,128)(2,1)} %param.12), channel_id=1, source_target_pairs={{0,1},{1,0},{2,3},{3,2},{4,5},{5,4},{6,7},{7,6},{8,9},{9,8},{10,11... | collective-permute-start | bytes 11010056 | tf_op jit(solution)/shard_map/ppermute | solution.py:8
  91.0 140.2 %all-to-all-start = ((bf16[32,20,7168]{2,1,0:T(8,128)(2,1)}), bf16[32,20,7168]{2,1,0:T(8,128)(2,1)}, u32[]{:S(2)}, u32[]{:S(2)}) async-start(bf16[32,20,7168]{2,1,0:T(8,128)(2,1)} %reshape.79), calls=%async_computation | async-start | bytes 22020096 | tf_op jit(solution)/shard_map/all_to_all | solution.py:36
  98.7 6.8 %collective-permute-start = (bf16[1,7168,256]{2,1,0:T(8,128)(2,1)}, bf16[1,7168,256]{2,1,0:T(8,128)(2,1)}, u32[]{:S(2)}, u32[]{:S(2)}) collective-permute-start(bf16[1,7168,256]{2,1,0:T(8,128)(2,1)} %param.11), channel_id=1, source_target_pairs={{0,1},{1,0},{2,3},{3,2},{4,5},{5,4},{6,7},{7,6},{8,9},{9,8},{10,11... | collective-permute-start | bytes 11010056 | tf_op jit(solution)/shard_map/ppermute | solution.py:8
  99.1 11.7 %collective-permute-start.2 = (bf16[1,256,7168]{2,1,0:T(8,128)(2,1)}, bf16[1,256,7168]{2,1,0:T(8,128)(2,1)}, u32[]{:S(2)}, u32[]{:S(2)}) collective-permute-start(bf16[1,256,7168]{2,1,0:T(8,128)(2,1)} %param.13), channel_id=1, source_target_pairs={{0,1},{1,0},{2,3},{3,2},{4,5},{5,4},{6,7},{7,6},{8,9},{9,8},{10,11... | collective-permute-start | bytes 11010056 | tf_op jit(solution)/shard_map/ppermute | solution.py:8
  99.9 5.7 %copy-start = (bf16[1,7168,256]{2,1,0:T(8,128)(2,1)S(1)}, bf16[1,7168,256]{2,1,0:T(8,128)(2,1)}, u32[]{:S(2)}) copy-start(bf16[1,7168,256]{2,1,0:T(8,128)(2,1)} %param.11) | copy-start | bytes 11010052
  104.3 6.5 %copy-start.1 = (bf16[1,256,7168]{2,1,0:T(8,128)(2,1)S(1)}, bf16[1,256,7168]{2,1,0:T(8,128)(2,1)}, u32[]{:S(2)}) copy-start(bf16[1,256,7168]{2,1,0:T(8,128)(2,1)} %param.13) | copy-start | bytes 11010052
  283.9 12.7 %copy-start.2 = (s32[320,8]{0,1:T(8,128)S(1)}, s32[320,8]{0,1:T(8,128)}, u32[]{:S(2)}) copy-start(s32[320,8]{0,1:T(8,128)} %param.8) | copy-start | bytes 30724
  283.9 12.7 %copy-start.3 = (f32[320,8]{0,1:T(8,128)S(1)}, f32[320,8]{0,1:T(8,128)}, u32[]{:S(2)}) copy-start(f32[320,8]{0,1:T(8,128)} %param.9) | copy-start | bytes 30724
  283.9 144.6 %all-to-all-start.1 = ((bf16[32,20,7168]{2,1,0:T(8,128)(2,1)}), bf16[32,20,7168]{2,1,0:T(8,128)(2,1)}, u32[]{:S(2)}, u32[]{:S(2)}) async-start(bf16[32,20,7168]{2,1,0:T(8,128)(2,1)} %reshape.81), calls=%async_computation.1 | async-start | bytes 22020096 | tf_op jit(solution)/shard_map/all_to_all | solution.py:50
  296.5 222.2 %reduce-scatter.2.cloned.1.call-start = ((), (), s32[]{:S(2)}) async-start(), calls=%async_computation.4 | async-start | bytes 5734400 | tf_op jit(solution)/shard_map/reduce_scatter | solution.py:59
Sparse Core Ops, SparseCore 0:
  9.7 54.6 all-gather.1
  465.3 53.3 reduce-scatter.1
where the time goes:
time: 528 us; the launch traced here: 526 us
  waiting for transfers between devices  334 us (63%)
  local copies, waits for them, and re-layouts  88.3 us (17%)
  other arithmetic  40 us (8%)
  matrix products  26.1 us (5%)
  starting transfers between devices  22.5 us (4%)
  between operations  14.7 us (3%)
    all_to_all x1, waiting for transfers between devices, body(): lax.all_to_all(partial_value.reshape(expert_count, capacity, partial_valu...  132 us
    all_to_all x1, waiting for transfers between devices, body(): lax.all_to_all(send_buffer.reshape(expert_count, capacity, gathered.shape...  116 us
    reduce_scatter x1, waiting for transfers between devices, body(): lax.psum_scatter(term_rows.astype(jnp.bfloat16), 'dp', scatter_dimension=...  53.5 us
    all_gather x1, waiting for transfers between devices, body(): gathered = lax.all_gather(tokens, 'dp', axis=1, tiled=True)  29.4 us
    gather x3, other arithmetic, body(): target = partner[expert_pick]  19.6 us
    dot_general x1, matrix products, body(): jnp.dot(hidden, down_matrix, preferred_element_type=jnp.float32)  18.9 us
    gather x1, local copies, waits for them, and re-layouts, body(): returned.reshape(slot_count, partial_value.shape[1])[slot_index]  17.7 us
    scatter x1, local copies, waits for them, and re-layouts, body(): jnp.zeros((slot_count, gathered.shape[1]), jnp.bfloat16).at[slot_index]  13.4 us
  transfers between devices with their start and end apart: 7, of which 6 were waited for; matrix products, arithmetic and copies ran while one was open for 12% of the time, Pallas kernels for 0%

commit v1 on v0

v1 whole, which is shorter than its diff:
```python
import jax
import jax.numpy as jnp
from jax import lax
from jax.sharding import PartitionSpec as P

CHUNKS = (8, 12)
SEND_SLOTS = 24
CAP = 20


def shifted(value, step):
    size = lax.axis_size("dp")
    return lax.ppermute(value, "dp", [(i, (i + step) % size) for i in range(size)])


def swapped(value):
    return lax.ppermute(value, "expert", [(i, i ^ 1) for i in range(lax.axis_size("expert"))])


def dot32(left, right):
    return jnp.dot(left, right, preferred_element_type=jnp.float32)


def ring_gather(rows):
    half = rows.shape[0] // 2
    first, second = rows[:half], rows[half:]
    left_first, right_second = shifted(first, 1), shifted(second, -1)
    left_second, right_first = shifted(second, 1), shifted(first, -1)
    far_first, far_second = shifted(left_first, 1), shifted(right_second, -1)
    return (
        (first, left_first, right_first, far_first),
        (second, left_second, right_second, far_second),
    )


def body(tokens, route_ids, route_scores, partner, w_gate, w_up, w_down):
    experts = lax.axis_size("expert")
    ring = lax.axis_size("dp")
    place = lax.axis_index("dp")
    own_index = lax.axis_index("expert")
    token_rows, width = tokens.shape
    offsets = (0, -1, 1, 2)

    in_window = route_ids < experts
    expert_pick = jnp.sum(jnp.where(in_window, route_ids, 0), axis=1)
    window_score = jnp.sum(jnp.where(in_window, route_scores, jnp.zeros_like(route_scores)), axis=1)
    gate_weight = 2.5 * window_score / jnp.sum(route_scores, axis=1)
    one_hot = expert_pick[:, None] == jnp.arange(experts, dtype=jnp.int32)[None, :]
    order = jnp.arange(token_rows, dtype=jnp.int32)
    earlier = (order[:, None] > order[None, :]).astype(jnp.bfloat16)
    counts = dot32(earlier, one_hot.astype(jnp.bfloat16))
    rank = jnp.sum(jnp.where(one_hot, counts, 0.0), axis=1).astype(jnp.int32)

    def columns(offset):
        start = ((place + offset) % ring) * width
        return lax.dynamic_slice(w_down[0], (0, start), (w_down.shape[1], width))

    down = jnp.concatenate(
        [
            columns(0),
            shifted(columns(1), 1),
            shifted(columns(-1), -1),
            shifted(columns(2), 2),
        ],
        axis=0,
    )
    in_weights = []
    for offset in offsets:
        start = ((place + offset) % ring) * width
        size = (width, w_gate.shape[2])
        in_weights.append(
            jnp.concatenate(
                [
                    lax.dynamic_slice(w_gate[0], (start, 0), size),
                    lax.dynamic_slice(w_up[0], (start, 0), size),
                ],
                axis=1,
            )
        )

    slot = expert_pick * SEND_SLOTS + rank
    slots = jnp.arange(experts * SEND_SLOTS, dtype=jnp.int32)
    spread = (slots[:, None] == slot[None, :]).astype(jnp.bfloat16)
    send = dot32(spread, tokens).astype(jnp.bfloat16).reshape(experts, SEND_SLOTS, width)
    arrived = lax.all_to_all(send, "expert", split_axis=0, concat_axis=0, tiled=True)

    moved = partner[own_index] != own_index
    placed = [jnp.where(moved, swapped(w), w) for w in (w_gate, w_up, w_down)]

    total = jnp.zeros((token_rows, width), jnp.float32)
    hidden_width = w_gate.shape[2]
    low = 0
    for size in CHUNKS:
        rows = arrived[:, low : low + size].reshape(experts * size, width)
        outs = []
        hidden = []
        for shards in ring_gather(rows):
            both = sum(dot32(s, w) for s, w in zip(shards, in_weights))
            gate_proj, up_proj = both[:, :hidden_width], both[:, hidden_width:]
            hidden.append((jax.nn.silu(gate_proj) * up_proj).astype(jnp.bfloat16))
        hidden = jnp.concatenate(hidden, axis=0)
        all_hidden = jnp.concatenate(
            [hidden, shifted(hidden, 1), shifted(hidden, -1), shifted(hidden, 2)], axis=1
        )
        out = dot32(all_hidden, down).astype(jnp.bfloat16)
        back = lax.all_to_all(
            out.reshape(experts, size, width), "expert", split_axis=0, concat_axis=0, tiled=True
        ).reshape(experts * size, width)
        spot = jnp.where(
            (rank >= low) & (rank < low + size), expert_pick * size + rank - low, -1
        )
        pick = spot[:, None] == jnp.arange(experts * size, dtype=jnp.int32)[None, :]
        total = total + dot32(pick.astype(jnp.bfloat16), back)
        low += size
    mixed = (gate_weight[:, None] * total).astype(jnp.bfloat16)
    return (mixed, *placed)


def solution(mesh):
    weights = (P("expert", None, "dp"), P("expert", None, "dp"), P("expert", "dp", None))
    return jax.shard_map(
        body,
        mesh=mesh,
        in_specs=(P("expert", "dp"), P("expert", None), P("expert", None), P(), *weights),
        out_specs=(P("expert", "dp"), *weights),
        check_vma=False,
    )
```

time: 528 us -> 266 us (0.50)
  waiting for transfers between devices: 334 us -> 143 us
  local copies, waits for them, and re-layouts: 88.3 us -> 22.1 us
  starting transfers between devices: 22.5 us -> 53.2 us
  other arithmetic: 40 us -> 11.8 us
  between operations: 14.7 us -> 1.79 us
  matrix products: 26.1 us -> 31.9 us
    all_to_all x2 -> x3, waiting for transfers between devices: 248 us -> 39.5 us  [the longest x2 20.2 us: body(): lax.all_to_all(out.reshape(experts, size, width), 'expert', split_axis=0,...]
    ppermute x3 -> x24, waiting for transfers between devices: 2.22 us -> 103 us  [the longest x21 103 us: shifted(): lax.ppermute(value, 'dp', [(i, (i + step) % size) for i in range(size)])]
    reduce_scatter x1 -> x0, waiting for transfers between devices: 53.5 us -> none  [body(): lax.psum_scatter(term_rows.astype(jnp.bfloat16), 'dp', scatter_dimension=...]
    reshape x4 -> x2, local copies, waits for them, and re-layouts: 53.2 us -> 4.91 us  [the longest x1 3.5 us: body(): back = lax.all_to_all(out.reshape(experts, size, width), 'expert', split_...]
    all_gather x1 -> x0, waiting for transfers between devices: 29.4 us -> none  [body(): gathered = lax.all_gather(tokens, 'dp', axis=1, tiled=True)]
    ppermute x3 -> x24, starting transfers between devices: 2.09 us -> 25.2 us  [the longest x21 19.8 us: shifted(): lax.ppermute(value, 'dp', [(i, (i + step) % size) for i in range(size)])]
    gather x3 -> x0, local copies, waits for them, and re-layouts: 21.6 us -> none  [the longest x1 17.7 us: body(): returned.reshape(slot_count, partial_value.shape[1])[slot_index]]
    gather x4 -> x0, other arithmetic: 19.6 us -> none  [the longest x3 19.6 us: body(): target = partner[expert_pick]]
  transfers between devices with their start and end apart: 7 -> 27, of which waited for: 6 -> 13; matrix products, arithmetic and copies ran while one was open for 12% -> 21% of each run, Pallas kernels for 0% -> 0%
where the time goes in v1:
time: 266 us; the launch traced here: 264 us
  waiting for transfers between devices  143 us (54%)
  starting transfers between devices  53.2 us (20%)
  matrix products  31.9 us (12%)
  local copies, waits for them, and re-layouts  22.1 us (8%)
  other arithmetic  11.8 us (4%)
    ppermute x21, waiting for transfers between devices, shifted(): lax.ppermute(value, 'dp', [(i, (i + step) % size) for i in range(size)])  103 us
    dot_general x22, matrix products, dot32(): return jnp.dot(left, right, preferred_element_type=jnp.float32)  31.9 us
    all_to_all x2, waiting for transfers between devices, body(): lax.all_to_all(out.reshape(experts, size, width), 'expert', split_axis=0,...  20.2 us
    ppermute x21, starting transfers between devices, shifted(): lax.ppermute(value, 'dp', [(i, (i + step) % size) for i in range(size)])  19.8 us
    all_to_all x1, waiting for transfers between devices, body(): lax.all_to_all(send, 'expert', split_axis=0, concat_axis=0, tiled=True)  19.4 us
    all_to_all x2, starting transfers between devices, body(): lax.all_to_all(out.reshape(experts, size, width), 'expert', split_axis=0,...  18.3 us
    select_n x3, other arithmetic, body(): placed = [jnp.where(moved, swapped(w), w) for w in (w_gate, w_up, w_down)]  10.7 us
    all_to_all x1, starting transfers between devices, body(): lax.all_to_all(send, 'expert', split_axis=0, concat_axis=0, tiled=True)  9.65 us
  transfers between devices with their start and end apart: 27, of which 13 were waited for; matrix products, arithmetic and copies ran while one was open for 21% of the time, Pallas kernels for 0%

profile of v1, /device:TPU:1, one launch (start us, length us, event | category | flops | bytes accessed | tf_op | source)
XLA Modules:
  0.0 263.8 jit_solution(14768257220532690283)
XLA Ops:
  1.9 3.1 %convolution_convert_fusion = bf16[768,1792]{1,0:T(8,128)(2,1)} fusion(bf16[320,1792]{1,0:T(8,128)(2,1)S(1)} %copy-done, s32[320]{0:T(512)S(1)} %get-tuple-element.23), kind=kOutput, calls=%fused_computation.4 | convolution fusion | flops 882425856 | bytes 3900672 | tf_op jit(solution)/shard_map/dot_general | solution.py:21
  5.0 9.7 %all-to-all-start = ((bf16[32,24,1792]{2,1,0:T(8,128)(2,1)}), bf16[32,24,1792]{2,1,0:T(8,128)(2,1)}, u32[]{:S(2)}, u32[]{:S(2)}) async-start(bf16[32,24,1792]{2,1,0:T(8,128)(2,1)} %bitcast.53), calls=%async_computation | async-start | bytes 5505024 | tf_op jit(solution)/shard_map/all_to_all | solution.py:85
  15.1 3.6 %dynamic-slice_bitcast_fusion.3 = (bf16[256,1792]{1,0:T(8,128)(2,1)S(1)}, bf16[256,1792]{1,0:T(8,128)(2,1)}, bf16[256,1792]{1,0:T(8,128)(2,1)}, bf16[256,1792]{1,0:T(8,128)(2,1)}) fusion(bf16[1,256,7168]{2,1,0:T(8,128)(2,1)} %param.13, s32[]{:T(128)S(6)} %select_n.102, s32[]{:T(128)S(6)} %select_n.108, s32[]{:T(128)S(6)} %select_n.104, s32[]{:T(128)S(6)} %select_n.106), kind=kLoop, calls=%fused_computation.35 | loop fusion | bytes 7340048 | tf_op jit(solution)/shard_map/dynamic_slice | solution.py:56
  18.7 2.5 collective-permute-start.10
  22.6 3.9 %dynamic-slice_bitcast_fusion.4 = (bf16[1792,256]{1,0:T(8,128)(2,1)}, bf16[1792,256]{1,0:T(8,128)(2,1)}, bf16[1792,256]{1,0:T(8,128)(2,1)}, bf16[1792,256]{1,0:T(8,128)(2,1)}) fusion(bf16[1,7168,256]{2,1,0:T(8,128)(2,1)} %param.12, s32[]{:T(128)S(6)} %select_n.108, s32[]{:T(128)S(6)} %select_n.106, s32[]{:T(128)S(6)} %select_n.104, s32[]{:T(128)S(6)} %select_n.102), kind=kLoop, calls=%fused_computation.36 | loop fusion | bytes 7340048 | tf_op jit(solution)/shard_map/dynamic_slice | solution.py:75
  26.5 3.9 %dynamic-slice_bitcast_fusion.5 = (bf16[1792,256]{1,0:T(8,128)(2,1)}, bf16[1792,256]{1,0:T(8,128)(2,1)}, bf16[1792,256]{1,0:T(8,128)(2,1)}, bf16[1792,256]{1,0:T(8,128)(2,1)}) fusion(bf16[1,7168,256]{2,1,0:T(8,128)(2,1)} %param.11, s32[]{:T(128)S(6)} %select_n.108, s32[]{:T(128)S(6)} %select_n.106, s32[]{:T(128)S(6)} %select_n.104, s32[]{:T(128)S(6)} %select_n.102), kind=kLoop, calls=%fused_computation.37 | loop fusion | bytes 7340048 | tf_op jit(solution)/shard_map/dynamic_slice | solution.py:74
  30.4 19.4 %all-to-all-done = bf16[32,24,1792]{2,1,0:T(8,128)(2,1)} async-done(((bf16[32,24,1792]{2,1,0:T(8,128)(2,1)}), bf16[32,24,1792]{2,1,0:T(8,128)(2,1)}, u32[]{:S(2)}, u32[]{:S(2)}) %all-to-all-start) | async-done | bytes 2752544 | tf_op jit(solution)/shard_map/all_to_all | solution.py:85
  49.7 1.6 fusion.42
  54.5 2.3 fusion.41
  56.9 1.2 slice_bitcast_fusion.1
  58.1 1.6 fusion.40
  59.7 1.3 collective-permute-start
  61.9 1.4 fusion.38
  63.4 1.6 fusion.39
  64.9 12.8 %collective-permute-done = bf16[128,1792]{1,0:T(8,128)(2,1)S(1)} collective-permute-done((bf16[128,1792]{1,0:T(8,128)(2,1)S(1)}, bf16[128,1792]{1,0:T(8,128)(2,1)S(1)}, u32[]{:S(2)}, u32[]{:S(2)}) %collective-permute-start) | collective-permute-done | bytes 458784 | tf_op jit(solution)/shard_map/ppermute | solution.py:13
  77.8 1.3 collective-permute-start.1
  79.5 8.1 %collective-permute-done.3 = bf16[128,1792]{1,0:T(8,128)(2,1)S(1)} collective-permute-done((bf16[128,1792]{1,0:T(8,128)(2,1)S(1)}, bf16[128,1792]{1,0:T(8,128)(2,1)S(1)}, u32[]{:S(2)}, u32[]{:S(2)}) %collective-permute-start.3) | collective-permute-done | bytes 458784 | tf_op jit(solution)/shard_map/ppermute | solution.py:13
  87.6 1.3 collective-permute-start.4
  90.3 9.9 %collective-permute-done.4 = bf16[128,1792]{1,0:T(8,128)(2,1)S(1)} collective-permute-done((bf16[128,1792]{1,0:T(8,128)(2,1)S(1)}, bf16[128,1792]{1,0:T(8,128)(2,1)S(1)}, u32[]{:S(2)}, u32[]{:S(2)}) %collective-permute-start.4) | collective-permute-done | bytes 458784 | tf_op jit(solution)/shard_map/ppermute | solution.py:13
  100.6 2.7 %collective-permute-start.16 = (bf16[192,1792]{1,0:T(8,128)(2,1)}, bf16[192,1792]{1,0:T(8,128)(2,1)}, u32[]{:S(2)}, u32[]{:S(2)}) collective-permute-start(bf16[192,1792]{1,0:T(8,128)(2,1)} %slice.67), channel_id=1, source_target_pairs={{0,96},{32,0},{64,32},{96,64},{1,97},{33,1},{65,33},{97,65},{2,98}... | collective-permute-start | bytes 2064392 | tf_op jit(solution)/shard_map/ppermute | solution.py:13
  103.4 1.6 convolution_add_fusion.6
  105.0 9.9 %collective-permute-done.13 = bf16[192,1792]{1,0:T(8,128)(2,1)S(1)} collective-permute-done((bf16[192,1792]{1,0:T(8,128)(2,1)S(1)}, bf16[192,1792]{1,0:T(8,128)(2,1)S(1)}, u32[]{:S(2)}, u32[]{:S(2)}) %collective-permute-start.13) | collective-permute-done | bytes 688160 | tf_op jit(solution)/shard_map/ppermute | solution.py:13
  115.0 1.5 collective-permute-start.11
  116.5 1.3 convolution_add_fusion.5
  117.8 1.5 collective-permute-start.2
  119.9 9.9 %collective-permute-done.16 = bf16[192,1792]{1,0:T(8,128)(2,1)} collective-permute-done((bf16[192,1792]{1,0:T(8,128)(2,1)}, bf16[192,1792]{1,0:T(8,128)(2,1)}, u32[]{:S(2)}, u32[]{:S(2)}) %collective-permute-start.16) | collective-permute-done | bytes 688160 | tf_op jit(solution)/shard_map/ppermute | solution.py:13
  129.8 2.4 convolution_add_fusion.2
  132.2 17.3 %collective-permute-done.2 = bf16[128,1792]{1,0:T(8,128)(2,1)S(1)} collective-permute-done((bf16[128,1792]{1,0:T(8,128)(2,1)S(1)}, bf16[128,1792]{1,0:T(8,128)(2,1)S(1)}, u32[]{:S(2)}, u32[]{:S(2)}) %collective-permute-start.2) | collective-permute-done | bytes 458784 | tf_op jit(solution)/shard_map/ppermute | solution.py:13
  150.0 7.9 %collective-permute-done.5 = bf16[128,1792]{1,0:T(8,128)(2,1)S(1)} collective-permute-done((bf16[128,1792]{1,0:T(8,128)(2,1)S(1)}, bf16[128,1792]{1,0:T(8,128)(2,1)S(1)}, u32[]{:S(2)}, u32[]{:S(2)}) %collective-permute-start.5) | collective-permute-done | bytes 458784 | tf_op jit(solution)/shard_map/ppermute | solution.py:13
  157.9 4.5 %collective-permute-start.22 = (bf16[1,7168,256]{2,1,0:T(8,128)(2,1)}, bf16[1,7168,256]{2,1,0:T(8,128)(2,1)}, u32[]{:S(2)}, u32[]{:S(2)}) collective-permute-start(bf16[1,7168,256]{2,1,0:T(8,128)(2,1)} %param.12), channel_id=1, source_target_pairs={{0,1},{1,0},{2,3},{3,2},{4,5},{5,4},{6,7},{7,6},{8,9},{9,8},{10,11... | collective-permute-start | bytes 11010056 | tf_op jit(solution)/shard_map/ppermute | solution.py:17
  163.9 5.2 %collective-permute-done.9 = bf16[256,1792]{1,0:T(8,128)(2,1)S(1)} collective-permute-done((bf16[256,1792]{1,0:T(8,128)(2,1)S(1)}, bf16[256,1792]{1,0:T(8,128)(2,1)S(1)}, u32[]{:S(2)}, u32[]{:S(2)}) %collective-permute-start.9) | collective-permute-done | bytes 917536 | tf_op jit(solution)/shard_map/ppermute | solution.py:13
  169.9 2.2 broadcast_select_fusion
  172.1 15.7 %collective-permute-done.6 = bf16[256,256]{1,0:T(8,128)(2,1)S(1)} collective-permute-done((bf16[256,256]{1,0:T(8,128)(2,1)S(1)}, bf16[256,256]{1,0:T(8,128)(2,1)S(1)}, u32[]{:S(2)}, u32[]{:S(2)}) %collective-permute-start.6) | collective-permute-done | bytes 131104 | tf_op jit(solution)/shard_map/ppermute | solution.py:13
  188.8 3.2 %fusion.2 = bf16[32,8,1792]{2,1,0:T(8,128)(2,1)} fusion(bf16[256,1792]{1,0:T(8,128)(2,1)S(1)} %collective-permute-done.11, bf16[256,1792]{1,0:T(8,128)(2,1)} %collective-permute-done.10, bf16[256,1792]{1,0:T(8,128)(2,1)S(1)} %collective-permute-done.9, bf16[256,1792]{1,0:T(8,128)(2,1)S(1)} %get-tuple-element.14, ...), kind=kOutput, calls=%fused_computation.10 | convolution fusion | flops 957284352 | bytes 5111808 | tf_op jit(solution)/shard_map/dot_general | solution.py:21
  192.0 9.1 %all-to-all-start.1 = ((bf16[32,8,1792]{2,1,0:T(8,128)(2,1)}), bf16[32,8,1792]{2,1,0:T(8,128)(2,1)S(1)}, u32[]{:S(2)}, u32[]{:S(2)}) async-start(bf16[32,8,1792]{2,1,0:T(8,128)(2,1)} %fusion.2), calls=%async_computation.1 | async-start | bytes 1835008 | tf_op jit(solution)/shard_map/all_to_all | solution.py:106
  201.2 2.1 convolution_add_fusion.4
  203.3 2.4 collective-permute-done.17
  205.8 1.6 convolution_add_fusion.1
  207.6 2.7 %collective-permute-start.19 = (bf16[384,256]{1,0:T(8,128)(2,1)S(1)}, bf16[384,256]{1,0:T(8,128)(2,1)S(1)}, u32[]{:S(2)}, u32[]{:S(2)}) collective-permute-start(bf16[384,256]{1,0:T(8,128)(2,1)S(1)} %pad_maximum_fusion.7), channel_id=1, source_target_pairs={{0,96},{32,0},{64,32},{96,64},{1,97},{33,1},{65,33},{97,65},{2,98}... | collective-permute-start | bytes 589832 | tf_op jit(solution)/shard_map/ppermute | solution.py:13
  210.4 4.3 %broadcast_select_fusion.1 = bf16[1,7168,256]{2,1,0:T(8,128)(2,1)} fusion(bf16[1,7168,256]{2,1,0:T(8,128)(2,1)} %collective-permute-done.22, bf16[1,7168,256]{2,1,0:T(8,128)(2,1)} %param.12, pred[]{:T(512)S(6)} %ne.33), kind=kLoop, calls=%fused_computation.2 | loop fusion | flops 1835008 | bytes 11010049 | tf_op jit(solution)/shard_map/jit(_where)/select_n | solution.py:88
  214.7 4.1 %collective-permute-done.20 = bf16[384,256]{1,0:T(8,128)(2,1)S(1)} collective-permute-done((bf16[384,256]{1,0:T(8,128)(2,1)S(1)}, bf16[384,256]{1,0:T(8,128)(2,1)S(1)}, u32[]{:S(2)}, u32[]{:S(2)}) %collective-permute-start.20) | collective-permute-done | bytes 196640 | tf_op jit(solution)/shard_map/ppermute | solution.py:13
  218.8 2.8 %convolution_convert_fusion.1 = bf16[384,1792]{1,0:T(8,128)(2,1)S(1)} fusion(bf16[384,256]{1,0:T(8,128)(2,1)S(1)} %collective-permute-done.20, bf16[384,256]{1,0:T(8,128)(2,1)S(1)} %collective-permute-done.19, bf16[384,256]{1,0:T(8,128)(2,1)S(1)} %collective-permute-done.18, bf16[192,256]{1,0:T(8,128)(2,1)S(1)} %fusion.26, bf16[192,256]{1,0:T(8,128)(2,1)S(1)} %fusion.27, ...), kind=kOutput, calls=%fused_computation.7 | convolution fusion | flops 1428586496 | bytes 5832704 | tf_op jit(solution)/shard_map/dot_general | solution.py:21
  221.5 1.4 reshape.80
  223.0 9.2 %all-to-all-start.2 = ((bf16[32,12,1792]{2,1,0:T(8,128)(2,1)}), bf16[32,12,1792]{2,1,0:T(8,128)(2,1)}, u32[]{:S(2)}, u32[]{:S(2)}) async-start(bf16[32,12,1792]{2,1,0:T(8,128)(2,1)} %reshape.80), calls=%async_computation.2 | async-start | bytes 3670016 | tf_op jit(solution)/shard_map/all_to_all | solution.py:106
  232.2 4.3 %broadcast_select_fusion.2 = bf16[1,7168,256]{2,1,0:T(8,128)(2,1)} fusion(bf16[1,7168,256]{2,1,0:T(8,128)(2,1)} %collective-permute-done.21, bf16[1,7168,256]{2,1,0:T(8,128)(2,1)} %param.11, pred[]{:T(512)S(6)} %ne.33), kind=kLoop, calls=%fused_computation.3 | loop fusion | flops 1835008 | bytes 11010049 | tf_op jit(solution)/shard_map/jit(_where)/select_n | solution.py:88
  237.0 20.2 %all-to-all-done.2 = bf16[32,12,1792]{2,1,0:T(8,128)(2,1)} async-done(((bf16[32,12,1792]{2,1,0:T(8,128)(2,1)}), bf16[32,12,1792]{2,1,0:T(8,128)(2,1)}, u32[]{:S(2)}, u32[]{:S(2)}) %all-to-all-start.2) | async-done | bytes 1376288 | tf_op jit(solution)/shard_map/all_to_all | solution.py:106
  257.1 3.5 %reshape.81 = bf16[384,1792]{1,0:T(8,128)(2,1)} reshape(bf16[32,12,1792]{2,1,0:T(8,128)(2,1)} %all-to-all-done.2) | data formatting | bytes 2752512 | tf_op jit(solution)/shard_map/reshape | solution.py:108
  260.6 3.1 %fusion.1 = bf16[320,1792]{1,0:T(8,128)(2,1)} fusion(f32[320,1792]{1,0:T(8,128)S(1)} %fusion.4, bf16[384,1792]{1,0:T(8,128)(2,1)} %reshape.81, f32[320]{0:T(512)S(1)} %multiply_divide_fusion, s32[320]{0:T(512)S(1)} %get-tuple-element.22), kind=kOutput, calls=%fused_computation.8 | convolution fusion | flops 442245120 | bytes 4819456 | tf_op jit(solution)/shard_map/dot_general | solution.py:21
  (97 shorter events, 13.8 us)
Async XLA Ops:
  5.0 44.7 %all-to-all-start = ((bf16[32,24,1792]{2,1,0:T(8,128)(2,1)}), bf16[32,24,1792]{2,1,0:T(8,128)(2,1)}, u32[]{:S(2)}, u32[]{:S(2)}) async-start(bf16[32,24,1792]{2,1,0:T(8,128)(2,1)} %bitcast.53), calls=%async_computation | async-start | bytes 5505024 | tf_op jit(solution)/shard_map/all_to_all | solution.py:85
  14.7 154.4 %collective-permute-start.23 = (bf16[1,256,7168]{2,1,0:T(8,128)(2,1)}, bf16[1,256,7168]{2,1,0:T(8,128)(2,1)}, u32[]{:S(2)}, u32[]{:S(2)}) collective-permute-start(bf16[1,256,7168]{2,1,0:T(8,128)(2,1)} %param.13), channel_id=1, source_target_pairs={{0,1},{1,0},{2,3},{3,2},{4,5},{5,4},{6,7},{7,6},{8,9},{9,8},{10,11... | collective-permute-start | bytes 11010056 | tf_op jit(solution)/shard_map/ppermute | solution.py:17
  15.1 6.1 %copy-start.21 = (s32[32]{0:T(128)S(1)}, s32[32]{0:T(128)}, u32[]{:S(2)}) copy-start(s32[32]{0:T(128)} %param.10) | copy-start | bytes 388
  15.1 7.5 %copy-start.15 = (s32[320,8]{0,1:T(8,128)S(1)}, s32[320,8]{0,1:T(8,128)}, u32[]{:S(2)}) copy-start(s32[320,8]{0,1:T(8,128)} %param.8) | copy-start | bytes 30724
  15.1 7.5 %copy-start.16 = (f32[320,8]{0,1:T(8,128)S(1)}, f32[320,8]{0,1:T(8,128)}, u32[]{:S(2)}) copy-start(f32[320,8]{0,1:T(8,128)} %param.9) | copy-start | bytes 30724
  18.7 144.2 %collective-permute-start.10 = (bf16[256,1792]{1,0:T(8,128)(2,1)}, bf16[256,1792]{1,0:T(8,128)(2,1)}, u32[]{:S(2)}, u32[]{:S(2)}) collective-permute-start(bf16[256,1792]{1,0:T(8,128)(2,1)} %get-tuple-element.16), channel_id=1, source_target_pairs={{0,96},{32,0},{64,32},{96,64},{1,97},{33,1},{65,33},{97,65},{2,98}... | collective-permute-start | bytes 2752520 | tf_op jit(solution)/shard_map/ppermute | solution.py:13
  52.3 48.3 %collective-permute-start.12 = (bf16[192,1792]{1,0:T(8,128)(2,1)}, bf16[192,1792]{1,0:T(8,128)(2,1)}, u32[]{:S(2)}, u32[]{:S(2)}) collective-permute-start(bf16[192,1792]{1,0:T(8,128)(2,1)} %slice.63), channel_id=1, source_target_pairs={{0,32},{32,64},{64,96},{96,0},{1,33},{33,65},{65,97},{97,1},{2,34}... | collective-permute-start | bytes 2064392 | tf_op jit(solution)/shard_map/ppermute | solution.py:13
  54.5 3.6 %copy-start.13 = (bf16[1792,256]{1,0:T(8,128)(2,1)S(1)}, bf16[1792,256]{1,0:T(8,128)(2,1)}, u32[]{:S(2)}) copy-start(bf16[1792,256]{1,0:T(8,128)(2,1)} %get-tuple-element.9) | copy-start | bytes 2752516
  59.7 18.0 %collective-permute-start = (bf16[128,1792]{1,0:T(8,128)(2,1)S(1)}, bf16[128,1792]{1,0:T(8,128)(2,1)S(1)}, u32[]{:S(2)}, u32[]{:S(2)}) collective-permute-start(bf16[128,1792]{1,0:T(8,128)(2,1)S(1)} %get-tuple-element.20), channel_id=1, source_target_pairs={{0,32},{32,64},{64,96},{96,0},{1,33},{33,65},{65,97},{97,1},{2,34}... | collective-permute-start | bytes 1376264 | tf_op jit(solution)/shard_map/ppermute | solution.py:13
  61.0 26.6 %collective-permute-start.3 = (bf16[128,1792]{1,0:T(8,128)(2,1)S(1)}, bf16[128,1792]{1,0:T(8,128)(2,1)S(1)}, u32[]{:S(2)}, u32[]{:S(2)}) collective-permute-start(bf16[128,1792]{1,0:T(8,128)(2,1)S(1)} %get-tuple-element.21), channel_id=1, source_target_pairs={{0,32},{32,64},{64,96},{96,0},{1,33},{33,65},{65,97},{97,1},{2,34}... | collective-permute-start | bytes 1376264 | tf_op jit(solution)/shard_map/ppermute | solution.py:13
  63.4 15.7 %copy-start.10 = (bf16[1792,256]{1,0:T(8,128)(2,1)S(1)}, bf16[1792,256]{1,0:T(8,128)(2,1)}, u32[]{:S(2)}) copy-start(bf16[1792,256]{1,0:T(8,128)(2,1)} %get-tuple-element.12) | copy-start | bytes 2752516
  63.4 15.7 %copy-start.11 = (bf16[1792,256]{1,0:T(8,128)(2,1)S(1)}, bf16[1792,256]{1,0:T(8,128)(2,1)}, u32[]{:S(2)}) copy-start(bf16[1792,256]{1,0:T(8,128)(2,1)} %get-tuple-element.8) | copy-start | bytes 2752516
  77.8 11.5 %collective-permute-start.1 = (bf16[128,1792]{1,0:T(8,128)(2,1)S(1)}, bf16[128,1792]{1,0:T(8,128)(2,1)S(1)}, u32[]{:S(2)}, u32[]{:S(2)}) collective-permute-start(bf16[128,1792]{1,0:T(8,128)(2,1)S(1)} %get-tuple-element.20), channel_id=1, source_target_pairs={{0,96},{32,0},{64,32},{96,64},{1,97},{33,1},{65,33},{97,65},{2,98}... | collective-permute-start | bytes 1376264 | tf_op jit(solution)/shard_map/ppermute | solution.py:13
  79.5 9.8 %copy-start.14 = (bf16[192,1792]{1,0:T(8,128)(2,1)S(1)}, bf16[192,1792]{1,0:T(8,128)(2,1)}, u32[]{:S(2)}) copy-start(bf16[192,1792]{1,0:T(8,128)(2,1)} %slice.63) | copy-start | bytes 2064388
  79.5 10.5 %copy-start.8 = (bf16[1792,256]{1,0:T(8,128)(2,1)S(1)}, bf16[1792,256]{1,0:T(8,128)(2,1)}, u32[]{:S(2)}) copy-start(bf16[1792,256]{1,0:T(8,128)(2,1)} %get-tuple-element.11) | copy-start | bytes 2752516
  79.5 10.4 %copy-start.9 = (bf16[1792,256]{1,0:T(8,128)(2,1)S(1)}, bf16[1792,256]{1,0:T(8,128)(2,1)}, u32[]{:S(2)}) copy-start(bf16[1792,256]{1,0:T(8,128)(2,1)} %get-tuple-element.7) | copy-start | bytes 2752516
  87.6 12.6 %collective-permute-start.4 = (bf16[128,1792]{1,0:T(8,128)(2,1)S(1)}, bf16[128,1792]{1,0:T(8,128)(2,1)S(1)}, u32[]{:S(2)}, u32[]{:S(2)}) collective-permute-start(bf16[128,1792]{1,0:T(8,128)(2,1)S(1)} %get-tuple-element.21), channel_id=1, source_target_pairs={{0,96},{32,0},{64,32},{96,64},{1,97},{33,1},{65,33},{97,65},{2,98}... | collective-permute-start | bytes 1376264 | tf_op jit(solution)/shard_map/ppermute | solution.py:13
  89.3 25.6 %collective-permute-start.13 = (bf16[192,1792]{1,0:T(8,128)(2,1)S(1)}, bf16[192,1792]{1,0:T(8,128)(2,1)S(1)}, u32[]{:S(2)}, u32[]{:S(2)}) collective-permute-start(bf16[192,1792]{1,0:T(8,128)(2,1)S(1)} %copy-done.14), channel_id=1, source_target_pairs={{0,96},{32,0},{64,32},{96,64},{1,97},{33,1},{65,33},{97,65},{2,98}... | collective-permute-start | bytes 2064392 | tf_op jit(solution)/shard_map/ppermute | solution.py:13
  100.2 17.6 %collective-permute-start.15 = (bf16[192,1792]{1,0:T(8,128)(2,1)}, bf16[192,1792]{1,0:T(8,128)(2,1)S(1)}, u32[]{:S(2)}, u32[]{:S(2)}) collective-permute-start(bf16[192,1792]{1,0:T(8,128)(2,1)} %slice.67), channel_id=1, source_target_pairs={{0,32},{32,64},{64,96},{96,0},{1,33},{33,65},{65,97},{97,1},{2,34}... | collective-permute-start | bytes 2064392 | tf_op jit(solution)/shard_map/ppermute | solution.py:13
  100.6 14.3 %copy-start.7 = (bf16[256,1792]{1,0:T(8,128)(2,1)S(1)}, bf16[256,1792]{1,0:T(8,128)(2,1)}, u32[]{:S(2)}) copy-start(bf16[256,1792]{1,0:T(8,128)(2,1)} %get-tuple-element.15) | copy-start | bytes 2752516
  100.6 29.2 %collective-permute-start.16 = (bf16[192,1792]{1,0:T(8,128)(2,1)}, bf16[192,1792]{1,0:T(8,128)(2,1)}, u32[]{:S(2)}, u32[]{:S(2)}) collective-permute-start(bf16[192,1792]{1,0:T(8,128)(2,1)} %slice.67), channel_id=1, source_target_pairs={{0,96},{32,0},{64,32},{96,64},{1,97},{33,1},{65,33},{97,65},{2,98}... | collective-permute-start | bytes 2064392 | tf_op jit(solution)/shard_map/ppermute | solution.py:13
  115.0 48.9 %collective-permute-start.11 = (bf16[256,1792]{1,0:T(8,128)(2,1)S(1)}, bf16[256,1792]{1,0:T(8,128)(2,1)S(1)}, u32[]{:S(2)}, u32[]{:S(2)}) collective-permute-start(bf16[256,1792]{1,0:T(8,128)(2,1)S(1)} %copy-done.7), channel_id=1, source_target_pairs={{0,64},{32,96},{64,0},{96,32},{1,65},{33,97},{65,1},{97,33},{2,66}... | collective-permute-start | bytes 2752520 | tf_op jit(solution)/shard_map/ppermute | solution.py:13
  117.8 12.0 %copy-start.6 = (bf16[256,1792]{1,0:T(8,128)(2,1)S(1)}, bf16[256,1792]{1,0:T(8,128)(2,1)}, u32[]{:S(2)}) copy-start(bf16[256,1792]{1,0:T(8,128)(2,1)} %get-tuple-element.17) | copy-start | bytes 2752516
  117.8 31.7 %collective-permute-start.2 = (bf16[128,1792]{1,0:T(8,128)(2,1)S(1)}, bf16[128,1792]{1,0:T(8,128)(2,1)S(1)}, u32[]{:S(2)}, u32[]{:S(2)}) collective-permute-start(bf16[128,1792]{1,0:T(8,128)(2,1)S(1)} %collective-permute-done), channel_id=1, source_target_pairs={{0,32},{32,64},{64,96},{96,0},{1,33},{33,65},{65,97},{97,1},{2,34}... | collective-permute-start | bytes 1376264 | tf_op jit(solution)/shard_map/ppermute | solution.py:13
  119.8 29.6 %copy-start.3 = (bf16[1792,256]{1,0:T(8,128)(2,1)S(1)}, bf16[1792,256]{1,0:T(8,128)(2,1)}, u32[]{:S(2)}) copy-start(bf16[1792,256]{1,0:T(8,128)(2,1)} %get-tuple-element.10) | copy-start | bytes 2752516
  119.8 29.6 %copy-start.4 = (bf16[1792,256]{1,0:T(8,128)(2,1)S(1)}, bf16[1792,256]{1,0:T(8,128)(2,1)}, u32[]{:S(2)}) copy-start(bf16[1792,256]{1,0:T(8,128)(2,1)} %get-tuple-element.6) | copy-start | bytes 2752516
  129.8 39.3 %collective-permute-start.9 = (bf16[256,1792]{1,0:T(8,128)(2,1)S(1)}, bf16[256,1792]{1,0:T(8,128)(2,1)S(1)}, u32[]{:S(2)}, u32[]{:S(2)}) collective-permute-start(bf16[256,1792]{1,0:T(8,128)(2,1)S(1)} %copy-done.6), channel_id=1, source_target_pairs={{0,32},{32,64},{64,96},{96,0},{1,33},{33,65},{65,97},{97,1},{2,34}... | collective-permute-start | bytes 2752520 | tf_op jit(solution)/shard_map/ppermute | solution.py:13
  149.5 8.4 %collective-permute-start.5 = (bf16[128,1792]{1,0:T(8,128)(2,1)S(1)}, bf16[128,1792]{1,0:T(8,128)(2,1)S(1)}, u32[]{:S(2)}, u32[]{:S(2)}) collective-permute-start(bf16[128,1792]{1,0:T(8,128)(2,1)S(1)} %collective-permute-done.4), channel_id=1, source_target_pairs={{0,96},{32,0},{64,32},{96,64},{1,97},{33,1},{65,33},{97,65},{2,98}... | collective-permute-start | bytes 1376264 | tf_op jit(solution)/shard_map/ppermute | solution.py:13
  149.9 20.0 %copy-start.2 = (bf16[1,256,7168]{2,1,0:T(8,128)(2,1)S(1)}, bf16[1,256,7168]{2,1,0:T(8,128)(2,1)}, u32[]{:S(2)}) copy-start(bf16[1,256,7168]{2,1,0:T(8,128)(2,1)} %param.13) | copy-start | bytes 11010052
  157.9 52.5 %collective-permute-start.22 = (bf16[1,7168,256]{2,1,0:T(8,128)(2,1)}, bf16[1,7168,256]{2,1,0:T(8,128)(2,1)}, u32[]{:S(2)}, u32[]{:S(2)}) collective-permute-start(bf16[1,7168,256]{2,1,0:T(8,128)(2,1)} %param.12), channel_id=1, source_target_pairs={{0,1},{1,0},{2,3},{3,2},{4,5},{5,4},{6,7},{7,6},{8,9},{9,8},{10,11... | collective-permute-start | bytes 11010056 | tf_op jit(solution)/shard_map/ppermute | solution.py:17
  162.9 38.3 %collective-permute-start.14 = (bf16[192,1792]{1,0:T(8,128)(2,1)}, bf16[192,1792]{1,0:T(8,128)(2,1)}, u32[]{:S(2)}, u32[]{:S(2)}) collective-permute-start(bf16[192,1792]{1,0:T(8,128)(2,1)} %collective-permute-done.12), channel_id=1, source_target_pairs={{0,32},{32,64},{64,96},{96,0},{1,33},{33,65},{65,97},{97,1},{2,34}... | collective-permute-start | bytes 2064392 | tf_op jit(solution)/shard_map/ppermute | solution.py:13
  163.8 25.0 %copy-start.17 = (bf16[256,1792]{1,0:T(8,128)(2,1)}, bf16[256,1792]{1,0:T(8,128)(2,1)S(1)}, u32[]{:S(2)}) copy-start(bf16[256,1792]{1,0:T(8,128)(2,1)S(1)} %collective-permute-done.11) | copy-start | bytes 2752516
  163.8 24.0 %collective-permute-start.6 = (bf16[256,256]{1,0:T(8,128)(2,1)S(1)}, bf16[256,256]{1,0:T(8,128)(2,1)S(1)}, u32[]{:S(2)}, u32[]{:S(2)}) collective-permute-start(bf16[256,256]{1,0:T(8,128)(2,1)S(1)} %pad_maximum_fusion.8), channel_id=1, source_target_pairs={{0,32},{32,64},{64,96},{96,0},{1,33},{33,65},{65,97},{97,1},{2,34}... | collective-permute-start | bytes 393224 | tf_op jit(solution)/shard_map/ppermute | solution.py:13
  169.1 19.7 %copy-start.19 = (bf16[256,1792]{1,0:T(8,128)(2,1)}, bf16[256,1792]{1,0:T(8,128)(2,1)S(1)}, u32[]{:S(2)}) copy-start(bf16[256,1792]{1,0:T(8,128)(2,1)S(1)} %collective-permute-done.9) | copy-start | bytes 2752516
  169.1 19.3 %collective-permute-start.7 = (bf16[256,256]{1,0:T(8,128)(2,1)S(1)}, bf16[256,256]{1,0:T(8,128)(2,1)S(1)}, u32[]{:S(2)}, u32[]{:S(2)}) collective-permute-start(bf16[256,256]{1,0:T(8,128)(2,1)S(1)} %pad_maximum_fusion.8), channel_id=1, source_target_pairs={{0,96},{32,0},{64,32},{96,64},{1,97},{33,1},{65,33},{97,65},{2,98}... | collective-permute-start | bytes 393224 | tf_op jit(solution)/shard_map/ppermute | solution.py:13
  169.1 19.6 %collective-permute-start.8 = (bf16[256,256]{1,0:T(8,128)(2,1)S(1)}, bf16[256,256]{1,0:T(8,128)(2,1)S(1)}, u32[]{:S(2)}, u32[]{:S(2)}) collective-permute-start(bf16[256,256]{1,0:T(8,128)(2,1)S(1)} %pad_maximum_fusion.8), channel_id=1, source_target_pairs={{0,64},{32,96},{64,0},{96,32},{1,65},{33,97},{65,1},{97,33},{2,66}... | collective-permute-start | bytes 393224 | tf_op jit(solution)/shard_map/ppermute | solution.py:13
  187.8 44.4 %collective-permute-start.21 = (bf16[1,7168,256]{2,1,0:T(8,128)(2,1)}, bf16[1,7168,256]{2,1,0:T(8,128)(2,1)}, u32[]{:S(2)}, u32[]{:S(2)}) collective-permute-start(bf16[1,7168,256]{2,1,0:T(8,128)(2,1)} %param.11), channel_id=1, source_target_pairs={{0,1},{1,0},{2,3},{3,2},{4,5},{5,4},{6,7},{7,6},{8,9},{9,8},{10,11... | collective-permute-start | bytes 11010056 | tf_op jit(solution)/shard_map/ppermute | solution.py:17
  188.4 17.4 %collective-permute-start.17 = (bf16[192,1792]{1,0:T(8,128)(2,1)}, bf16[192,1792]{1,0:T(8,128)(2,1)}, u32[]{:S(2)}, u32[]{:S(2)}) collective-permute-start(bf16[192,1792]{1,0:T(8,128)(2,1)} %collective-permute-done.16), channel_id=1, source_target_pairs={{0,96},{32,0},{64,32},{96,64},{1,97},{33,1},{65,33},{97,65},{2,98}... | collective-permute-start | bytes 2064392 | tf_op jit(solution)/shard_map/ppermute | solution.py:13
  192.0 30.9 %all-to-all-start.1 = ((bf16[32,8,1792]{2,1,0:T(8,128)(2,1)}), bf16[32,8,1792]{2,1,0:T(8,128)(2,1)S(1)}, u32[]{:S(2)}, u32[]{:S(2)}) async-start(bf16[32,8,1792]{2,1,0:T(8,128)(2,1)} %fusion.2), calls=%async_computation.1 | async-start | bytes 1835008 | tf_op jit(solution)/shard_map/all_to_all | solution.py:106
  201.1 4.7 %copy-start.5 = (bf16[1792,256]{1,0:T(8,128)(2,1)S(1)}, bf16[1792,256]{1,0:T(8,128)(2,1)}, u32[]{:S(2)}) copy-start(bf16[1792,256]{1,0:T(8,128)(2,1)} %get-tuple-element.6) | copy-start | bytes 2752516
  201.1 4.7 %copy-start.22 = (f32[192,512]{1,0:T(8,128)S(1)}, f32[192,512]{1,0:T(8,128)}, u32[]{:S(2)}) copy-start(f32[192,512]{1,0:T(8,128)} %convolution_add_fusion.2) | copy-start | bytes 1179652
  207.5 11.2 %copy-start.18 = (bf16[256,1792]{1,0:T(8,128)(2,1)S(1)}, bf16[256,1792]{1,0:T(8,128)(2,1)}, u32[]{:S(2)}) copy-start(bf16[256,1792]{1,0:T(8,128)(2,1)} %copy-done.17) | copy-start | bytes 2752516
  207.5 11.2 %copy-start.20 = (bf16[256,1792]{1,0:T(8,128)(2,1)S(1)}, bf16[256,1792]{1,0:T(8,128)(2,1)}, u32[]{:S(2)}) copy-start(bf16[256,1792]{1,0:T(8,128)(2,1)} %copy-done.19) | copy-start | bytes 2752516
  207.5 7.1 %collective-permute-start.18 = (bf16[384,256]{1,0:T(8,128)(2,1)S(1)}, bf16[384,256]{1,0:T(8,128)(2,1)S(1)}, u32[]{:S(2)}, u32[]{:S(2)}) collective-permute-start(bf16[384,256]{1,0:T(8,128)(2,1)S(1)} %pad_maximum_fusion.7), channel_id=1, source_target_pairs={{0,32},{32,64},{64,96},{96,0},{1,33},{33,65},{65,97},{97,1},{2,34}... | collective-permute-start | bytes 589832 | tf_op jit(solution)/shard_map/ppermute | solution.py:13
  207.6 7.0 %collective-permute-start.19 = (bf16[384,256]{1,0:T(8,128)(2,1)S(1)}, bf16[384,256]{1,0:T(8,128)(2,1)S(1)}, u32[]{:S(2)}, u32[]{:S(2)}) collective-permute-start(bf16[384,256]{1,0:T(8,128)(2,1)S(1)} %pad_maximum_fusion.7), channel_id=1, source_target_pairs={{0,96},{32,0},{64,32},{96,64},{1,97},{33,1},{65,33},{97,65},{2,98}... | collective-permute-start | bytes 589832 | tf_op jit(solution)/shard_map/ppermute | solution.py:13
  210.3 8.5 %collective-permute-start.20 = (bf16[384,256]{1,0:T(8,128)(2,1)S(1)}, bf16[384,256]{1,0:T(8,128)(2,1)S(1)}, u32[]{:S(2)}, u32[]{:S(2)}) collective-permute-start(bf16[384,256]{1,0:T(8,128)(2,1)S(1)} %pad_maximum_fusion.7), channel_id=1, source_target_pairs={{0,64},{32,96},{64,0},{96,32},{1,65},{33,97},{65,1},{97,33},{2,66}... | collective-permute-start | bytes 589832 | tf_op jit(solution)/shard_map/ppermute | solution.py:13
  223.0 34.2 %all-to-all-start.2 = ((bf16[32,12,1792]{2,1,0:T(8,128)(2,1)}), bf16[32,12,1792]{2,1,0:T(8,128)(2,1)}, u32[]{:S(2)}, u32[]{:S(2)}) async-start(bf16[32,12,1792]{2,1,0:T(8,128)(2,1)} %reshape.80), calls=%async_computation.2 | async-start | bytes 3670016 | tf_op jit(solution)/shard_map/all_to_all | solution.py:106
  257.1 6.7 %copy-start.1 = (bf16[320,1792]{1,0:T(8,128)(2,1)S(1)}, bf16[320,1792]{1,0:T(8,128)(2,1)}, u32[]{:S(2)}) copy-start(bf16[320,1792]{1,0:T(8,128)(2,1)} %param.7) | copy-start | bytes 3440644
  (2 other events, 4.8 us)

commit v2 on v1

v2 whole, which is shorter than its diff:
```python
import jax
import jax.numpy as jnp
from jax import lax
from jax.sharding import PartitionSpec as P

CHUNKS = (12, 8)
SEND_SLOTS = 24
CAP = 20


def shifted(value, step):
    size = lax.axis_size("dp")
    return lax.ppermute(value, "dp", [(i, (i + step) % size) for i in range(size)])


def swapped(value):
    return lax.ppermute(value, "expert", [(i, i ^ 1) for i in range(lax.axis_size("expert"))])


def dot32(left, right):
    return jnp.dot(left, right, preferred_element_type=jnp.float32)


def body(tokens, route_ids, route_scores, partner, w_gate, w_up, w_down):
    experts = lax.axis_size("expert")
    ring = lax.axis_size("dp")
    place = lax.axis_index("dp")
    own_index = lax.axis_index("expert")
    token_rows, width = tokens.shape
    offsets = (0, -1, 1, 2)

    in_window = route_ids < experts
    expert_pick = jnp.sum(jnp.where(in_window, route_ids, 0), axis=1)
    window_score = jnp.sum(jnp.where(in_window, route_scores, jnp.zeros_like(route_scores)), axis=1)
    gate_weight = 2.5 * window_score / jnp.sum(route_scores, axis=1)
    one_hot = expert_pick[:, None] == jnp.arange(experts, dtype=jnp.int32)[None, :]
    order = jnp.arange(token_rows, dtype=jnp.int32)
    earlier = (order[:, None] > order[None, :]).astype(jnp.bfloat16)
    counts = dot32(earlier, one_hot.astype(jnp.bfloat16))
    rank = jnp.sum(jnp.where(one_hot, counts, 0.0), axis=1).astype(jnp.int32)

    def columns(offset):
        start = ((place + offset) % ring) * width
        return lax.dynamic_slice(w_down[0], (0, start), (w_down.shape[1], width))

    down = [
        columns(0),
        shifted(columns(1), 1),
        shifted(columns(-1), -1),
        shifted(columns(2), 2),
    ]
    in_weights = []
    for offset in offsets:
        start = ((place + offset) % ring) * width
        size = (width, w_gate.shape[2])
        in_weights.append(
            jnp.concatenate(
                [
                    lax.dynamic_slice(w_gate[0], (start, 0), size),
                    lax.dynamic_slice(w_up[0], (start, 0), size),
                ],
                axis=1,
            )
        )

    slot = expert_pick * SEND_SLOTS + rank
    slots = jnp.arange(experts * SEND_SLOTS, dtype=jnp.int32)
    spread = (slots[:, None] == slot[None, :]).astype(jnp.bfloat16)
    send = dot32(spread, tokens).astype(jnp.bfloat16).reshape(experts, SEND_SLOTS, width)
    arrived = lax.all_to_all(send, "expert", split_axis=0, concat_axis=0, tiled=True)
    arrived = arrived.reshape(experts * SEND_SLOTS, width)

    moved = partner[own_index] != own_index
    own = (w_gate, w_up, w_down)
    others = [swapped(w) for w in own[:2]]
    others, down = lax.optimization_barrier((others, down))
    placed = [jnp.where(moved, o, w) for o, w in zip(others, own)]
    arrived, down, placed, in_weights, w_last = lax.optimization_barrier(
        (arrived, down, placed, in_weights, w_down)
    )

    total = jnp.zeros((token_rows, width), jnp.float32)
    hidden_width = w_gate.shape[2]
    low = 0
    picks = []

    def project(parts):
        return sum(dot32(h, w) for h, w in zip(parts, down)).astype(jnp.bfloat16)

    def send_back(out, size):
        blocks = out.reshape(experts, size, width)
        back = lax.all_to_all(blocks, "expert", split_axis=0, concat_axis=0, tiled=True)
        return back.reshape(experts * size, width)

    for size in CHUNKS:
        count = experts * size
        half = count // 2
        source = jnp.arange(count, dtype=jnp.int32)
        source = source // size * SEND_SLOTS + low + source % size
        select = (source[:, None] == slots[None, :]).astype(jnp.bfloat16)
        rows = dot32(select, arrived).astype(jnp.bfloat16)
        if low:
            rows, all_hidden = lax.optimization_barrier((rows, all_hidden))
            out = project(all_hidden)
        left, right = shifted(rows, 1), shifted(rows, -1)
        left_half, right_half = left[:half], right[half:]
        if low:
            left_half, right_half, out = lax.optimization_barrier((left_half, right_half, out))
            back = send_back(out, size_before)
        far = jnp.concatenate([shifted(left_half, 1), shifted(right_half, -1)], axis=0)
        both = sum(dot32(s, w) for s, w in zip((rows, left, right, far), in_weights))
        gate_proj, up_proj = both[:, :hidden_width], both[:, hidden_width:]
        hidden = (jax.nn.silu(gate_proj) * up_proj).astype(jnp.bfloat16)
        all_hidden = (hidden, shifted(hidden, 1), shifted(hidden, -1), shifted(hidden, 2))
        spot = jnp.where(
            (rank >= low) & (rank < low + size), expert_pick * size + rank - low, -1
        )
        picks.append((spot[:, None] == jnp.arange(count, dtype=jnp.int32)[None, :]).astype(jnp.bfloat16))
        low += size
        size_before = size
        if low > size: total = total + dot32(picks[0], back)
    other = swapped(w_last)
    other, all_hidden = lax.optimization_barrier((other, all_hidden))
    out = project(all_hidden)
    other, out = lax.optimization_barrier((other, out))
    placed.append(jnp.where(moved, other, w_last))
    total = total + dot32(picks[1], send_back(out, size))
    mixed = (gate_weight[:, None] * total).astype(jnp.bfloat16)
    return (mixed, *placed)


def solution(mesh):
    weights = (P("expert", None, "dp"), P("expert", None, "dp"), P("expert", "dp", None))
    return jax.shard_map(
        body,
        mesh=mesh,
        in_specs=(P("expert", "dp"), P("expert", None), P("expert", None), P(), *weights),
        out_specs=(P("expert", "dp"), *weights),
        check_vma=False,
    )
```

time: 266 us -> 213 us (0.80)
  waiting for transfers between devices: 143 us -> 83 us
  starting transfers between devices: 53.2 us -> 58.9 us
  other arithmetic: 11.8 us -> 16.9 us
  local copies, waits for them, and re-layouts: 22.1 us -> 18.6 us
    ppermute x21 -> x17, waiting for transfers between devices: 103 us -> 67.5 us  [shifted(): lax.ppermute(value, 'dp', [(i, (i + step) % size) for i in range(size)])]
    all_to_all x1, waiting for transfers between devices: 19.4 us -> 2.06 us  [body(): lax.all_to_all(send, 'expert', split_axis=0, concat_axis=0, tiled=True)]
    all_to_all x2, waiting for transfers between devices: 20.2 us -> 13.5 us  [send_back(): lax.all_to_all(blocks, 'expert', split_axis=0, concat_axis=0, tiled=True)]
    concatenate x2, other arithmetic: 0.03 us -> 6.1 us  [body(): jnp.concatenate([lax.dynamic_slice(w_gate[0], (start, 0), size), lax.dyna...]
    all_to_all x2, starting transfers between devices: 18.3 us -> 22.5 us  [send_back(): lax.all_to_all(blocks, 'expert', split_axis=0, concat_axis=0, tiled=True)]
    slice x4, local copies, waits for them, and re-layouts: 4.81 us -> 0.93 us  [body(): left_half, right_half = (left[:half], right[half:])]
    ppermute x21 -> x17, starting transfers between devices: 19.8 us -> 21.2 us  [shifted(): lax.ppermute(value, 'dp', [(i, (i + step) % size) for i in range(size)])]
    select_n x3 -> x2, other arithmetic: 10.7 us -> 10.5 us  [the longest x1 6.28 us: body(): placed = [jnp.where(moved, o, w) for o, w in zip(others, own)]]
  transfers between devices with their start and end apart: 27 -> 23, of which waited for: 13 -> 13; matrix products, arithmetic and copies ran while one was open for 21% -> 28% of each run, Pallas kernels for 0% -> 0%
where the time goes in v2:
time: 213 us; the launch traced here: 212 us
  waiting for transfers between devices  83 us (39%)
  starting transfers between devices  58.9 us (28%)
  matrix products  33.1 us (16%)
  local copies, waits for them, and re-layouts  18.6 us (9%)
  other arithmetic  16.9 us (8%)
    ppermute x17, waiting for transfers between devices, shifted(): lax.ppermute(value, 'dp', [(i, (i + step) % size) for i in range(size)])  67.5 us
    dot_general x22, matrix products, dot32(): return jnp.dot(left, right, preferred_element_type=jnp.float32)  33.1 us
    all_to_all x2, starting transfers between devices, send_back(): lax.all_to_all(blocks, 'expert', split_axis=0, concat_axis=0, tiled=True)  22.5 us
    ppermute x17, starting transfers between devices, shifted(): lax.ppermute(value, 'dp', [(i, (i + step) % size) for i in range(size)])  21.2 us
    all_to_all x2, waiting for transfers between devices, send_back(): lax.all_to_all(blocks, 'expert', split_axis=0, concat_axis=0, tiled=True)  13.5 us
    all_to_all x1, starting transfers between devices, body(): lax.all_to_all(send, 'expert', split_axis=0, concat_axis=0, tiled=True)  9.4 us
    select_n x1, other arithmetic, body(): placed = [jnp.where(moved, o, w) for o, w in zip(others, own)]  6.28 us
    concatenate x2, other arithmetic, body(): jnp.concatenate([lax.dynamic_slice(w_gate[0], (start, 0), size), lax.dyna...  6.1 us
  transfers between devices with their start and end apart: 23, of which 13 were waited for; matrix products, arithmetic and copies ran while one was open for 28% of the time, Pallas kernels for 0%

profile of v2, /device:TPU:1, one launch (start us, length us, event | category | flops | bytes accessed | tf_op | source)
XLA Modules:
  0.0 212.3 jit_solution(6918805497127083296)
XLA Ops:
  0.6 1.5 collective-permute-start
  2.2 3.9 %dynamic-slice_bitcast_fusion.8 = (bf16[256,1792]{1,0:T(8,128)(2,1)}, bf16[256,1792]{1,0:T(8,128)(2,1)}, bf16[256,1792]{1,0:T(8,128)(2,1)}, bf16[256,1792]{1,0:T(8,128)(2,1)}) fusion(bf16[1,256,7168]{2,1,0:T(8,128)(2,1)} %param.13, s32[]{:T(128)S(6)} %select_n.148, s32[]{:T(128)S(6)} %select_n.146, s32[]{:T(128)S(6)} %select_n.144, s32[]{:T(128)S(6)} %select_n.142), kind=kLoop, calls=%fused_computation.49 | loop fusion | bytes 7340048 | tf_op jit(solution)/shard_map/dynamic_slice | solution.py:44
  7.4 1.4 collective-permute-start.3
  8.8 1.6 collective-permute-start.4
  10.7 3.1 %convolution_convert_fusion = bf16[768,1792]{1,0:T(8,128)(2,1)} fusion(bf16[320,1792]{1,0:T(8,128)(2,1)S(1)} %copy-done, s32[320]{0:T(512)S(1)} %get-tuple-element.86), kind=kOutput, calls=%fused_computation.3 | convolution fusion | flops 882425856 | bytes 3900672 | tf_op jit(solution)/shard_map/dot_general | solution.py:21
  13.8 9.4 %all-to-all-start = ((bf16[32,24,1792]{2,1,0:T(8,128)(2,1)}), bf16[32,24,1792]{2,1,0:T(8,128)(2,1)}, u32[]{:S(2)}, u32[]{:S(2)}) async-start(bf16[32,24,1792]{2,1,0:T(8,128)(2,1)} %bitcast.65), calls=%async_computation | async-start | bytes 5505024 | tf_op jit(solution)/shard_map/all_to_all | solution.py:70
  23.2 3.3 %dynamic-slice_bitcast_fusion.1 = (bf16[1792,256]{1,0:T(8,128)(2,1)S(1)}, bf16[1792,256]{1,0:T(8,128)(2,1)S(1)}, bf16[1792,256]{1,0:T(8,128)(2,1)S(1)}, bf16[1792,256]{1,0:T(8,128)(2,1)}) fusion(bf16[1,7168,256]{2,1,0:T(8,128)(2,1)} %param.11, s32[]{:T(128)S(6)} %select_n.148, s32[]{:T(128)S(6)} %select_n.146, s32[]{:T(128)S(6)} %select_n.142, s32[]{:T(128)S(6)} %select_n.144), kind=kLoop, calls=%fused_computation.42 | loop fusion | bytes 7340048 | tf_op jit(solution)/shard_map/dynamic_slice | solution.py:59
  26.5 1.5 dynamic-slice_bitcast_fusion
  28.0 2.1 pad_maximum_fusion
  31.5 4.0 %pad_maximum_fusion.2 = (bf16[1792,512]{1,0:T(8,128)(2,1)}, bf16[1792,512]{1,0:T(8,128)(2,1)}) fusion(bf16[1792,256]{1,0:T(8,128)(2,1)} %get-tuple-element.79, bf16[1792,256]{1,0:T(8,128)(2,1)} %get-tuple-element.75, bf16[1792,256]{1,0:T(8,128)(2,1)} %get-tuple-element.76, bf16[1792,256]{1,0:T(8,128)(2,1)S(1)} %get-tuple-element.72), kind=kLoop, calls=%fused_computation.19 | loop fusion | flops 7340032 | bytes 7340032 | tf_op jit(solution)/shard_map/concatenate | solution.py:57
  35.5 14.4 %collective-permute-done.4 = bf16[256,1792]{1,0:T(8,128)(2,1)} collective-permute-done((bf16[256,1792]{1,0:T(8,128)(2,1)}, bf16[256,1792]{1,0:T(8,128)(2,1)}, u32[]{:S(2)}, u32[]{:S(2)}) %collective-permute-start.4) | collective-permute-done | bytes 917536 | tf_op jit(solution)/shard_map/ppermute | solution.py:13
  49.9 6.3 %broadcast_select_fusion.1 = (bf16[1,7168,256]{2,1,0:T(8,128)(2,1)}, bf16[1,7168,256]{2,1,0:T(8,128)(2,1)}) fusion(bf16[1,7168,256]{2,1,0:T(8,128)(2,1)} %collective-permute-done.1, bf16[1,7168,256]{2,1,0:T(8,128)(2,1)S(1)} %copy-done.3, pred[]{:T(512)S(6)} %ne.110, bf16[1,7168,256]{2,1,0:T(8,128)(2,1)} %collective-permute-done, bf16[1,7168,256]{2,1,0:T(8,128)(2,1)} %param.11), kind=kLoop, calls=%fused_computation.1 | loop fusion | flops 3670016 | bytes 22020096 | tf_op jit(solution)/shard_map/jit(_where)/select_n | solution.py:77
  56.2 2.1 all-to-all-done
  58.2 3.1 %convolution_convert_fusion.1 = bf16[384,1792]{1,0:T(8,128)(2,1)S(1)} fusion(bf16[768,1792]{1,0:T(8,128)(2,1)} %bitcast.1, s32[384]{0:T(512)S(1)} %fusion.37), kind=kOutput, calls=%fused_computation.9 | convolution fusion | flops 1057947648 | bytes 4130304 | tf_op jit(solution)/shard_map/dot_general | solution.py:21
  61.7 2.4 %collective-permute-start.6 = (bf16[384,1792]{1,0:T(8,128)(2,1)S(1)}, bf16[384,1792]{1,0:T(8,128)(2,1)S(1)}, u32[]{:S(2)}, u32[]{:S(2)}) collective-permute-start(bf16[384,1792]{1,0:T(8,128)(2,1)S(1)} %convolution_convert_fusion.1), channel_id=1, source_target_pairs={{0,96},{32,0},{64,32},{96,64},{1,97},{33,1},{65,33},{97,65},{2,98}... | collective-permute-start | bytes 4128776 | tf_op jit(solution)/shard_map/ppermute | solution.py:13
  64.1 27.5 %collective-permute-done.5 = bf16[384,1792]{1,0:T(8,128)(2,1)S(1)} collective-permute-done((bf16[384,1792]{1,0:T(8,128)(2,1)S(1)}, bf16[384,1792]{1,0:T(8,128)(2,1)S(1)}, u32[]{:S(2)}, u32[]{:S(2)}) %collective-permute-start.5) | collective-permute-done | bytes 1376288 | tf_op jit(solution)/shard_map/ppermute | solution.py:13
  91.8 2.7 %collective-permute-start.8 = (bf16[192,1792]{1,0:T(8,128)(2,1)S(1)}, bf16[192,1792]{1,0:T(8,128)(2,1)S(1)}, u32[]{:S(2)}, u32[]{:S(2)}) collective-permute-start(bf16[192,1792]{1,0:T(8,128)(2,1)S(1)} %slice.33), channel_id=1, source_target_pairs={{0,96},{32,0},{64,32},{96,64},{1,97},{33,1},{65,33},{97,65},{2,98}... | collective-permute-start | bytes 2064392 | tf_op jit(solution)/shard_map/ppermute | solution.py:13
  94.5 4.2 %collective-permute-start.14 = (bf16[1,256,7168]{2,1,0:T(8,128)(2,1)}, bf16[1,256,7168]{2,1,0:T(8,128)(2,1)}, u32[]{:S(2)}, u32[]{:S(2)}) collective-permute-start(bf16[1,256,7168]{2,1,0:T(8,128)(2,1)} %param.13), channel_id=1, source_target_pairs={{0,1},{1,0},{2,3},{3,2},{4,5},{5,4},{6,7},{7,6},{8,9},{9,8},{10,11... | collective-permute-start | bytes 11010056 | tf_op jit(solution)/shard_map/ppermute | solution.py:17
  100.5 5.7 %collective-permute-done.7 = bf16[192,1792]{1,0:T(8,128)(2,1)S(1)} collective-permute-done((bf16[192,1792]{1,0:T(8,128)(2,1)S(1)}, bf16[192,1792]{1,0:T(8,128)(2,1)S(1)}, u32[]{:S(2)}, u32[]{:S(2)}) %collective-permute-start.7) | collective-permute-done | bytes 688160 | tf_op jit(solution)/shard_map/ppermute | solution.py:13
  108.1 2.6 %collective-permute-start.10 = (bf16[384,256]{1,0:T(8,128)(2,1)S(1)}, bf16[384,256]{1,0:T(8,128)(2,1)S(1)}, u32[]{:S(2)}, u32[]{:S(2)}) collective-permute-start(bf16[384,256]{1,0:T(8,128)(2,1)S(1)} %fusion.24), channel_id=1, source_target_pairs={{0,96},{32,0},{64,32},{96,64},{1,97},{33,1},{65,33},{97,65},{2,98}... | collective-permute-start | bytes 589832 | tf_op jit(solution)/shard_map/ppermute | solution.py:13
  111.3 2.7 %convolution_convert_fusion.2 = bf16[256,1792]{1,0:T(8,128)(2,1)S(1)} fusion(bf16[768,1792]{1,0:T(8,128)(2,1)} %bitcast.1, s32[256]{0:T(256)S(1)} %fusion.45), kind=kOutput, calls=%fused_computation.16 | convolution fusion | flops 705298432 | bytes 3671040 | tf_op jit(solution)/shard_map/dot_general | solution.py:21
  114.1 1.3 collective-permute-done.10
  115.4 1.4 collective-permute-done.11
  116.8 1.7 collective-permute-done.9
  118.5 2.7 %collective-permute-start.13 = (bf16[256,1792]{1,0:T(8,128)(2,1)S(1)}, bf16[256,1792]{1,0:T(8,128)(2,1)S(1)}, u32[]{:S(2)}, u32[]{:S(2)}) collective-permute-start(bf16[256,1792]{1,0:T(8,128)(2,1)S(1)} %convolution_convert_fusion.2), channel_id=1, source_target_pairs={{0,96},{32,0},{64,32},{96,64},{1,97},{33,1},{65,33},{97,65},{2,98}... | collective-permute-start | bytes 2752520 | tf_op jit(solution)/shard_map/ppermute | solution.py:13
  121.2 1.7 fusion.51
  122.9 1.7 fusion.52
  124.6 1.8 fusion.53
  126.4 1.7 fusion.3
  128.2 9.8 %collective-permute-done.12 = bf16[256,1792]{1,0:T(8,128)(2,1)S(1)} collective-permute-done((bf16[256,1792]{1,0:T(8,128)(2,1)S(1)}, bf16[256,1792]{1,0:T(8,128)(2,1)S(1)}, u32[]{:S(2)}, u32[]{:S(2)}) %collective-permute-start.12) | collective-permute-done | bytes 917536 | tf_op jit(solution)/shard_map/ppermute | solution.py:13
  140.7 2.7 %collective-permute-start.16 = (bf16[128,1792]{1,0:T(8,128)(2,1)}, bf16[128,1792]{1,0:T(8,128)(2,1)}, u32[]{:S(2)}, u32[]{:S(2)}) collective-permute-start(bf16[128,1792]{1,0:T(8,128)(2,1)} %slice.37), channel_id=1, source_target_pairs={{0,96},{32,0},{64,32},{96,64},{1,97},{33,1},{65,33},{97,65},{2,98}... | collective-permute-start | bytes 1376264 | tf_op jit(solution)/shard_map/ppermute | solution.py:13
  143.3 3.3 %reshape.118 = bf16[32,12,1792]{2,1,0:T(8,128)(2,1)} reshape(bf16[384,1792]{1,0:T(8,128)(2,1)} %fusion.3) | data formatting | bytes 2752512 | tf_op jit(solution)/shard_map/reshape | solution.py:91
  146.6 16.6 %all-to-all-start.1 = ((bf16[32,12,1792]{2,1,0:T(8,128)(2,1)}), bf16[32,12,1792]{2,1,0:T(8,128)(2,1)}, u32[]{:S(2)}, u32[]{:S(2)}) async-start(bf16[32,12,1792]{2,1,0:T(8,128)(2,1)} %reshape.118), calls=%async_computation.1 | async-start | bytes 3670016 | tf_op jit(solution)/shard_map/all_to_all | solution.py:92
  163.3 2.0 fusion.54
  166.8 1.8 fusion.16
  169.4 2.7 %collective-permute-start.18 = (bf16[256,256]{1,0:T(8,128)(2,1)S(1)}, bf16[256,256]{1,0:T(8,128)(2,1)S(1)}, u32[]{:S(2)}, u32[]{:S(2)}) collective-permute-start(bf16[256,256]{1,0:T(8,128)(2,1)S(1)} %fusion.26), channel_id=1, source_target_pairs={{0,96},{32,0},{64,32},{96,64},{1,97},{33,1},{65,33},{97,65},{2,98}... | collective-permute-start | bytes 393224 | tf_op jit(solution)/shard_map/ppermute | solution.py:13
  172.1 3.4 %collective-permute-done.17 = bf16[256,256]{1,0:T(8,128)(2,1)S(1)} collective-permute-done((bf16[256,256]{1,0:T(8,128)(2,1)S(1)}, bf16[256,256]{1,0:T(8,128)(2,1)S(1)}, u32[]{:S(2)}, u32[]{:S(2)}) %collective-permute-start.17) | collective-permute-done | bytes 131104 | tf_op jit(solution)/shard_map/ppermute | solution.py:13
  175.5 1.7 collective-permute-done.18
  177.8 1.6 fusion.56
  179.4 1.6 fusion.57
  181.0 1.6 fusion.58
  182.6 1.4 fusion.7
  184.0 4.2 %all-to-all-done.1 = bf16[32,12,1792]{2,1,0:T(8,128)(2,1)} async-done(((bf16[32,12,1792]{2,1,0:T(8,128)(2,1)}), bf16[32,12,1792]{2,1,0:T(8,128)(2,1)}, u32[]{:S(2)}, u32[]{:S(2)}) %all-to-all-start.1) | async-done | bytes 1376288 | tf_op jit(solution)/shard_map/all_to_all | solution.py:92
  188.2 5.8 %all-to-all-start.2 = ((bf16[32,8,1792]{2,1,0:T(8,128)(2,1)}), bf16[32,8,1792]{2,1,0:T(8,128)(2,1)S(1)}, u32[]{:S(2)}, u32[]{:S(2)}) async-start(bf16[32,8,1792]{2,1,0:T(8,128)(2,1)} %bitcast.15), calls=%async_computation.2 | async-start | bytes 1835008 | tf_op jit(solution)/shard_map/all_to_all | solution.py:92
  194.0 4.3 %broadcast_select_fusion = bf16[1,256,7168]{2,1,0:T(8,128)(2,1)} fusion(bf16[1,256,7168]{2,1,0:T(8,128)(2,1)} %collective-permute-done.14, bf16[1,256,7168]{2,1,0:T(8,128)(2,1)} %param.13, pred[]{:T(512)S(6)} %ne.110), kind=kLoop, calls=%fused_computation | loop fusion | flops 1835008 | bytes 11010049 | tf_op jit(solution)/shard_map/jit(_where)/select_n | solution.py:126
  198.3 2.4 %reshape.119 = bf16[384,1792]{1,0:T(8,128)(2,1)S(1)} reshape(bf16[32,12,1792]{2,1,0:T(8,128)(2,1)} %all-to-all-done.1) | data formatting | bytes 2752512 | tf_op jit(solution)/shard_map/reshape | solution.py:93
  200.7 9.2 %all-to-all-done.2 = bf16[32,8,1792]{2,1,0:T(8,128)(2,1)S(1)} async-done(((bf16[32,8,1792]{2,1,0:T(8,128)(2,1)}), bf16[32,8,1792]{2,1,0:T(8,128)(2,1)S(1)}, u32[]{:S(2)}, u32[]{:S(2)}) %all-to-all-start.2) | async-done | bytes 917536 | tf_op jit(solution)/shard_map/all_to_all | solution.py:92
  210.4 1.9 fusion.6
  (82 shorter events, 13.3 us)
Async XLA Ops:
  0.6 10.0 %copy-start = (bf16[320,1792]{1,0:T(8,128)(2,1)S(1)}, bf16[320,1792]{1,0:T(8,128)(2,1)}, u32[]{:S(2)}) copy-start(bf16[320,1792]{1,0:T(8,128)(2,1)} %param.7) | copy-start | bytes 3440644
  0.6 49.3 %collective-permute-start = (bf16[1,7168,256]{2,1,0:T(8,128)(2,1)}, bf16[1,7168,256]{2,1,0:T(8,128)(2,1)}, u32[]{:S(2)}, u32[]{:S(2)}) collective-permute-start(bf16[1,7168,256]{2,1,0:T(8,128)(2,1)} %param.11), channel_id=1, source_target_pairs={{0,1},{1,0},{2,3},{3,2},{4,5},{5,4},{6,7},{7,6},{8,9},{9,8},{10,11... | collective-permute-start | bytes 11010056 | tf_op jit(solution)/shard_map/ppermute | solution.py:17
  2.1 47.8 %collective-permute-start.1 = (bf16[1,7168,256]{2,1,0:T(8,128)(2,1)}, bf16[1,7168,256]{2,1,0:T(8,128)(2,1)}, u32[]{:S(2)}, u32[]{:S(2)}) collective-permute-start(bf16[1,7168,256]{2,1,0:T(8,128)(2,1)} %param.12), channel_id=1, source_target_pairs={{0,1},{1,0},{2,3},{3,2},{4,5},{5,4},{6,7},{7,6},{8,9},{9,8},{10,11... | collective-permute-start | bytes 11010056 | tf_op jit(solution)/shard_map/ppermute | solution.py:17
  2.2 8.2 %copy-start.17 = (s32[320,8]{0,1:T(8,128)S(1)}, s32[320,8]{0,1:T(8,128)}, u32[]{:S(2)}) copy-start(s32[320,8]{0,1:T(8,128)} %param.8) | copy-start | bytes 30724
  6.1 29.4 %collective-permute-start.2 = (bf16[256,1792]{1,0:T(8,128)(2,1)}, bf16[256,1792]{1,0:T(8,128)(2,1)}, u32[]{:S(2)}, u32[]{:S(2)}) collective-permute-start(bf16[256,1792]{1,0:T(8,128)(2,1)} %get-tuple-element.82), channel_id=1, source_target_pairs={{0,32},{32,64},{64,96},{96,0},{1,33},{33,65},{65,97},{97,1},{2,34}... | collective-permute-start | bytes 2752520 | tf_op jit(solution)/shard_map/ppermute | solution.py:13
  7.4 28.1 %collective-permute-start.3 = (bf16[256,1792]{1,0:T(8,128)(2,1)}, bf16[256,1792]{1,0:T(8,128)(2,1)}, u32[]{:S(2)}, u32[]{:S(2)}) collective-permute-start(bf16[256,1792]{1,0:T(8,128)(2,1)} %get-tuple-element.81), channel_id=1, source_target_pairs={{0,96},{32,0},{64,32},{96,64},{1,97},{33,1},{65,33},{97,65},{2,98}... | collective-permute-start | bytes 2752520 | tf_op jit(solution)/shard_map/ppermute | solution.py:13
  8.8 41.1 %collective-permute-start.4 = (bf16[256,1792]{1,0:T(8,128)(2,1)}, bf16[256,1792]{1,0:T(8,128)(2,1)}, u32[]{:S(2)}, u32[]{:S(2)}) collective-permute-start(bf16[256,1792]{1,0:T(8,128)(2,1)} %get-tuple-element.80), channel_id=1, source_target_pairs={{0,64},{32,96},{64,0},{96,32},{1,65},{33,97},{65,1},{97,33},{2,66}... | collective-permute-start | bytes 2752520 | tf_op jit(solution)/shard_map/ppermute | solution.py:13
  13.8 44.4 %all-to-all-start = ((bf16[32,24,1792]{2,1,0:T(8,128)(2,1)}), bf16[32,24,1792]{2,1,0:T(8,128)(2,1)}, u32[]{:S(2)}, u32[]{:S(2)}) async-start(bf16[32,24,1792]{2,1,0:T(8,128)(2,1)} %bitcast.65), calls=%async_computation | async-start | bytes 5505024 | tf_op jit(solution)/shard_map/all_to_all | solution.py:70
  23.2 3.3 %copy-start.2 = (bf16[1,7168,256]{2,1,0:T(8,128)(2,1)S(1)}, bf16[1,7168,256]{2,1,0:T(8,128)(2,1)}, u32[]{:S(2)}) copy-start(bf16[1,7168,256]{2,1,0:T(8,128)(2,1)} %param.12) | copy-start | bytes 11010052
  28.0 2.1 copy-start.19
  31.5 18.4 %copy-start.3 = (bf16[1,7168,256]{2,1,0:T(8,128)(2,1)S(1)}, bf16[1,7168,256]{2,1,0:T(8,128)(2,1)}, u32[]{:S(2)}) copy-start(bf16[1,7168,256]{2,1,0:T(8,128)(2,1)} %param.12) | copy-start | bytes 11010052
  58.2 5.9 %copy-start.18 = (f32[320,8]{0,1:T(8,128)S(1)}, f32[320,8]{0,1:T(8,128)}, u32[]{:S(2)}) copy-start(f32[320,8]{0,1:T(8,128)} %param.9) | copy-start | bytes 30724
  61.4 37.4 %copy-start.8 = (bf16[1792,512]{1,0:T(8,128)(2,1)S(1)}, bf16[1792,512]{1,0:T(8,128)(2,1)}, u32[]{:S(2)}) copy-start(bf16[1792,512]{1,0:T(8,128)(2,1)} %get-tuple-element.44) | copy-start | bytes 5505028
  61.4 30.2 %collective-permute-start.5 = (bf16[384,1792]{1,0:T(8,128)(2,1)S(1)}, bf16[384,1792]{1,0:T(8,128)(2,1)S(1)}, u32[]{:S(2)}, u32[]{:S(2)}) collective-permute-start(bf16[384,1792]{1,0:T(8,128)(2,1)S(1)} %convolution_convert_fusion.1), channel_id=1, source_target_pairs={{0,32},{32,64},{64,96},{96,0},{1,33},{33,65},{65,97},{97,1},{2,34}... | collective-permute-start | bytes 4128776 | tf_op jit(solution)/shard_map/ppermute | solution.py:13
  61.7 30.0 %collective-permute-start.6 = (bf16[384,1792]{1,0:T(8,128)(2,1)S(1)}, bf16[384,1792]{1,0:T(8,128)(2,1)S(1)}, u32[]{:S(2)}, u32[]{:S(2)}) collective-permute-start(bf16[384,1792]{1,0:T(8,128)(2,1)S(1)} %convolution_convert_fusion.1), channel_id=1, source_target_pairs={{0,96},{32,0},{64,32},{96,64},{1,97},{33,1},{65,33},{97,65},{2,98}... | collective-permute-start | bytes 4128776 | tf_op jit(solution)/shard_map/ppermute | solution.py:13
  91.6 14.6 %collective-permute-start.7 = (bf16[192,1792]{1,0:T(8,128)(2,1)S(1)}, bf16[192,1792]{1,0:T(8,128)(2,1)S(1)}, u32[]{:S(2)}, u32[]{:S(2)}) collective-permute-start(bf16[192,1792]{1,0:T(8,128)(2,1)S(1)} %slice.32), channel_id=1, source_target_pairs={{0,32},{32,64},{64,96},{96,0},{1,33},{33,65},{65,97},{97,1},{2,34}... | collective-permute-start | bytes 2064392 | tf_op jit(solution)/shard_map/ppermute | solution.py:13
  91.8 14.4 %collective-permute-start.8 = (bf16[192,1792]{1,0:T(8,128)(2,1)S(1)}, bf16[192,1792]{1,0:T(8,128)(2,1)S(1)}, u32[]{:S(2)}, u32[]{:S(2)}) collective-permute-start(bf16[192,1792]{1,0:T(8,128)(2,1)S(1)} %slice.33), channel_id=1, source_target_pairs={{0,96},{32,0},{64,32},{96,64},{1,97},{33,1},{65,33},{97,65},{2,98}... | collective-permute-start | bytes 2064392 | tf_op jit(solution)/shard_map/ppermute | solution.py:13
  94.5 5.1 %copy-start.5 = (bf16[1792,512]{1,0:T(8,128)(2,1)S(1)}, bf16[1792,512]{1,0:T(8,128)(2,1)}, u32[]{:S(2)}) copy-start(bf16[1792,512]{1,0:T(8,128)(2,1)} %get-tuple-element.45) | copy-start | bytes 5505028
  94.5 77.6 %collective-permute-start.14 = (bf16[1,256,7168]{2,1,0:T(8,128)(2,1)}, bf16[1,256,7168]{2,1,0:T(8,128)(2,1)}, u32[]{:S(2)}, u32[]{:S(2)}) collective-permute-start(bf16[1,256,7168]{2,1,0:T(8,128)(2,1)} %param.13), channel_id=1, source_target_pairs={{0,1},{1,0},{2,3},{3,2},{4,5},{5,4},{6,7},{7,6},{8,9},{9,8},{10,11... | collective-permute-start | bytes 11010056 | tf_op jit(solution)/shard_map/ppermute | solution.py:17
  99.6 6.6 %copy-start.13 = (bf16[1792,512]{1,0:T(8,128)(2,1)S(1)}, bf16[1792,512]{1,0:T(8,128)(2,1)}, u32[]{:S(2)}) copy-start(bf16[1792,512]{1,0:T(8,128)(2,1)} %get-tuple-element.47) | copy-start | bytes 5505028
  100.5 6.6 %copy-start.6 = (bf16[1792,512]{1,0:T(8,128)(2,1)S(1)}, bf16[1792,512]{1,0:T(8,128)(2,1)}, u32[]{:S(2)}) copy-start(bf16[1792,512]{1,0:T(8,128)(2,1)} %get-tuple-element.46) | copy-start | bytes 5505028
  108.1 7.3 %collective-permute-start.10 = (bf16[384,256]{1,0:T(8,128)(2,1)S(1)}, bf16[384,256]{1,0:T(8,128)(2,1)S(1)}, u32[]{:S(2)}, u32[]{:S(2)}) collective-permute-start(bf16[384,256]{1,0:T(8,128)(2,1)S(1)} %fusion.24), channel_id=1, source_target_pairs={{0,96},{32,0},{64,32},{96,64},{1,97},{33,1},{65,33},{97,65},{2,98}... | collective-permute-start | bytes 589832 | tf_op jit(solution)/shard_map/ppermute | solution.py:13
  110.7 6.1 %collective-permute-start.11 = (bf16[384,256]{1,0:T(8,128)(2,1)S(1)}, bf16[384,256]{1,0:T(8,128)(2,1)S(1)}, u32[]{:S(2)}, u32[]{:S(2)}) collective-permute-start(bf16[384,256]{1,0:T(8,128)(2,1)S(1)} %fusion.24), channel_id=1, source_target_pairs={{0,64},{32,96},{64,0},{96,32},{1,65},{33,97},{65,1},{97,33},{2,66}... | collective-permute-start | bytes 589832 | tf_op jit(solution)/shard_map/ppermute | solution.py:13
  110.7 7.8 %collective-permute-start.9 = (bf16[384,256]{1,0:T(8,128)(2,1)S(1)}, bf16[384,256]{1,0:T(8,128)(2,1)S(1)}, u32[]{:S(2)}, u32[]{:S(2)}) collective-permute-start(bf16[384,256]{1,0:T(8,128)(2,1)S(1)} %fusion.24), channel_id=1, source_target_pairs={{0,32},{32,64},{64,96},{96,0},{1,33},{33,65},{65,97},{97,1},{2,34}... | collective-permute-start | bytes 589832 | tf_op jit(solution)/shard_map/ppermute | solution.py:13
  114.1 8.8 %copy-start.15 = (bf16[256,1792]{1,0:T(8,128)(2,1)}, bf16[256,1792]{1,0:T(8,128)(2,1)S(1)}, u32[]{:S(2)}) copy-start(bf16[256,1792]{1,0:T(8,128)(2,1)S(1)} %convolution_convert_fusion.2) | copy-start | bytes 2752516
  118.5 19.4 %collective-permute-start.12 = (bf16[256,1792]{1,0:T(8,128)(2,1)S(1)}, bf16[256,1792]{1,0:T(8,128)(2,1)S(1)}, u32[]{:S(2)}, u32[]{:S(2)}) collective-permute-start(bf16[256,1792]{1,0:T(8,128)(2,1)S(1)} %convolution_convert_fusion.2), channel_id=1, source_target_pairs={{0,32},{32,64},{64,96},{96,0},{1,33},{33,65},{65,97},{97,1},{2,34}... | collective-permute-start | bytes 2752520 | tf_op jit(solution)/shard_map/ppermute | solution.py:13
  118.5 20.4 %collective-permute-start.13 = (bf16[256,1792]{1,0:T(8,128)(2,1)S(1)}, bf16[256,1792]{1,0:T(8,128)(2,1)S(1)}, u32[]{:S(2)}, u32[]{:S(2)}) collective-permute-start(bf16[256,1792]{1,0:T(8,128)(2,1)S(1)} %convolution_convert_fusion.2), channel_id=1, source_target_pairs={{0,96},{32,0},{64,32},{96,64},{1,97},{33,1},{65,33},{97,65},{2,98}... | collective-permute-start | bytes 2752520 | tf_op jit(solution)/shard_map/ppermute | solution.py:13
  124.6 1.8 copy-start.4
  137.9 0.9 copy-start.10
  138.9 0.9 copy-start.11
  140.7 25.3 %collective-permute-start.15 = (bf16[128,1792]{1,0:T(8,128)(2,1)S(1)}, bf16[128,1792]{1,0:T(8,128)(2,1)}, u32[]{:S(2)}, u32[]{:S(2)}) collective-permute-start(bf16[128,1792]{1,0:T(8,128)(2,1)S(1)} %slice.36), channel_id=1, source_target_pairs={{0,32},{32,64},{64,96},{96,0},{1,33},{33,65},{65,97},{97,1},{2,34}... | collective-permute-start | bytes 1376264 | tf_op jit(solution)/shard_map/ppermute | solution.py:13
  140.7 25.3 %collective-permute-start.16 = (bf16[128,1792]{1,0:T(8,128)(2,1)}, bf16[128,1792]{1,0:T(8,128)(2,1)}, u32[]{:S(2)}, u32[]{:S(2)}) collective-permute-start(bf16[128,1792]{1,0:T(8,128)(2,1)} %slice.37), channel_id=1, source_target_pairs={{0,96},{32,0},{64,32},{96,64},{1,97},{33,1},{65,33},{97,65},{2,98}... | collective-permute-start | bytes 1376264 | tf_op jit(solution)/shard_map/ppermute | solution.py:13
  146.6 41.6 %all-to-all-start.1 = ((bf16[32,12,1792]{2,1,0:T(8,128)(2,1)}), bf16[32,12,1792]{2,1,0:T(8,128)(2,1)}, u32[]{:S(2)}, u32[]{:S(2)}) async-start(bf16[32,12,1792]{2,1,0:T(8,128)(2,1)} %reshape.118), calls=%async_computation.1 | async-start | bytes 3670016 | tf_op jit(solution)/shard_map/all_to_all | solution.py:92
  163.2 2.0 copy-start.7
  163.3 2.0 copy-start.12
  165.3 1.5 copy-start.14
  165.9 2.6 %copy-start.9 = (bf16[1792,512]{1,0:T(8,128)(2,1)S(1)}, bf16[1792,512]{1,0:T(8,128)(2,1)}, u32[]{:S(2)}) copy-start(bf16[1792,512]{1,0:T(8,128)(2,1)} %get-tuple-element.44) | copy-start | bytes 5505028
  165.9 2.6 %copy-start.16 = (bf16[256,1792]{1,0:T(8,128)(2,1)S(1)}, bf16[256,1792]{1,0:T(8,128)(2,1)}, u32[]{:S(2)}) copy-start(bf16[256,1792]{1,0:T(8,128)(2,1)} %copy-done.15) | copy-start | bytes 2752516
  169.3 6.2 %collective-permute-start.17 = (bf16[256,256]{1,0:T(8,128)(2,1)S(1)}, bf16[256,256]{1,0:T(8,128)(2,1)S(1)}, u32[]{:S(2)}, u32[]{:S(2)}) collective-permute-start(bf16[256,256]{1,0:T(8,128)(2,1)S(1)} %fusion.26), channel_id=1, source_target_pairs={{0,32},{32,64},{64,96},{96,0},{1,33},{33,65},{65,97},{97,1},{2,34}... | collective-permute-start | bytes 393224 | tf_op jit(solution)/shard_map/ppermute | solution.py:13
  169.4 7.8 %collective-permute-start.18 = (bf16[256,256]{1,0:T(8,128)(2,1)S(1)}, bf16[256,256]{1,0:T(8,128)(2,1)S(1)}, u32[]{:S(2)}, u32[]{:S(2)}) collective-permute-start(bf16[256,256]{1,0:T(8,128)(2,1)S(1)} %fusion.26), channel_id=1, source_target_pairs={{0,96},{32,0},{64,32},{96,64},{1,97},{33,1},{65,33},{97,65},{2,98}... | collective-permute-start | bytes 393224 | tf_op jit(solution)/shard_map/ppermute | solution.py:13
  172.1 5.8 %collective-permute-start.19 = (bf16[256,256]{1,0:T(8,128)(2,1)S(1)}, bf16[256,256]{1,0:T(8,128)(2,1)S(1)}, u32[]{:S(2)}, u32[]{:S(2)}) collective-permute-start(bf16[256,256]{1,0:T(8,128)(2,1)S(1)} %fusion.26), channel_id=1, source_target_pairs={{0,64},{32,96},{64,0},{96,32},{1,65},{33,97},{65,1},{97,33},{2,66}... | collective-permute-start | bytes 393224 | tf_op jit(solution)/shard_map/ppermute | solution.py:13
  188.2 21.7 %all-to-all-start.2 = ((bf16[32,8,1792]{2,1,0:T(8,128)(2,1)}), bf16[32,8,1792]{2,1,0:T(8,128)(2,1)S(1)}, u32[]{:S(2)}, u32[]{:S(2)}) async-start(bf16[32,8,1792]{2,1,0:T(8,128)(2,1)} %bitcast.15), calls=%async_computation.2 | async-start | bytes 1835008 | tf_op jit(solution)/shard_map/all_to_all | solution.py:92
  210.4 1.9 copy-start.1

commit v3 on v1

v3 whole, which is shorter than its diff:
```python
import jax
import jax.numpy as jnp
from jax import lax
from jax.experimental import pallas as pl
from jax.experimental.pallas import tpu as pltpu
from jax.sharding import PartitionSpec as P

CHUNKS = ((0, 12, 16), (12, 8, 8))


def tied(*values):
    return lax.optimization_barrier(values)


def shifted(value, step):
    size = lax.axis_size("dp")
    return lax.ppermute(value, "dp", [(i, (i + step) % size) for i in range(size)])


def swapped(value):
    return lax.ppermute(value, "expert", [(i, i ^ 1) for i in range(lax.axis_size("expert"))])


def dot32(left, right):
    return jnp.dot(left, right, preferred_element_type=jnp.float32)


FREE = pl.CostEstimate(flops=0, transcendentals=0, bytes_accessed=0)
LONG = pl.CostEstimate(flops=50_000_000_000, transcendentals=0, bytes_accessed=250_000_000)
PARAMS = pltpu.CompilerParams(vmem_limit_bytes=16 << 20)


def in_hbm(value):
    return pltpu.with_memory_space_constraint(value, pltpu.HBM)


def whole(shape):
    return pl.BlockSpec(shape, lambda *_: (0,) * len(shape), pipeline_mode=pl.Buffered(1))


def near_sums(shards, spots, w_gate, w_up):
    width = w_gate.shape[1] // lax.axis_size("dp")
    units = w_gate.shape[2]
    steps = len(shards)
    pieces = [piece for shard in shards for piece in shard]
    count = sum(piece.shape[0] for piece in shards[0])

    def kernel(spot_ref, *refs):
        step = pl.program_id(0)
        gate_ref, up_ref, sum_ref = refs[len(pieces) :]
        at = 0
        for i, shard in enumerate(shards):
            own = refs[at : at + len(shard)]
            at += len(shard)

            @pl.when(step == i)
            def _():
                low = 0
                for ref in own:
                    rows = ref[...]
                    span = slice(low, low + rows.shape[0])
                    low += rows.shape[0]
                    for j, weight_ref in enumerate((gate_ref, up_ref)):
                        part = dot32(rows, weight_ref[0])
                        cut = slice(j * units, (j + 1) * units)
                        sum_ref[span, cut] = part if i == 0 else sum_ref[span, cut] + part

    weight = pl.BlockSpec((1, width, units), lambda i, spot: (0, spot[i], 0))
    return pl.pallas_call(
        kernel,
        out_shape=jax.ShapeDtypeStruct((count, 2 * units), jnp.float32),
        grid_spec=pltpu.PrefetchScalarGridSpec(
            num_scalar_prefetch=1,
            grid=(steps,),
            in_specs=[whole(piece.shape) for piece in pieces] + [weight] * 2,
            out_specs=pl.BlockSpec((count, 2 * units), lambda i, spot: (0, 0)),
        ),
        compiler_params=PARAMS,
        cost_estimate=FREE,
        name="near_sums",
    )(spots, *map(in_hbm, pieces), in_hbm(w_gate), in_hbm(w_up))


def far_hidden(halves, sums, spots, w_gate, w_up):
    half, width = halves[0].shape
    units = w_gate.shape[2]
    pieces = 2
    depth = width // pieces

    def kernel(spot_ref, first_ref, second_ref, sum_ref, gate_ref, up_ref, out_ref, gates, ups):
        step = pl.program_id(0)

        @pl.when(step == 0)
        def _():
            gates[...] = sum_ref[:, :units]
            ups[...] = sum_ref[:, units:]

        for low, ref in ((0, first_ref), (half, second_ref)):
            rows = ref[...]
            gates[low : low + half] += dot32(rows, gate_ref[0])
            ups[low : low + half] += dot32(rows, up_ref[0])

        @pl.when(step == pieces - 1)
        def _():
            value = gates[...]
            out_ref[...] = (value / (1.0 + jnp.exp(-value)) * ups[...]).astype(out_ref.dtype)

    weight = pl.BlockSpec((1, depth, units), lambda i, spot: (0, spot[0] * pieces + i, 0))
    rows = pl.BlockSpec((half, depth), lambda i, spot: (0, i))
    return pl.pallas_call(
        kernel,
        out_shape=jax.ShapeDtypeStruct((2 * half, units), jnp.bfloat16),
        grid_spec=pltpu.PrefetchScalarGridSpec(
            num_scalar_prefetch=1,
            grid=(pieces,),
            in_specs=[rows, rows, whole((2 * half, 2 * units)), weight, weight],
            out_specs=pl.BlockSpec((2 * half, units), lambda i, spot: (0, 0)),
            scratch_shapes=[pltpu.VMEM((2 * half, units), jnp.float32)] * 2,
        ),
        compiler_params=PARAMS,
        cost_estimate=FREE,
        name="far_hidden",
    )(spots, *halves, sums, in_hbm(w_gate), in_hbm(w_up))


def projected(parts, down, size, held, cost):
    count, units = parts[0].shape
    steps = len(parts)
    width = down[0].shape[1]
    slots = count // size * held
    pieces = 2

    def kernel(*refs):
        hidden_refs, down_refs = refs[:steps], refs[steps : 2 * steps]
        out_ref, spread = refs[2 * steps :]

        @pl.when(pl.program_id(0) == 0)
        def _():
            if held != size:
                slot = lax.broadcasted_iota(jnp.int32, (slots, count), 0)
                row = lax.broadcasted_iota(jnp.int32, (slots, count), 1)
                source = slot // held * size + slot % held
                keep = (source == row) & (slot % held < size)
                select = jnp.where(keep, 1.0, 0.0).astype(jnp.bfloat16)
            for i, ref in enumerate(hidden_refs):
                rows = ref[...]
                if held != size:
                    rows = dot32(select, rows).astype(jnp.bfloat16)
                spread[:, i * units : (i + 1) * units] = rows

        total = dot32(spread[:, :units], down_refs[0][...])
        for i in range(1, steps):
            total += dot32(spread[:, i * units : (i + 1) * units], down_refs[i][...])
        out_ref[...] = total.astype(out_ref.dtype)

    return pl.pallas_call(
        kernel,
        out_shape=pltpu.HBM((slots, width), jnp.bfloat16),
        grid=(pieces,),
        in_specs=[whole((count, units))] * steps
        + [pl.BlockSpec((units, width // pieces), lambda i: (0, i))] * steps,
        out_specs=pl.BlockSpec((slots, width // pieces), lambda i: (0, i)),
        scratch_shapes=[pltpu.VMEM((slots, steps * units), jnp.bfloat16)],
        compiler_params=PARAMS,
        cost_estimate=cost,
        name="projected",
    )(*parts, *down)


def gate_weights(ids, scores, experts):
    count = ids.shape[0]

    def kernel(ids_ref, scores_ref, out_ref):
        value = scores_ref[...]
        inside = jnp.where(ids_ref[...] < experts, value, 0.0)
        chosen = jnp.sum(inside, axis=1, keepdims=True)
        out_ref[...] = 2.5 * chosen / jnp.sum(value, axis=1, keepdims=True)

    return pl.pallas_call(
        kernel,
        out_shape=jax.ShapeDtypeStruct((count, 1), jnp.float32),
        compiler_params=PARAMS,
        cost_estimate=LONG,
        name="gate_weights",
    )(ids, scores)


def collected(slot, back):
    count = slot.shape[0]
    slots, width = back.shape
    pieces = 2

    def kernel(slot_ref, back_ref, out_ref, pick):
        @pl.when(pl.program_id(0) == 0)
        def _():
            place = lax.broadcasted_iota(jnp.int32, (count, slots), 1)
            pick[...] = jnp.where(place == slot_ref[...], 1.0, 0.0).astype(jnp.bfloat16)

        out_ref[...] = dot32(pick[...], back_ref[...])

    return pl.pallas_call(
        kernel,
        out_shape=jax.ShapeDtypeStruct((count, width), jnp.float32),
        grid=(pieces,),
        in_specs=[whole((count, 1)), pl.BlockSpec((slots, width // pieces), lambda i: (0, i))],
        out_specs=pl.BlockSpec((count, width // pieces), lambda i: (0, i)),
        scratch_shapes=[pltpu.VMEM((count, slots), jnp.bfloat16)],
        compiler_params=PARAMS,
        cost_estimate=LONG,
        name="collected",
    )(slot, in_hbm(back))


def exchanged(rows):
    experts = lax.axis_size("expert")
    blocks = rows.reshape(experts, rows.shape[0] // experts, rows.shape[1])
    got = lax.all_to_all(blocks, "expert", split_axis=0, concat_axis=0, tiled=True)
    return got.reshape(rows.shape)


def matches(left, right):
    return (left[:, None] == right[None, :]).astype(jnp.bfloat16)


def body(tokens, route_ids, route_scores, partner, w_gate, w_up, w_down):
    experts = lax.axis_size("expert")
    ring = lax.axis_size("dp")
    place = lax.axis_index("dp")
    own_index = lax.axis_index("expert")
    token_rows, width = tokens.shape
    hidden_width = w_gate.shape[2]
    moved = partner[own_index] != own_index

    in_window = route_ids < experts
    expert_pick = jnp.sum(jnp.where(in_window, route_ids, 0), axis=1)
    one_hot = expert_pick[:, None] == jnp.arange(experts, dtype=jnp.int32)[None, :]
    order = jnp.arange(token_rows, dtype=jnp.int32)
    earlier = (order[:, None] > order[None, :]).astype(jnp.bfloat16)
    counts = dot32(earlier, one_hot.astype(jnp.bfloat16))
    rank = jnp.sum(jnp.where(one_hot, counts, 0.0), axis=1).astype(jnp.int32)

    def send_rows(chunk, source):
        low, size, held = chunk
        inside = (rank >= low) & (rank < low + size)
        slot = jnp.where(inside, expert_pick * held + rank - low, -1)
        slots = jnp.arange(experts * held, dtype=jnp.int32)
        return dot32(matches(slots, slot), source).astype(jnp.bfloat16), slot

    def live_rows(chunk, got):
        low, size, held = chunk
        if size == held:
            return got
        rows = jnp.arange(experts * size, dtype=jnp.int32)
        slots = jnp.arange(experts * held, dtype=jnp.int32)
        return dot32(matches(rows // size * held + rows % size, slots), got).astype(jnp.bfloat16)

    def columns(offset):
        start = ((place + offset) % ring) * width
        return lax.dynamic_slice(w_down[0], (0, start), (w_down.shape[1], width))

    send_a, slot_a = send_rows(CHUNKS[0], tokens)
    send_a, gate_own, up_own = tied(send_a, w_gate, w_up)
    got_a = exchanged(send_a)

    down = [
        columns(0),
        shifted(columns(1), 1),
        shifted(columns(-1), -1),
        shifted(columns(2), 2),
    ]
    swaps = [swapped(w_gate), swapped(w_up)]
    swaps, down, scores = tied(swaps, down, route_scores)
    gate_weight = gate_weights(route_ids, scores, experts)
    got_a, down, tokens, gate_weight, swaps, own = tied(
        got_a, down, tokens, gate_weight, swaps, (w_gate, w_up, w_down)
    )
    send_b, slot_b = send_rows(CHUNKS[1], tokens)
    got_b = exchanged(send_b)

    def split(rows):
        half = rows.shape[0] // 2
        return rows[:half], rows[half:]

    def first_step(halves):
        return shifted(halves[0], 1), shifted(halves[1], -1)

    spots = [(place + offset) % ring for offset in (0, -1, 1, 2)]
    near_spots = jnp.stack(spots[:3]).astype(jnp.int32)
    far_spots = jnp.stack(spots[3:]).astype(jnp.int32)

    def activations(halves, near):
        far = first_step(near)
        left = (near[0], shifted(halves[1], 1))
        right = (shifted(halves[0], -1), near[1])
        sums = near_sums((halves, left, right), near_spots, gate_own, up_own)
        hidden = far_hidden(far, sums, far_spots, gate_own, up_own)
        return [hidden, shifted(hidden, 1), shifted(hidden, -1), shifted(hidden, 2)]

    def project(chunk, hidden, cost):
        return projected(hidden, down, chunk[1], chunk[2], cost)

    halves_a = split(live_rows(CHUNKS[0], got_a))
    hidden_a = activations(halves_a, first_step(halves_a))
    halves_b = split(live_rows(CHUNKS[1], got_b))
    halves_b, hidden_a = tied(halves_b, hidden_a)
    near = first_step(halves_b)
    out_a = project(CHUNKS[0], hidden_a, LONG)
    near, out_a = tied(near, out_a)
    back_a = exchanged(out_a)
    hidden_b = activations(halves_b, near)
    other = swapped(own[2])
    total, hidden_b = tied(collected(slot_a[:, None], back_a), hidden_b)
    out_b = project(CHUNKS[1], hidden_b, FREE)
    swaps, other, out_b, own = tied(swaps, other, out_b, own)
    placed = [jnp.where(moved, o, w) for o, w in zip((*swaps, other), own)]
    back_b = exchanged(out_b)
    slots = jnp.arange(back_b.shape[0], dtype=jnp.int32)
    total = total + dot32(matches(slot_b, slots), back_b)
    mixed = (gate_weight * total).astype(jnp.bfloat16)
    return (mixed, *placed)


def solution(mesh):
    weights = (P("expert", None, "dp"), P("expert", None, "dp"), P("expert", "dp", None))
    return jax.shard_map(
        body,
        mesh=mesh,
        in_specs=(P("expert", "dp"), P("expert", None), P("expert", None), P(), *weights),
        out_specs=(P("expert", "dp"), *weights),
        check_vma=False,
    )
```

time: 266 us -> 209 us (0.79)
  waiting for transfers between devices: 143 us -> 82.7 us
  Pallas kernels: 0 us -> 28.6 us
  matrix products: 31.9 us -> 8.29 us
  starting transfers between devices: 53.2 us -> 64.7 us
  local copies, waits for them, and re-layouts: 22.1 us -> 11.1 us
    all_to_all x3 -> x4, waiting for transfers between devices: 39.5 us -> 6.43 us  [exchanged(): lax.all_to_all(blocks, 'expert', split_axis=0, concat_axis=0, tiled=True)]
    pallas_call x0 -> x8, Pallas kernels: none -> 28.6 us  [the longest x2 12.2 us: near_sums(): pl.pallas_call(kernel, out_shape=jax.ShapeDtypeStruct((count, 2 * units),...]
    ppermute x21, waiting for transfers between devices: 103 us -> 76.3 us  [shifted(): lax.ppermute(value, 'dp', [(i, (i + step) % size) for i in range(size)])]
    dot_general x22 -> x5, matrix products: 31.9 us -> 8.29 us  [dot32(): return jnp.dot(left, right, preferred_element_type=jnp.float32)]
    all_to_all x3 -> x4, starting transfers between devices: 28 us -> 37.2 us  [exchanged(): lax.all_to_all(blocks, 'expert', split_axis=0, concat_axis=0, tiled=True)]
    dynamic_slice x2 -> x0, local copies, waits for them, and re-layouts: 7.78 us -> none  [the longest x1 3.93 us: body(): lax.dynamic_slice(w_up[0], (start, 0), size)]
    reshape x2 -> x0, local copies, waits for them, and re-layouts: 4.91 us -> none  [the longest x1 3.5 us: body(): back = lax.all_to_all(out.reshape(experts, size, width), 'expert', split_...]
    ppermute x21, starting transfers between devices: 19.8 us -> 24.6 us  [shifted(): lax.ppermute(value, 'dp', [(i, (i + step) % size) for i in range(size)])]
  transfers between devices with their start and end apart: 27 -> 28, of which waited for: 13 -> 17; matrix products, arithmetic and copies ran while one was open for 21% -> 10% of each run, Pallas kernels for 0% -> 14%
where the time goes in v3:
time: 209 us; the launch traced here: 208 us
  waiting for transfers between devices  82.7 us (40%)
  starting transfers between devices  64.7 us (31%)
  Pallas kernels  28.6 us (14%)
  local copies, waits for them, and re-layouts  11.1 us (5%)
  other arithmetic  11 us (5%)
  matrix products  8.29 us (4%)
    ppermute x21, waiting for transfers between devices, shifted(): lax.ppermute(value, 'dp', [(i, (i + step) % size) for i in range(size)])  76.3 us
    all_to_all x4, starting transfers between devices, exchanged(): lax.all_to_all(blocks, 'expert', split_axis=0, concat_axis=0, tiled=True)  37.2 us
    ppermute x21, starting transfers between devices, shifted(): lax.ppermute(value, 'dp', [(i, (i + step) % size) for i in range(size)])  24.6 us
    pallas_call x2, Pallas kernels, near_sums(): pl.pallas_call(kernel, out_shape=jax.ShapeDtypeStruct((count, 2 * units),...  12.2 us
    select_n x2, other arithmetic, body(): placed = [jnp.where(moved, o, w) for o, w in zip((*swaps, other), own)]  9.38 us
    pallas_call x2, Pallas kernels, projected(): pl.pallas_call(kernel, out_shape=pltpu.HBM((slots, width), jnp.bfloat16),...  8.85 us
    dot_general x5, matrix products, dot32(): return jnp.dot(left, right, preferred_element_type=jnp.float32)  8.29 us
    all_to_all x4, waiting for transfers between devices, exchanged(): lax.all_to_all(blocks, 'expert', split_axis=0, concat_axis=0, tiled=True)  6.43 us
  transfers between devices with their start and end apart: 28, of which 17 were waited for; matrix products, arithmetic and copies ran while one was open for 10% of the time, Pallas kernels for 14%

profile of v3, /device:TPU:1, one launch (start us, length us, event | category | flops | bytes accessed | tf_op | source)
XLA Modules:
  0.0 207.8 jit_solution(16082447315992843555)
XLA Ops:
  0.6 1.5 collective-permute-start
  2.2 3.6 %dynamic-slice_bitcast_fusion = (bf16[256,1792]{1,0:T(8,128)(2,1)}, bf16[256,1792]{1,0:T(8,128)(2,1)}, bf16[256,1792]{1,0:T(8,128)(2,1)}, bf16[256,1792]{1,0:T(8,128)(2,1)S(1)}) fusion(bf16[1,256,7168]{2,1,0:T(8,128)(2,1)} %param.13, s32[]{:T(128)S(6)} %select_n.128, s32[]{:T(128)S(6)} %select_n.126, s32[]{:T(128)S(6)} %select_n.124, s32[]{:T(128)S(6)} %select_n.122), kind=kLoop, calls=%fused_computation.12 | loop fusion | bytes 7340048 | tf_op jit(solution)/shard_map/dynamic_slice | solution.py:259
  5.9 2.8 %collective-permute-start.4 = (bf16[256,1792]{1,0:T(8,128)(2,1)}, bf16[256,1792]{1,0:T(8,128)(2,1)S(1)}, u32[]{:S(2)}, u32[]{:S(2)}) collective-permute-start(bf16[256,1792]{1,0:T(8,128)(2,1)} %get-tuple-element.90), channel_id=1, source_target_pairs={{0,64},{32,96},{64,0},{96,32},{1,65},{33,97},{65,1},{97,33},{2,66}... | collective-permute-start | bytes 2752520 | tf_op jit(solution)/shard_map/ppermute | solution.py:17
  10.4 2.3 %convolution_convert_fusion = bf16[512,1792]{1,0:T(8,128)(2,1)} fusion(bf16[320,1792]{1,0:T(8,128)(2,1)S(1)} %copy-done, s32[320]{0:T(512)S(1)} %get-tuple-element.99), kind=kOutput, calls=%fused_computation.3 | convolution fusion | flops 588283904 | bytes 2983168 | tf_op jit(solution)/shard_map/dot_general | solution.py:25
  12.7 9.5 %all-to-all-start = ((bf16[32,16,1792]{2,1,0:T(8,128)(2,1)}), bf16[32,16,1792]{2,1,0:T(8,128)(2,1)}, u32[]{:S(2)}, u32[]{:S(2)}) async-start(bf16[32,16,1792]{2,1,0:T(8,128)(2,1)} %bitcast.32), calls=%async_computation | async-start | bytes 3670016 | tf_op jit(solution)/shard_map/all_to_all | solution.py:217
  22.4 6.8 %collective-permute-done.4.refs_7_ = bf16[256,1792]{1,0:T(8,128)(2,1)S(1)} collective-permute-done((bf16[256,1792]{1,0:T(8,128)(2,1)}, bf16[256,1792]{1,0:T(8,128)(2,1)S(1)}, u32[]{:S(2)}, u32[]{:S(2)}) %collective-permute-start.4) | collective-permute-done | bytes 917536 | tf_op jit(solution)/shard_map/ppermute | solution.py:17
  29.2 19.8 %collective-permute-done.3.refs_6_ = bf16[256,1792]{1,0:T(8,128)(2,1)} collective-permute-done((bf16[256,1792]{1,0:T(8,128)(2,1)}, bf16[256,1792]{1,0:T(8,128)(2,1)}, u32[]{:S(2)}, u32[]{:S(2)}) %collective-permute-start.3) | collective-permute-done | bytes 917536 | tf_op jit(solution)/shard_map/ppermute | solution.py:17
  49.9 2.4 %convolution_convert_fusion.1 = bf16[384,1792]{1,0:T(8,128)(2,1)S(1)} fusion(bf16[512,1792]{1,0:T(8,128)(2,1)} %bitcast.1, s32[384]{0:T(512)S(1)} %fusion.15), kind=kOutput, calls=%fused_computation.4 | convolution fusion | flops 705527808 | bytes 3212800 | tf_op jit(solution)/shard_map/dot_general | solution.py:25
  52.4 1.2 fusion.21
  53.5 2.6 %collective-permute-start.7 = (bf16[192,1792]{1,0:T(8,128)(2,1)}, bf16[192,1792]{1,0:T(8,128)(2,1)}, u32[]{:S(2)}, u32[]{:S(2)}) collective-permute-start(bf16[192,1792]{1,0:T(8,128)(2,1)} %get-tuple-element.94.refs_1_), channel_id=1, source_target_pairs={{0,96},{32,0},{64,32},{96,64},{1,97},{33,1},{65,33},{97,65},{2,98}... | collective-permute-start | bytes 2064392 | tf_op jit(solution)/shard_map/ppermute | solution.py:17
  56.1 1.5 fusion
  57.7 8.9 %all-to-all-start.1 = ((bf16[32,8,1792]{2,1,0:T(8,128)(2,1)}), bf16[32,8,1792]{2,1,0:T(8,128)(2,1)}, u32[]{:S(2)}, u32[]{:S(2)}) async-start(bf16[32,8,1792]{2,1,0:T(8,128)(2,1)} %fusion), calls=%async_computation.1 | async-start | bytes 1835008 | tf_op jit(solution)/shard_map/all_to_all | solution.py:217
  67.2 2.5 %collective-permute-start.10 = (bf16[192,1792]{1,0:T(8,128)(2,1)}, bf16[192,1792]{1,0:T(8,128)(2,1)S(1)}, u32[]{:S(2)}, u32[]{:S(2)}) collective-permute-start(bf16[192,1792]{1,0:T(8,128)(2,1)} %get-tuple-element.95.refs_0_), channel_id=1, source_target_pairs={{0,96},{32,0},{64,32},{96,64},{1,97},{33,1},{65,33},{97,65},{2,98}... | collective-permute-start | bytes 2064392 | tf_op jit(solution)/shard_map/ppermute | solution.py:17
  69.7 1.0 collective-permute-done.7.refs_5_
  70.7 3.4 %collective-permute-start.8 = (bf16[192,1792]{1,0:T(8,128)(2,1)}, bf16[192,1792]{1,0:T(8,128)(2,1)S(1)}, u32[]{:S(2)}, u32[]{:S(2)}) collective-permute-start(bf16[192,1792]{1,0:T(8,128)(2,1)} %collective-permute-done.7.refs_5_), channel_id=1, source_target_pairs={{0,96},{32,0},{64,32},{96,64},{1,97},{33,1},{65,33},{97,65},{2,98}... | collective-permute-start | bytes 2064392 | tf_op jit(solution)/shard_map/ppermute | solution.py:17
  74.2 14.2 %collective-permute-done.9.refs_3_ = bf16[192,1792]{1,0:T(8,128)(2,1)S(1)} collective-permute-done((bf16[192,1792]{1,0:T(8,128)(2,1)}, bf16[192,1792]{1,0:T(8,128)(2,1)S(1)}, u32[]{:S(2)}, u32[]{:S(2)}) %collective-permute-start.9) | collective-permute-done | bytes 688160 | tf_op jit(solution)/shard_map/ppermute | solution.py:17
  90.2 6.6 %near_sums.2.sum_ref = f32[384,512]{1,0:T(8,128)S(1)} custom-call(s32[3]{0:T(128)S(1)} %pad_add_fusion.spot_ref, bf16[192,1792]{1,0:T(8,128)(2,1)} %get-tuple-element.95.refs_0_, bf16[192,1792]{1,0:T(8,128)(2,1)} %get-tuple-element.94.refs_1_, bf16[192,1792]{1,0:T(8,128)(2,1)} %collective-permute-done.5.refs_2_, bf16[192,1792]{1,0:T(8,128)(2,1)} %copy-done.5, ...), custom_call_target="tpu_custom_call" | custom-call | tf_op jit(solution)/shard_map/near_sums/pallas_call | solution.py:69
  96.8 3.5 %collective-permute-done.8.second_ref = bf16[192,1792]{1,0:T(8,128)(2,1)S(1)} collective-permute-done((bf16[192,1792]{1,0:T(8,128)(2,1)}, bf16[192,1792]{1,0:T(8,128)(2,1)S(1)}, u32[]{:S(2)}, u32[]{:S(2)}) %collective-permute-start.8) | collective-permute-done | bytes 688160 | tf_op jit(solution)/shard_map/ppermute | solution.py:17
  100.2 3.0 %collective-permute-done.6.first_ref = bf16[192,1792]{1,0:T(8,128)(2,1)S(1)} collective-permute-done((bf16[192,1792]{1,0:T(8,128)(2,1)}, bf16[192,1792]{1,0:T(8,128)(2,1)S(1)}, u32[]{:S(2)}, u32[]{:S(2)}) %collective-permute-start.6) | collective-permute-done | bytes 688160 | tf_op jit(solution)/shard_map/ppermute | solution.py:17
  103.2 2.6 %far_hidden.2.refs_0_ = bf16[384,256]{1,0:T(8,128)(2,1)S(1)} custom-call(s32[1]{0:T(128)} %bitcast.9.spot_ref, bf16[192,1792]{1,0:T(8,128)(2,1)S(1)} %collective-permute-done.6.first_ref, bf16[192,1792]{1,0:T(8,128)(2,1)S(1)} %collective-permute-done.8.second_ref, f32[384,512]{1,0:T(8,128)S(1)} %near_sums.2.sum_ref, bf16[1,7168,256]{2,1,0:T(8,128)(2,1)} %gate_ref.1, ...), custom_call_target="tpu_custom_call" | custom-call | tf_op jit(solution)/shard_map/far_hidden/pallas_call | solution.py:110
  105.9 1.5 collective-permute-start.12
  107.5 2.1 %slice_bitcast_fusion = (bf16[128,1792]{1,0:T(8,128)(2,1)}, bf16[128,1792]{1,0:T(8,128)(2,1)}) fusion(bf16[32,8,1792]{2,1,0:T(8,128)(2,1)} %all-to-all-done.1), kind=kLoop, calls=%fused_computation.19 | loop fusion | bytes 1835008 | tf_op jit(solution)/shard_map/slice | solution.py:282
  109.6 2.4 %collective-permute-done.13.refs_3_ = bf16[384,256]{1,0:T(8,128)(2,1)S(1)} collective-permute-done((bf16[384,256]{1,0:T(8,128)(2,1)S(1)}, bf16[384,256]{1,0:T(8,128)(2,1)S(1)}, u32[]{:S(2)}, u32[]{:S(2)}) %collective-permute-start.13) | collective-permute-done | bytes 196640 | tf_op jit(solution)/shard_map/ppermute | solution.py:17
  112.0 3.1 %collective-permute-done.12.refs_2_ = bf16[384,256]{1,0:T(8,128)(2,1)S(1)} collective-permute-done((bf16[384,256]{1,0:T(8,128)(2,1)S(1)}, bf16[384,256]{1,0:T(8,128)(2,1)S(1)}, u32[]{:S(2)}, u32[]{:S(2)}) %collective-permute-start.12) | collective-permute-done | bytes 196640 | tf_op jit(solution)/shard_map/ppermute | solution.py:17
  115.1 2.6 %collective-permute-done.11.refs_1_ = bf16[384,256]{1,0:T(8,128)(2,1)S(1)} collective-permute-done((bf16[384,256]{1,0:T(8,128)(2,1)S(1)}, bf16[384,256]{1,0:T(8,128)(2,1)S(1)}, u32[]{:S(2)}, u32[]{:S(2)}) %collective-permute-start.11) | collective-permute-done | bytes 196640 | tf_op jit(solution)/shard_map/ppermute | solution.py:17
  117.7 2.7 %collective-permute-start.15 = (bf16[128,1792]{1,0:T(8,128)(2,1)}, bf16[128,1792]{1,0:T(8,128)(2,1)S(1)}, u32[]{:S(2)}, u32[]{:S(2)}) collective-permute-start(bf16[128,1792]{1,0:T(8,128)(2,1)} %get-tuple-element.61.refs_1_), channel_id=1, source_target_pairs={{0,96},{32,0},{64,32},{96,64},{1,97},{33,1},{65,33},{97,65},{2,98}... | collective-permute-start | bytes 1376264 | tf_op jit(solution)/shard_map/ppermute | solution.py:17
  120.4 5.4 %projected.2 = bf16[512,1792]{1,0:T(8,128)(2,1)} custom-call(bf16[384,256]{1,0:T(8,128)(2,1)S(1)} %far_hidden.2.refs_0_, bf16[384,256]{1,0:T(8,128)(2,1)S(1)} %collective-permute-done.11.refs_1_, bf16[384,256]{1,0:T(8,128)(2,1)S(1)} %collective-permute-done.12.refs_2_, bf16[384,256]{1,0:T(8,128)(2,1)S(1)} %collective-permute-done.13.refs_3_, ...), custom_call_target="tpu_custom_call" | custom-call | flops 49999998976 | bytes 250000000 | tf_op jit(solution)/shard_map/projected/pallas_call | solution.py:156
  125.8 4.3 %collective-permute-done.14.refs_2_ = bf16[128,1792]{1,0:T(8,128)(2,1)} collective-permute-done((bf16[128,1792]{1,0:T(8,128)(2,1)}, bf16[128,1792]{1,0:T(8,128)(2,1)}, u32[]{:S(2)}, u32[]{:S(2)}) %collective-permute-start.14) | collective-permute-done | bytes 458784 | tf_op jit(solution)/shard_map/ppermute | solution.py:17
  130.0 10.3 %all-to-all-start.2 = ((bf16[32,16,1792]{2,1,0:T(8,128)(2,1)}), bf16[32,16,1792]{2,1,0:T(8,128)(2,1)}, u32[]{:S(2)}, u32[]{:S(2)}) async-start(bf16[32,16,1792]{2,1,0:T(8,128)(2,1)} %bitcast.31), calls=%async_computation.2 | async-start | bytes 3670016 | tf_op jit(solution)/shard_map/all_to_all | solution.py:217
  140.3 2.6 %collective-permute-start.19 = (bf16[128,1792]{1,0:T(8,128)(2,1)}, bf16[128,1792]{1,0:T(8,128)(2,1)}, u32[]{:S(2)}, u32[]{:S(2)}) collective-permute-start(bf16[128,1792]{1,0:T(8,128)(2,1)} %get-tuple-element.60.refs_0_), channel_id=1, source_target_pairs={{0,96},{32,0},{64,32},{96,64},{1,97},{33,1},{65,33},{97,65},{2,98}... | collective-permute-start | bytes 1376264 | tf_op jit(solution)/shard_map/ppermute | solution.py:17
  143.0 2.7 %collective-permute-start.17 = (bf16[128,1792]{1,0:T(8,128)(2,1)}, bf16[128,1792]{1,0:T(8,128)(2,1)S(1)}, u32[]{:S(2)}, u32[]{:S(2)}) collective-permute-start(bf16[128,1792]{1,0:T(8,128)(2,1)} %copy-done.7), channel_id=1, source_target_pairs={{0,96},{32,0},{64,32},{96,64},{1,97},{33,1},{65,33},{97,65},{2,98}... | collective-permute-start | bytes 1376264 | tf_op jit(solution)/shard_map/ppermute | solution.py:17
  146.9 1.2 collective-permute-start.23
  148.3 4.6 %collective-permute-done.19.refs_4_ = bf16[128,1792]{1,0:T(8,128)(2,1)} collective-permute-done((bf16[128,1792]{1,0:T(8,128)(2,1)}, bf16[128,1792]{1,0:T(8,128)(2,1)}, u32[]{:S(2)}, u32[]{:S(2)}) %collective-permute-start.19) | collective-permute-done | bytes 458784 | tf_op jit(solution)/shard_map/ppermute | solution.py:17
  152.9 3.1 %collective-permute-done.18.refs_3_ = bf16[128,1792]{1,0:T(8,128)(2,1)} collective-permute-done((bf16[128,1792]{1,0:T(8,128)(2,1)}, bf16[128,1792]{1,0:T(8,128)(2,1)}, u32[]{:S(2)}, u32[]{:S(2)}) %collective-permute-start.18) | collective-permute-done | bytes 458784 | tf_op jit(solution)/shard_map/ppermute | solution.py:17
  156.0 5.7 %near_sums.3.sum_ref = f32[256,512]{1,0:T(8,128)S(1)} custom-call(s32[3]{0:T(128)S(1)} %pad_add_fusion.spot_ref, bf16[128,1792]{1,0:T(8,128)(2,1)} %get-tuple-element.60.refs_0_, bf16[128,1792]{1,0:T(8,128)(2,1)} %get-tuple-element.61.refs_1_, bf16[128,1792]{1,0:T(8,128)(2,1)} %collective-permute-done.14.refs_2_, ...), custom_call_target="tpu_custom_call" | custom-call | tf_op jit(solution)/shard_map/near_sums/pallas_call | solution.py:69
  161.6 4.2 %collective-permute-done.16.first_ref = bf16[128,1792]{1,0:T(8,128)(2,1)S(1)} collective-permute-done((bf16[128,1792]{1,0:T(8,128)(2,1)}, bf16[128,1792]{1,0:T(8,128)(2,1)S(1)}, u32[]{:S(2)}, u32[]{:S(2)}) %collective-permute-start.16) | collective-permute-done | bytes 458784 | tf_op jit(solution)/shard_map/ppermute | solution.py:17
  165.8 2.3 %far_hidden.3.refs_0_ = bf16[256,256]{1,0:T(8,128)(2,1)S(1)} custom-call(s32[1]{0:T(128)} %bitcast.9.spot_ref, bf16[128,1792]{1,0:T(8,128)(2,1)S(1)} %collective-permute-done.16.first_ref, bf16[128,1792]{1,0:T(8,128)(2,1)S(1)} %collective-permute-done.17.second_ref, f32[256,512]{1,0:T(8,128)S(1)} %near_sums.3.sum_ref, bf16[1,7168,256]{2,1,0:T(8,128)(2,1)} %gate_ref.1, ...), custom_call_target="tpu_custom_call" | custom-call | tf_op jit(solution)/shard_map/far_hidden/pallas_call | solution.py:110
  168.2 1.5 collective-permute-start.21
  169.7 2.5 %collected.1 = f32[320,1792]{1,0:T(8,128)S(1)} custom-call(s32[320,1]{1,0:T(8,128)S(1)} %select_n.139.slot_ref, bf16[512,1792]{1,0:T(8,128)(2,1)} %bitcast.14.back_ref), custom_call_target="tpu_custom_call" | custom-call | flops 49999998976 | bytes 250000000 | tf_op jit(solution)/shard_map/collected/pallas_call | solution.py:201
  172.2 1.5 copy-done.2
  173.9 2.9 %collective-permute-done.20.refs_1_ = bf16[256,256]{1,0:T(8,128)(2,1)S(1)} collective-permute-done((bf16[256,256]{1,0:T(8,128)(2,1)S(1)}, bf16[256,256]{1,0:T(8,128)(2,1)S(1)}, u32[]{:S(2)}, u32[]{:S(2)}) %collective-permute-start.20) | collective-permute-done | bytes 131104 | tf_op jit(solution)/shard_map/ppermute | solution.py:17
  176.8 3.5 %projected.3 = bf16[256,1792]{1,0:T(8,128)(2,1)} custom-call(bf16[256,256]{1,0:T(8,128)(2,1)S(1)} %far_hidden.3.refs_0_, bf16[256,256]{1,0:T(8,128)(2,1)S(1)} %collective-permute-done.20.refs_1_, bf16[256,256]{1,0:T(8,128)(2,1)S(1)} %collective-permute-done.21.refs_2_, bf16[256,256]{1,0:T(8,128)(2,1)S(1)} %collective-permute-done.22.refs_3_, ...), custom_call_target="tpu_custom_call" | custom-call | tf_op jit(solution)/shard_map/projected/pallas_call | solution.py:156
  180.3 8.5 %all-to-all-start.3 = ((bf16[32,8,1792]{2,1,0:T(8,128)(2,1)}), bf16[32,8,1792]{2,1,0:T(8,128)(2,1)}, u32[]{:S(2)}, u32[]{:S(2)}) async-start(bf16[32,8,1792]{2,1,0:T(8,128)(2,1)} %bitcast.30), calls=%async_computation.3 | async-start | bytes 1835008 | tf_op jit(solution)/shard_map/all_to_all | solution.py:217
  188.8 7.1 %broadcast_select_fusion.1 = (bf16[1,7168,256]{2,1,0:T(8,128)(2,1)}, bf16[1,7168,256]{2,1,0:T(8,128)(2,1)}) fusion(bf16[1,7168,256]{2,1,0:T(8,128)(2,1)} %collective-permute-done.1, bf16[1,7168,256]{2,1,0:T(8,128)(2,1)} %up_ref.1, pred[]{:T(512)S(6)} %ne.72, bf16[1,7168,256]{2,1,0:T(8,128)(2,1)} %collective-permute-done, bf16[1,7168,256]{2,1,0:T(8,128)(2,1)} %gate_ref.1), kind=kLoop, calls=%fused_computation.1 | loop fusion | flops 3670016 | bytes 22020096 | tf_op jit(solution)/shard_map/jit(_where)/select_n | solution.py:315
  195.9 2.3 %broadcast_select_fusion = bf16[1,256,7168]{2,1,0:T(8,128)(2,1)} fusion(bf16[1,256,7168]{2,1,0:T(8,128)(2,1)} %collective-permute-done.23, bf16[1,256,7168]{2,1,0:T(8,128)(2,1)S(1)} %copy-done.4, pred[]{:T(512)S(6)} %ne.72), kind=kLoop, calls=%fused_computation | loop fusion | flops 1835008 | bytes 11010049 | tf_op jit(solution)/shard_map/jit(_where)/select_n | solution.py:315
  198.2 6.4 %all-to-all-done.3 = bf16[32,8,1792]{2,1,0:T(8,128)(2,1)} async-done(((bf16[32,8,1792]{2,1,0:T(8,128)(2,1)}), bf16[32,8,1792]{2,1,0:T(8,128)(2,1)}, u32[]{:S(2)}, u32[]{:S(2)}) %all-to-all-start.3) | async-done | bytes 917536 | tf_op jit(solution)/shard_map/all_to_all | solution.py:217
  204.6 1.8 fusion.2
  206.4 1.4 multiply_convert_fusion
  (58 shorter events, 6.5 us)
Async XLA Ops:
  0.6 9.8 %copy-start = (bf16[320,1792]{1,0:T(8,128)(2,1)S(1)}, bf16[320,1792]{1,0:T(8,128)(2,1)}, u32[]{:S(2)}) copy-start(bf16[320,1792]{1,0:T(8,128)(2,1)} %param.7) | copy-start | bytes 3440644
  0.6 49.0 %collective-permute-start = (bf16[1,7168,256]{2,1,0:T(8,128)(2,1)}, bf16[1,7168,256]{2,1,0:T(8,128)(2,1)}, u32[]{:S(2)}, u32[]{:S(2)}) collective-permute-start(bf16[1,7168,256]{2,1,0:T(8,128)(2,1)} %gate_ref.1), channel_id=1, source_target_pairs={{0,1},{1,0},{2,3},{3,2},{4,5},{5,4},{6,7},{7,6},{8,9},{9,8},{10,11... | collective-permute-start | bytes 11010056 | tf_op jit(solution)/shard_map/ppermute | solution.py:21
  2.1 47.5 %collective-permute-start.1 = (bf16[1,7168,256]{2,1,0:T(8,128)(2,1)}, bf16[1,7168,256]{2,1,0:T(8,128)(2,1)}, u32[]{:S(2)}, u32[]{:S(2)}) collective-permute-start(bf16[1,7168,256]{2,1,0:T(8,128)(2,1)} %up_ref.1), channel_id=1, source_target_pairs={{0,1},{1,0},{2,3},{3,2},{4,5},{5,4},{6,7},{7,6},{8,9},{9,8},{10,11... | collective-permute-start | bytes 11010056 | tf_op jit(solution)/shard_map/ppermute | solution.py:21
  2.2 7.9 %copy-start.8 = (s32[320,8]{0,1:T(8,128)S(1)}, s32[320,8]{0,1:T(8,128)}, u32[]{:S(2)}) copy-start(s32[320,8]{0,1:T(8,128)} %param.8) | copy-start | bytes 30724
  5.9 23.4 %collective-permute-start.4 = (bf16[256,1792]{1,0:T(8,128)(2,1)}, bf16[256,1792]{1,0:T(8,128)(2,1)S(1)}, u32[]{:S(2)}, u32[]{:S(2)}) collective-permute-start(bf16[256,1792]{1,0:T(8,128)(2,1)} %get-tuple-element.90), channel_id=1, source_target_pairs={{0,64},{32,96},{64,0},{96,32},{1,65},{33,97},{65,1},{97,33},{2,66}... | collective-permute-start | bytes 2752520 | tf_op jit(solution)/shard_map/ppermute | solution.py:17
  8.7 40.4 %collective-permute-start.3 = (bf16[256,1792]{1,0:T(8,128)(2,1)}, bf16[256,1792]{1,0:T(8,128)(2,1)}, u32[]{:S(2)}, u32[]{:S(2)}) collective-permute-start(bf16[256,1792]{1,0:T(8,128)(2,1)} %get-tuple-element.91), channel_id=1, source_target_pairs={{0,96},{32,0},{64,32},{96,64},{1,97},{33,1},{65,33},{97,65},{2,98}... | collective-permute-start | bytes 2752520 | tf_op jit(solution)/shard_map/ppermute | solution.py:17
  9.5 40.1 %collective-permute-start.2 = (bf16[256,1792]{1,0:T(8,128)(2,1)}, bf16[256,1792]{1,0:T(8,128)(2,1)}, u32[]{:S(2)}, u32[]{:S(2)}) collective-permute-start(bf16[256,1792]{1,0:T(8,128)(2,1)} %get-tuple-element.92), channel_id=1, source_target_pairs={{0,32},{32,64},{64,96},{96,0},{1,33},{33,65},{65,97},{97,1},{2,34}... | collective-permute-start | bytes 2752520 | tf_op jit(solution)/shard_map/ppermute | solution.py:17
  12.7 36.9 %copy-start.9 = (f32[320,8]{0,1:T(8,128)S(1)}, f32[320,8]{0,1:T(8,128)}, u32[]{:S(2)}) copy-start(f32[320,8]{0,1:T(8,128)} %param.9) | copy-start | bytes 30724
  12.7 37.2 %all-to-all-start = ((bf16[32,16,1792]{2,1,0:T(8,128)(2,1)}), bf16[32,16,1792]{2,1,0:T(8,128)(2,1)}, u32[]{:S(2)}, u32[]{:S(2)}) async-start(bf16[32,16,1792]{2,1,0:T(8,128)(2,1)} %bitcast.32), calls=%async_computation | async-start | bytes 3670016 | tf_op jit(solution)/shard_map/all_to_all | solution.py:217
  53.5 17.2 %collective-permute-start.7 = (bf16[192,1792]{1,0:T(8,128)(2,1)}, bf16[192,1792]{1,0:T(8,128)(2,1)}, u32[]{:S(2)}, u32[]{:S(2)}) collective-permute-start(bf16[192,1792]{1,0:T(8,128)(2,1)} %get-tuple-element.94.refs_1_), channel_id=1, source_target_pairs={{0,96},{32,0},{64,32},{96,64},{1,97},{33,1},{65,33},{97,65},{2,98}... | collective-permute-start | bytes 2064392 | tf_op jit(solution)/shard_map/ppermute | solution.py:17
  56.1 18.0 %collective-permute-start.5 = (bf16[192,1792]{1,0:T(8,128)(2,1)}, bf16[192,1792]{1,0:T(8,128)(2,1)}, u32[]{:S(2)}, u32[]{:S(2)}) collective-permute-start(bf16[192,1792]{1,0:T(8,128)(2,1)} %get-tuple-element.95.refs_0_), channel_id=1, source_target_pairs={{0,32},{32,64},{64,96},{96,0},{1,33},{33,65},{65,97},{97,1},{2,34}... | collective-permute-start | bytes 2064392 | tf_op jit(solution)/shard_map/ppermute | solution.py:17
  57.7 49.8 %all-to-all-start.1 = ((bf16[32,8,1792]{2,1,0:T(8,128)(2,1)}), bf16[32,8,1792]{2,1,0:T(8,128)(2,1)}, u32[]{:S(2)}, u32[]{:S(2)}) async-start(bf16[32,8,1792]{2,1,0:T(8,128)(2,1)} %fusion), calls=%async_computation.1 | async-start | bytes 1835008 | tf_op jit(solution)/shard_map/all_to_all | solution.py:217
  66.6 21.9 %collective-permute-start.9 = (bf16[192,1792]{1,0:T(8,128)(2,1)}, bf16[192,1792]{1,0:T(8,128)(2,1)S(1)}, u32[]{:S(2)}, u32[]{:S(2)}) collective-permute-start(bf16[192,1792]{1,0:T(8,128)(2,1)} %get-tuple-element.94.refs_1_), channel_id=1, source_target_pairs={{0,32},{32,64},{64,96},{96,0},{1,33},{33,65},{65,97},{97,1},{2,34}... | collective-permute-start | bytes 2064392 | tf_op jit(solution)/shard_map/ppermute | solution.py:17
  67.2 21.3 %collective-permute-start.10 = (bf16[192,1792]{1,0:T(8,128)(2,1)}, bf16[192,1792]{1,0:T(8,128)(2,1)S(1)}, u32[]{:S(2)}, u32[]{:S(2)}) collective-permute-start(bf16[192,1792]{1,0:T(8,128)(2,1)} %get-tuple-element.95.refs_0_), channel_id=1, source_target_pairs={{0,96},{32,0},{64,32},{96,64},{1,97},{33,1},{65,33},{97,65},{2,98}... | collective-permute-start | bytes 2064392 | tf_op jit(solution)/shard_map/ppermute | solution.py:17
  70.7 29.5 %collective-permute-start.8 = (bf16[192,1792]{1,0:T(8,128)(2,1)}, bf16[192,1792]{1,0:T(8,128)(2,1)S(1)}, u32[]{:S(2)}, u32[]{:S(2)}) collective-permute-start(bf16[192,1792]{1,0:T(8,128)(2,1)} %collective-permute-done.7.refs_5_), channel_id=1, source_target_pairs={{0,96},{32,0},{64,32},{96,64},{1,97},{33,1},{65,33},{97,65},{2,98}... | collective-permute-start | bytes 2064392 | tf_op jit(solution)/shard_map/ppermute | solution.py:17
  74.2 29.1 %collective-permute-start.6 = (bf16[192,1792]{1,0:T(8,128)(2,1)}, bf16[192,1792]{1,0:T(8,128)(2,1)S(1)}, u32[]{:S(2)}, u32[]{:S(2)}) collective-permute-start(bf16[192,1792]{1,0:T(8,128)(2,1)} %collective-permute-done.5.refs_2_), channel_id=1, source_target_pairs={{0,32},{32,64},{64,96},{96,0},{1,33},{33,65},{65,97},{97,1},{2,34}... | collective-permute-start | bytes 2064392 | tf_op jit(solution)/shard_map/ppermute | solution.py:17
  88.5 0.8 copy-start.5
  89.3 0.9 copy-start.6
  105.8 6.2 %collective-permute-start.13 = (bf16[384,256]{1,0:T(8,128)(2,1)S(1)}, bf16[384,256]{1,0:T(8,128)(2,1)S(1)}, u32[]{:S(2)}, u32[]{:S(2)}) collective-permute-start(bf16[384,256]{1,0:T(8,128)(2,1)S(1)} %far_hidden.2.refs_0_), channel_id=1, source_target_pairs={{0,64},{32,96},{64,0},{96,32},{1,65},{33,97},{65,1},{97,33},{2,66}... | collective-permute-start | bytes 589832 | tf_op jit(solution)/shard_map/ppermute | solution.py:17
  105.9 9.2 %collective-permute-start.12 = (bf16[384,256]{1,0:T(8,128)(2,1)S(1)}, bf16[384,256]{1,0:T(8,128)(2,1)S(1)}, u32[]{:S(2)}, u32[]{:S(2)}) collective-permute-start(bf16[384,256]{1,0:T(8,128)(2,1)S(1)} %far_hidden.2.refs_0_), channel_id=1, source_target_pairs={{0,96},{32,0},{64,32},{96,64},{1,97},{33,1},{65,33},{97,65},{2,98}... | collective-permute-start | bytes 589832 | tf_op jit(solution)/shard_map/ppermute | solution.py:17
  107.4 10.3 %collective-permute-start.11 = (bf16[384,256]{1,0:T(8,128)(2,1)S(1)}, bf16[384,256]{1,0:T(8,128)(2,1)S(1)}, u32[]{:S(2)}, u32[]{:S(2)}) collective-permute-start(bf16[384,256]{1,0:T(8,128)(2,1)S(1)} %far_hidden.2.refs_0_), channel_id=1, source_target_pairs={{0,32},{32,64},{64,96},{96,0},{1,33},{33,65},{65,97},{97,1},{2,34}... | collective-permute-start | bytes 589832 | tf_op jit(solution)/shard_map/ppermute | solution.py:17
  117.7 12.3 %collective-permute-start.14 = (bf16[128,1792]{1,0:T(8,128)(2,1)}, bf16[128,1792]{1,0:T(8,128)(2,1)}, u32[]{:S(2)}, u32[]{:S(2)}) collective-permute-start(bf16[128,1792]{1,0:T(8,128)(2,1)} %get-tuple-element.60.refs_0_), channel_id=1, source_target_pairs={{0,32},{32,64},{64,96},{96,0},{1,33},{33,65},{65,97},{97,1},{2,34}... | collective-permute-start | bytes 1376264 | tf_op jit(solution)/shard_map/ppermute | solution.py:17
  117.7 12.3 %collective-permute-start.15 = (bf16[128,1792]{1,0:T(8,128)(2,1)}, bf16[128,1792]{1,0:T(8,128)(2,1)S(1)}, u32[]{:S(2)}, u32[]{:S(2)}) collective-permute-start(bf16[128,1792]{1,0:T(8,128)(2,1)} %get-tuple-element.61.refs_1_), channel_id=1, source_target_pairs={{0,96},{32,0},{64,32},{96,64},{1,97},{33,1},{65,33},{97,65},{2,98}... | collective-permute-start | bytes 1376264 | tf_op jit(solution)/shard_map/ppermute | solution.py:17
  125.8 20.0 %copy-start.10 = (s32[32]{0:T(128)S(1)}, s32[32]{0:T(128)}, u32[]{:S(2)}) copy-start(s32[32]{0:T(128)} %param.10) | copy-start | bytes 388
  130.0 13.0 %copy-start.7 = (bf16[128,1792]{1,0:T(8,128)(2,1)}, bf16[128,1792]{1,0:T(8,128)(2,1)S(1)}, u32[]{:S(2)}) copy-start(bf16[128,1792]{1,0:T(8,128)(2,1)S(1)} %collective-permute-done.15.refs_5_) | copy-start | bytes 1376260
  130.0 39.7 %all-to-all-start.2 = ((bf16[32,16,1792]{2,1,0:T(8,128)(2,1)}), bf16[32,16,1792]{2,1,0:T(8,128)(2,1)}, u32[]{:S(2)}, u32[]{:S(2)}) async-start(bf16[32,16,1792]{2,1,0:T(8,128)(2,1)} %bitcast.31), calls=%async_computation.2 | async-start | bytes 3670016 | tf_op jit(solution)/shard_map/all_to_all | solution.py:217
  140.3 12.6 %collective-permute-start.19 = (bf16[128,1792]{1,0:T(8,128)(2,1)}, bf16[128,1792]{1,0:T(8,128)(2,1)}, u32[]{:S(2)}, u32[]{:S(2)}) collective-permute-start(bf16[128,1792]{1,0:T(8,128)(2,1)} %get-tuple-element.60.refs_0_), channel_id=1, source_target_pairs={{0,96},{32,0},{64,32},{96,64},{1,97},{33,1},{65,33},{97,65},{2,98}... | collective-permute-start | bytes 1376264 | tf_op jit(solution)/shard_map/ppermute | solution.py:17
  143.0 13.0 %collective-permute-start.18 = (bf16[128,1792]{1,0:T(8,128)(2,1)}, bf16[128,1792]{1,0:T(8,128)(2,1)}, u32[]{:S(2)}, u32[]{:S(2)}) collective-permute-start(bf16[128,1792]{1,0:T(8,128)(2,1)} %get-tuple-element.61.refs_1_), channel_id=1, source_target_pairs={{0,32},{32,64},{64,96},{96,0},{1,33},{33,65},{65,97},{97,1},{2,34}... | collective-permute-start | bytes 1376264 | tf_op jit(solution)/shard_map/ppermute | solution.py:17
  143.0 22.8 %collective-permute-start.16 = (bf16[128,1792]{1,0:T(8,128)(2,1)}, bf16[128,1792]{1,0:T(8,128)(2,1)S(1)}, u32[]{:S(2)}, u32[]{:S(2)}) collective-permute-start(bf16[128,1792]{1,0:T(8,128)(2,1)} %collective-permute-done.14.refs_2_), channel_id=1, source_target_pairs={{0,32},{32,64},{64,96},{96,0},{1,33},{33,65},{65,97},{97,1},{2,34}... | collective-permute-start | bytes 1376264 | tf_op jit(solution)/shard_map/ppermute | solution.py:17
  143.0 22.8 %collective-permute-start.17 = (bf16[128,1792]{1,0:T(8,128)(2,1)}, bf16[128,1792]{1,0:T(8,128)(2,1)S(1)}, u32[]{:S(2)}, u32[]{:S(2)}) collective-permute-start(bf16[128,1792]{1,0:T(8,128)(2,1)} %copy-done.7), channel_id=1, source_target_pairs={{0,96},{32,0},{64,32},{96,64},{1,97},{33,1},{65,33},{97,65},{2,98}... | collective-permute-start | bytes 1376264 | tf_op jit(solution)/shard_map/ppermute | solution.py:17
  146.9 33.4 %collective-permute-start.23 = (bf16[1,256,7168]{2,1,0:T(8,128)(2,1)}, bf16[1,256,7168]{2,1,0:T(8,128)(2,1)}, u32[]{:S(2)}, u32[]{:S(2)}) collective-permute-start(bf16[1,256,7168]{2,1,0:T(8,128)(2,1)} %param.13), channel_id=1, source_target_pairs={{0,1},{1,0},{2,3},{3,2},{4,5},{5,4},{6,7},{7,6},{8,9},{9,8},{10,11... | collective-permute-start | bytes 11010056 | tf_op jit(solution)/shard_map/ppermute | solution.py:21
  168.1 5.6 %collective-permute-start.22 = (bf16[256,256]{1,0:T(8,128)(2,1)S(1)}, bf16[256,256]{1,0:T(8,128)(2,1)S(1)}, u32[]{:S(2)}, u32[]{:S(2)}) collective-permute-start(bf16[256,256]{1,0:T(8,128)(2,1)S(1)} %far_hidden.3.refs_0_), channel_id=1, source_target_pairs={{0,64},{32,96},{64,0},{96,32},{1,65},{33,97},{65,1},{97,33},{2,66}... | collective-permute-start | bytes 393224 | tf_op jit(solution)/shard_map/ppermute | solution.py:17
  168.2 5.7 %collective-permute-start.21 = (bf16[256,256]{1,0:T(8,128)(2,1)S(1)}, bf16[256,256]{1,0:T(8,128)(2,1)S(1)}, u32[]{:S(2)}, u32[]{:S(2)}) collective-permute-start(bf16[256,256]{1,0:T(8,128)(2,1)S(1)} %far_hidden.3.refs_0_), channel_id=1, source_target_pairs={{0,96},{32,0},{64,32},{96,64},{1,97},{33,1},{65,33},{97,65},{2,98}... | collective-permute-start | bytes 393224 | tf_op jit(solution)/shard_map/ppermute | solution.py:17
  169.7 7.1 %collective-permute-start.20 = (bf16[256,256]{1,0:T(8,128)(2,1)S(1)}, bf16[256,256]{1,0:T(8,128)(2,1)S(1)}, u32[]{:S(2)}, u32[]{:S(2)}) collective-permute-start(bf16[256,256]{1,0:T(8,128)(2,1)S(1)} %far_hidden.3.refs_0_), channel_id=1, source_target_pairs={{0,32},{32,64},{64,96},{96,0},{1,33},{33,65},{65,97},{97,1},{2,34}... | collective-permute-start | bytes 393224 | tf_op jit(solution)/shard_map/ppermute | solution.py:17
  172.2 1.5 copy-start.2
  180.3 24.3 %all-to-all-start.3 = ((bf16[32,8,1792]{2,1,0:T(8,128)(2,1)}), bf16[32,8,1792]{2,1,0:T(8,128)(2,1)}, u32[]{:S(2)}, u32[]{:S(2)}) async-start(bf16[32,8,1792]{2,1,0:T(8,128)(2,1)} %bitcast.30), calls=%async_computation.3 | async-start | bytes 1835008 | tf_op jit(solution)/shard_map/all_to_all | solution.py:217
  188.8 7.1 %copy-start.4 = (bf16[1,256,7168]{2,1,0:T(8,128)(2,1)S(1)}, bf16[1,256,7168]{2,1,0:T(8,128)(2,1)}, u32[]{:S(2)}) copy-start(bf16[1,256,7168]{2,1,0:T(8,128)(2,1)} %param.13) | copy-start | bytes 11010052
  198.2 8.2 %copy-start.3 = (f32[320,1792]{1,0:T(8,128)S(1)}, f32[320,1792]{1,0:T(8,128)}, u32[]{:S(2)}) copy-start(f32[320,1792]{1,0:T(8,128)} %copy-done.2) | copy-start | bytes 6881284
  204.6 3.2 %copy-start.1 = (bf16[320,1792]{1,0:T(8,128)(2,1)S(1)}, bf16[320,1792]{1,0:T(8,128)(2,1)}, u32[]{:S(2)}) copy-start(bf16[320,1792]{1,0:T(8,128)(2,1)} %param.7) | copy-start | bytes 3440644

commit v4 on v3

--- a/solution.py
+++ b/solution.py
@@ -78,7 +78,7 @@
         compiler_params=PARAMS,
         cost_estimate=FREE,
         name="near_sums",
-    )(spots, *map(in_hbm, pieces), in_hbm(w_gate), in_hbm(w_up))
+    )(spots, *pieces, in_hbm(w_gate), in_hbm(w_up))
 
 
 def far_hidden(halves, sums, spots, w_gate, w_up):
@@ -196,11 +196,11 @@
             place = lax.broadcasted_iota(jnp.int32, (count, slots), 1)
             pick[...] = jnp.where(place == slot_ref[...], 1.0, 0.0).astype(jnp.bfloat16)
 
-        out_ref[...] = dot32(pick[...], back_ref[...])
-
-    return pl.pallas_call(
-        kernel,
-        out_shape=jax.ShapeDtypeStruct((count, width), jnp.float32),
+        out_ref[...] = dot32(pick[...], back_ref[...]).astype(out_ref.dtype)
+
+    return pl.pallas_call(
+        kernel,
+        out_shape=pltpu.HBM((count, width), jnp.bfloat16),
         grid=(pieces,),
         in_specs=[whole((count, 1)), pl.BlockSpec((slots, width // pieces), lambda i: (0, i))],
         out_specs=pl.BlockSpec((count, width // pieces), lambda i: (0, i)),
@@ -209,6 +209,36 @@
         cost_estimate=LONG,
         name="collected",
     )(slot, in_hbm(back))
+
+
+def mixed_rows(slot, back, total, weight):
+    count, width = total.shape
+    slots = back.shape[0]
+    pieces = 2
+
+    def kernel(slot_ref, back_ref, total_ref, weight_ref, out_ref, pick):
+        @pl.when(pl.program_id(0) == 0)
+        def _():
+            place = lax.broadcasted_iota(jnp.int32, (count, slots), 1)
+            pick[...] = jnp.where(place == slot_ref[...], 1.0, 0.0).astype(jnp.bfloat16)
+
+        rows = total_ref[...].astype(jnp.float32) + dot32(pick[...], back_ref[...])
+        out_ref[...] = (weight_ref[...] * rows).astype(out_ref.dtype)
+
+    def columns(rows):
+        return pl.BlockSpec((rows, width // pieces), lambda i: (0, i))
+
+    return pl.pallas_call(
+        kernel,
+        out_shape=jax.ShapeDtypeStruct((count, width), jnp.bfloat16),
+        grid=(pieces,),
+        in_specs=[whole((count, 1)), columns(slots), columns(count), whole((count, 1))],
+        out_specs=columns(count),
+        scratch_shapes=[pltpu.VMEM((count, slots), jnp.bfloat16)],
+        compiler_params=PARAMS,
+        cost_estimate=FREE,
+        name="mixed_rows",
+    )(slot, back, total, weight)
 
 
 def exchanged(rows):
@@ -288,10 +318,12 @@
     near_spots = jnp.stack(spots[:3]).astype(jnp.int32)
     far_spots = jnp.stack(spots[3:]).astype(jnp.int32)
 
-    def activations(halves, near):
+    def activations(halves, near, early):
         far = first_step(near)
         left = (near[0], shifted(halves[1], 1))
         right = (shifted(halves[0], -1), near[1])
+        if early:
+            (left, right), early[:] = tied((left, right), early)
         sums = near_sums((halves, left, right), near_spots, gate_own, up_own)
         hidden = far_hidden(far, sums, far_spots, gate_own, up_own)
         return [hidden, shifted(hidden, 1), shifted(hidden, -1), shifted(hidden, 2)]
@@ -299,24 +331,23 @@
     def project(chunk, hidden, cost):
         return projected(hidden, down, chunk[1], chunk[2], cost)
 
+    placed = [jnp.where(moved, o, w) for o, w in zip(swaps, own)]
     halves_a = split(live_rows(CHUNKS[0], got_a))
-    hidden_a = activations(halves_a, first_step(halves_a))
+    hidden_a = activations(halves_a, first_step(halves_a), placed)
     halves_b = split(live_rows(CHUNKS[1], got_b))
     halves_b, hidden_a = tied(halves_b, hidden_a)
     near = first_step(halves_b)
     out_a = project(CHUNKS[0], hidden_a, LONG)
     near, out_a = tied(near, out_a)
     back_a = exchanged(out_a)
-    hidden_b = activations(halves_b, near)
+    hidden_b = activations(halves_b, near, [])
     other = swapped(own[2])
     total, hidden_b = tied(collected(slot_a[:, None], back_a), hidden_b)
     out_b = project(CHUNKS[1], hidden_b, FREE)
-    swaps, other, out_b, own = tied(swaps, other, out_b, own)
-    placed = [jnp.where(moved, o, w) for o, w in zip((*swaps, other), own)]
+    other, out_b, last = tied(other, out_b, own[2])
+    placed.append(jnp.where(moved, other, last))
     back_b = exchanged(out_b)
-    slots = jnp.arange(back_b.shape[0], dtype=jnp.int32)
-    total = total + dot32(matches(slot_b, slots), back_b)
-    mixed = (gate_weight * total).astype(jnp.bfloat16)
+    mixed = mixed_rows(slot_b[:, None], back_b, total, gate_weight)
     return (mixed, *placed)
 
 

time: 209 us -> 201 us (0.962)
  waiting for transfers between devices: 82.7 us -> 70.6 us
  starting transfers between devices: 64.7 us -> 72.8 us
  local copies, waits for them, and re-layouts: 11.1 us -> 6.65 us
    ppermute x21, waiting for transfers between devices: 76.3 us -> 59.2 us  [shifted(): lax.ppermute(value, 'dp', [(i, (i + step) % size) for i in range(size)])]
    all_to_all x4, waiting for transfers between devices: 6.43 us -> 11.3 us  [exchanged(): lax.all_to_all(blocks, 'expert', split_axis=0, concat_axis=0, tiled=True)]
    all_to_all x4, starting transfers between devices: 37.2 us -> 41.5 us  [exchanged(): lax.all_to_all(blocks, 'expert', split_axis=0, concat_axis=0, tiled=True)]
    ppermute x21, starting transfers between devices: 24.6 us -> 28.3 us  [shifted(): lax.ppermute(value, 'dp', [(i, (i + step) % size) for i in range(size)])]
    unnamed x23 -> x21, local copies, waits for them, and re-layouts: 3.39 us -> 0.83 us
    pallas_call x1 -> x2, Pallas kernels: 2.46 us -> 4.96 us  [the longest x1 3.15 us: collected(): pl.pallas_call(kernel, out_shape=pltpu.HBM((count, width), jnp.bfloat16),...]
    dot_general x5 -> x4, matrix products: 8.29 us -> 6.51 us  [dot32(): return jnp.dot(left, right, preferred_element_type=jnp.float32)]
  transfers between devices with their start and end apart: 28 -> 28, of which waited for: 17 -> 11; matrix products, arithmetic and copies ran while one was open for 10% -> 11% of each run, Pallas kernels for 14% -> 14%
where the time goes in v4:
time: 201 us; the launch traced here: 200 us
  starting transfers between devices  72.8 us (36%)
  waiting for transfers between devices  70.6 us (35%)
  Pallas kernels  30.3 us (15%)
  other arithmetic  11.4 us (6%)
  local copies, waits for them, and re-layouts  6.65 us (3%)
  matrix products  6.51 us (3%)
    ppermute x21, waiting for transfers between devices, shifted(): lax.ppermute(value, 'dp', [(i, (i + step) % size) for i in range(size)])  59.2 us
    all_to_all x4, starting transfers between devices, exchanged(): lax.all_to_all(blocks, 'expert', split_axis=0, concat_axis=0, tiled=True)  41.5 us
    ppermute x21, starting transfers between devices, shifted(): lax.ppermute(value, 'dp', [(i, (i + step) % size) for i in range(size)])  28.3 us
    all_to_all x4, waiting for transfers between devices, exchanged(): lax.all_to_all(blocks, 'expert', split_axis=0, concat_axis=0, tiled=True)  11.3 us
    pallas_call x2, Pallas kernels, near_sums(): pl.pallas_call(kernel, out_shape=jax.ShapeDtypeStruct((count, 2 * units),...  11.2 us
    pallas_call x2, Pallas kernels, projected(): pl.pallas_call(kernel, out_shape=pltpu.HBM((slots, width), jnp.bfloat16),...  9.04 us
    select_n x1, other arithmetic, body(): placed = [jnp.where(moved, o, w) for o, w in zip(swaps, own)]  6.91 us
    dot_general x4, matrix products, dot32(): return jnp.dot(left, right, preferred_element_type=jnp.float32)  6.51 us
  transfers between devices with their start and end apart: 28, of which 11 were waited for; matrix products, arithmetic and copies ran while one was open for 11% of the time, Pallas kernels for 14%

profile of v4, /device:TPU:1, one launch (start us, length us, event | category | flops | bytes accessed | tf_op | source)
XLA Modules:
  0.0 199.8 jit_solution(6810095562598394961)
XLA Ops:
  0.6 1.5 collective-permute-start
  2.2 3.6 %dynamic-slice_bitcast_fusion = (bf16[256,1792]{1,0:T(8,128)(2,1)}, bf16[256,1792]{1,0:T(8,128)(2,1)}, bf16[256,1792]{1,0:T(8,128)(2,1)}, bf16[256,1792]{1,0:T(8,128)(2,1)S(1)}) fusion(bf16[1,256,7168]{2,1,0:T(8,128)(2,1)} %param.13, s32[]{:T(128)S(6)} %select_n.136, s32[]{:T(128)S(6)} %select_n.134, s32[]{:T(128)S(6)} %select_n.132, s32[]{:T(128)S(6)} %select_n.130), kind=kLoop, calls=%fused_computation.9 | loop fusion | bytes 7340048 | tf_op jit(solution)/shard_map/dynamic_slice | solution.py:289
  5.9 1.3 collective-permute-start.2
  7.2 1.4 collective-permute-start.3
  8.5 1.6 collective-permute-start.4
  10.4 2.3 %convolution_convert_fusion = bf16[512,1792]{1,0:T(8,128)(2,1)} fusion(bf16[320,1792]{1,0:T(8,128)(2,1)S(1)} %copy-done, s32[320]{0:T(512)S(1)} %get-tuple-element.102), kind=kOutput, calls=%fused_computation.3 | convolution fusion | flops 588283904 | bytes 2983168 | tf_op jit(solution)/shard_map/dot_general | solution.py:25
  12.7 9.5 %all-to-all-start = ((bf16[32,16,1792]{2,1,0:T(8,128)(2,1)}), bf16[32,16,1792]{2,1,0:T(8,128)(2,1)}, u32[]{:S(2)}, u32[]{:S(2)}) async-start(bf16[32,16,1792]{2,1,0:T(8,128)(2,1)} %bitcast.31), calls=%async_computation | async-start | bytes 3670016 | tf_op jit(solution)/shard_map/all_to_all | solution.py:247
  22.4 6.5 %collective-permute-done.2.refs_5_ = bf16[256,1792]{1,0:T(8,128)(2,1)S(1)} collective-permute-done((bf16[256,1792]{1,0:T(8,128)(2,1)}, bf16[256,1792]{1,0:T(8,128)(2,1)S(1)}, u32[]{:S(2)}, u32[]{:S(2)}) %collective-permute-start.2) | collective-permute-done | bytes 917536 | tf_op jit(solution)/shard_map/ppermute | solution.py:17
  28.9 20.7 %collective-permute-done.4.refs_7_ = bf16[256,1792]{1,0:T(8,128)(2,1)} collective-permute-done((bf16[256,1792]{1,0:T(8,128)(2,1)}, bf16[256,1792]{1,0:T(8,128)(2,1)}, u32[]{:S(2)}, u32[]{:S(2)}) %collective-permute-start.4) | collective-permute-done | bytes 917536 | tf_op jit(solution)/shard_map/ppermute | solution.py:17
  50.0 0.7 copy-done.5
  50.6 2.4 %convolution_convert_fusion.1 = bf16[384,1792]{1,0:T(8,128)(2,1)S(1)} fusion(bf16[512,1792]{1,0:T(8,128)(2,1)} %bitcast.1, s32[384]{0:T(512)S(1)} %fusion.12), kind=kOutput, calls=%fused_computation.4 | convolution fusion | flops 705527808 | bytes 3212800 | tf_op jit(solution)/shard_map/dot_general | solution.py:25
  53.8 2.1 %collective-permute-start.8 = (bf16[192,1792]{1,0:T(8,128)(2,1)S(1)}, bf16[192,1792]{1,0:T(8,128)(2,1)}, u32[]{:S(2)}, u32[]{:S(2)}) collective-permute-start(bf16[192,1792]{1,0:T(8,128)(2,1)S(1)} %get-tuple-element.98.refs_1_), channel_id=1, source_target_pairs={{0,96},{32,0},{64,32},{96,64},{1,97},{33,1},{65,33},{97,65},{2,98}... | collective-permute-start | bytes 2064392 | tf_op jit(solution)/shard_map/ppermute | solution.py:17
  57.3 2.7 %collective-permute-start.11 = (bf16[192,1792]{1,0:T(8,128)(2,1)S(1)}, bf16[192,1792]{1,0:T(8,128)(2,1)}, u32[]{:S(2)}, u32[]{:S(2)}) collective-permute-start(bf16[192,1792]{1,0:T(8,128)(2,1)S(1)} %get-tuple-element.99.refs_0_), channel_id=1, source_target_pairs={{0,96},{32,0},{64,32},{96,64},{1,97},{33,1},{65,33},{97,65},{2,98}... | collective-permute-start | bytes 2064392 | tf_op jit(solution)/shard_map/ppermute | solution.py:17
  59.9 1.5 fusion
  61.5 10.5 %all-to-all-start.1 = ((bf16[32,8,1792]{2,1,0:T(8,128)(2,1)}), bf16[32,8,1792]{2,1,0:T(8,128)(2,1)}, u32[]{:S(2)}, u32[]{:S(2)}) async-start(bf16[32,8,1792]{2,1,0:T(8,128)(2,1)} %fusion), calls=%async_computation.1 | async-start | bytes 1835008 | tf_op jit(solution)/shard_map/all_to_all | solution.py:247
  72.1 2.7 %collective-permute-start.9 = (bf16[192,1792]{1,0:T(8,128)(2,1)}, bf16[192,1792]{1,0:T(8,128)(2,1)S(1)}, u32[]{:S(2)}, u32[]{:S(2)}) collective-permute-start(bf16[192,1792]{1,0:T(8,128)(2,1)} %collective-permute-done.8.refs_5_), channel_id=1, source_target_pairs={{0,96},{32,0},{64,32},{96,64},{1,97},{33,1},{65,33},{97,65},{2,98}... | collective-permute-start | bytes 2064392 | tf_op jit(solution)/shard_map/ppermute | solution.py:17
  74.8 6.9 %broadcast_select_fusion.1 = (bf16[1,7168,256]{2,1,0:T(8,128)(2,1)}, bf16[1,7168,256]{2,1,0:T(8,128)(2,1)}) fusion(bf16[1,7168,256]{2,1,0:T(8,128)(2,1)} %collective-permute-done.1, bf16[1,7168,256]{2,1,0:T(8,128)(2,1)} %up_ref.1, pred[]{:T(512)S(6)} %ne.72, bf16[1,7168,256]{2,1,0:T(8,128)(2,1)} %collective-permute-done, bf16[1,7168,256]{2,1,0:T(8,128)(2,1)} %gate_ref.1), kind=kLoop, calls=%fused_computation.1 | loop fusion | flops 3670016 | bytes 22020096 | tf_op jit(solution)/shard_map/jit(_where)/select_n | solution.py:334
  81.7 3.3 %collective-permute-done.10.refs_3_ = bf16[192,1792]{1,0:T(8,128)(2,1)} collective-permute-done((bf16[192,1792]{1,0:T(8,128)(2,1)S(1)}, bf16[192,1792]{1,0:T(8,128)(2,1)}, u32[]{:S(2)}, u32[]{:S(2)}) %collective-permute-start.10) | collective-permute-done | bytes 688160 | tf_op jit(solution)/shard_map/ppermute | solution.py:17
  85.0 6.1 %near_sums.2.sum_ref = f32[384,512]{1,0:T(8,128)S(1)} custom-call(s32[3]{0:T(128)S(1)} %pad_add_fusion.spot_ref, bf16[192,1792]{1,0:T(8,128)(2,1)S(1)} %get-tuple-element.99.refs_0_, bf16[192,1792]{1,0:T(8,128)(2,1)S(1)} %get-tuple-element.98.refs_1_, bf16[192,1792]{1,0:T(8,128)(2,1)} %collective-permute-done.6.refs_2_, ...), custom_call_target="tpu_custom_call" | custom-call | tf_op jit(solution)/shard_map/near_sums/pallas_call | solution.py:69
  91.1 8.5 %collective-permute-done.7.first_ref = bf16[192,1792]{1,0:T(8,128)(2,1)S(1)} collective-permute-done((bf16[192,1792]{1,0:T(8,128)(2,1)}, bf16[192,1792]{1,0:T(8,128)(2,1)S(1)}, u32[]{:S(2)}, u32[]{:S(2)}) %collective-permute-start.7) | collective-permute-done | bytes 688160 | tf_op jit(solution)/shard_map/ppermute | solution.py:17
  99.6 2.6 %far_hidden.2.refs_0_ = bf16[384,256]{1,0:T(8,128)(2,1)S(1)} custom-call(s32[1]{0:T(128)} %bitcast.9.spot_ref, bf16[192,1792]{1,0:T(8,128)(2,1)S(1)} %collective-permute-done.7.first_ref, bf16[192,1792]{1,0:T(8,128)(2,1)S(1)} %collective-permute-done.9.second_ref, f32[384,512]{1,0:T(8,128)S(1)} %near_sums.2.sum_ref, bf16[1,7168,256]{2,1,0:T(8,128)(2,1)} %gate_ref.1, ...), custom_call_target="tpu_custom_call" | custom-call | tf_op jit(solution)/shard_map/far_hidden/pallas_call | solution.py:110
  102.5 2.7 %collective-permute-start.13 = (bf16[384,256]{1,0:T(8,128)(2,1)S(1)}, bf16[384,256]{1,0:T(8,128)(2,1)S(1)}, u32[]{:S(2)}, u32[]{:S(2)}) collective-permute-start(bf16[384,256]{1,0:T(8,128)(2,1)S(1)} %far_hidden.2.refs_0_), channel_id=1, source_target_pairs={{0,96},{32,0},{64,32},{96,64},{1,97},{33,1},{65,33},{97,65},{2,98}... | collective-permute-start | bytes 589832 | tf_op jit(solution)/shard_map/ppermute | solution.py:17
  105.2 0.9 collective-permute-start.14
  106.1 1.2 slice_bitcast_fusion
  107.3 0.9 collective-permute-done.12.refs_1_
  108.3 4.3 %collective-permute-done.14.refs_3_ = bf16[384,256]{1,0:T(8,128)(2,1)} collective-permute-done((bf16[384,256]{1,0:T(8,128)(2,1)S(1)}, bf16[384,256]{1,0:T(8,128)(2,1)}, u32[]{:S(2)}, u32[]{:S(2)}) %collective-permute-start.14) | collective-permute-done | bytes 196640 | tf_op jit(solution)/shard_map/ppermute | solution.py:17
  112.6 0.7 collective-permute-start.15
  113.2 2.0 %collective-permute-start.16 = (bf16[128,1792]{1,0:T(8,128)(2,1)S(1)}, bf16[128,1792]{1,0:T(8,128)(2,1)}, u32[]{:S(2)}, u32[]{:S(2)}) collective-permute-start(bf16[128,1792]{1,0:T(8,128)(2,1)S(1)} %get-tuple-element.71.refs_1_), channel_id=1, source_target_pairs={{0,96},{32,0},{64,32},{96,64},{1,97},{33,1},{65,33},{97,65},{2,98}... | collective-permute-start | bytes 1376264 | tf_op jit(solution)/shard_map/ppermute | solution.py:17
  115.2 5.5 %projected.2 = bf16[512,1792]{1,0:T(8,128)(2,1)} custom-call(bf16[384,256]{1,0:T(8,128)(2,1)S(1)} %far_hidden.2.refs_0_, bf16[384,256]{1,0:T(8,128)(2,1)S(1)} %collective-permute-done.12.refs_1_, bf16[384,256]{1,0:T(8,128)(2,1)S(1)} %collective-permute-done.13.refs_2_, bf16[384,256]{1,0:T(8,128)(2,1)} %collective-permute-done.14.refs_3_, ...), custom_call_target="tpu_custom_call" | custom-call | flops 49999998976 | bytes 250000000 | tf_op jit(solution)/shard_map/projected/pallas_call | solution.py:156
  120.7 1.5 collective-permute-done.15.refs_2_
  122.2 12.7 %all-to-all-start.2 = ((bf16[32,16,1792]{2,1,0:T(8,128)(2,1)}), bf16[32,16,1792]{2,1,0:T(8,128)(2,1)}, u32[]{:S(2)}, u32[]{:S(2)}) async-start(bf16[32,16,1792]{2,1,0:T(8,128)(2,1)} %bitcast.30), calls=%async_computation.2 | async-start | bytes 3670016 | tf_op jit(solution)/shard_map/all_to_all | solution.py:247
  135.5 2.3 %collective-permute-start.20 = (bf16[128,1792]{1,0:T(8,128)(2,1)S(1)}, bf16[128,1792]{1,0:T(8,128)(2,1)S(1)}, u32[]{:S(2)}, u32[]{:S(2)}) collective-permute-start(bf16[128,1792]{1,0:T(8,128)(2,1)S(1)} %get-tuple-element.70.refs_0_), channel_id=1, source_target_pairs={{0,96},{32,0},{64,32},{96,64},{1,97},{33,1},{65,33},{97,65},{2,98}... | collective-permute-start | bytes 1376264 | tf_op jit(solution)/shard_map/ppermute | solution.py:17
  137.8 2.7 %collective-permute-start.18 = (bf16[128,1792]{1,0:T(8,128)(2,1)}, bf16[128,1792]{1,0:T(8,128)(2,1)S(1)}, u32[]{:S(2)}, u32[]{:S(2)}) collective-permute-start(bf16[128,1792]{1,0:T(8,128)(2,1)} %collective-permute-done.16.refs_5_), channel_id=1, source_target_pairs={{0,96},{32,0},{64,32},{96,64},{1,97},{33,1},{65,33},{97,65},{2,98}... | collective-permute-start | bytes 1376264 | tf_op jit(solution)/shard_map/ppermute | solution.py:17
  140.7 1.4 collective-permute-start.5
  142.1 6.1 %collective-permute-done.19.refs_3_ = bf16[128,1792]{1,0:T(8,128)(2,1)S(1)} collective-permute-done((bf16[128,1792]{1,0:T(8,128)(2,1)S(1)}, bf16[128,1792]{1,0:T(8,128)(2,1)S(1)}, u32[]{:S(2)}, u32[]{:S(2)}) %collective-permute-start.19) | collective-permute-done | bytes 458784 | tf_op jit(solution)/shard_map/ppermute | solution.py:17
  148.2 5.1 %near_sums.3.sum_ref = f32[256,512]{1,0:T(8,128)S(1)} custom-call(s32[3]{0:T(128)S(1)} %pad_add_fusion.spot_ref, bf16[128,1792]{1,0:T(8,128)(2,1)S(1)} %get-tuple-element.70.refs_0_, bf16[128,1792]{1,0:T(8,128)(2,1)S(1)} %get-tuple-element.71.refs_1_, bf16[128,1792]{1,0:T(8,128)(2,1)} %collective-permute-done.15.refs_2_, ...), custom_call_target="tpu_custom_call" | custom-call | tf_op jit(solution)/shard_map/near_sums/pallas_call | solution.py:69
  153.3 4.6 %collective-permute-done.17.first_ref = bf16[128,1792]{1,0:T(8,128)(2,1)S(1)} collective-permute-done((bf16[128,1792]{1,0:T(8,128)(2,1)}, bf16[128,1792]{1,0:T(8,128)(2,1)S(1)}, u32[]{:S(2)}, u32[]{:S(2)}) %collective-permute-start.17) | collective-permute-done | bytes 458784 | tf_op jit(solution)/shard_map/ppermute | solution.py:17
  157.9 2.3 %far_hidden.3.refs_0_ = bf16[256,256]{1,0:T(8,128)(2,1)S(1)} custom-call(s32[1]{0:T(128)} %bitcast.9.spot_ref, bf16[128,1792]{1,0:T(8,128)(2,1)S(1)} %collective-permute-done.17.first_ref, bf16[128,1792]{1,0:T(8,128)(2,1)S(1)} %collective-permute-done.18.second_ref, f32[256,512]{1,0:T(8,128)S(1)} %near_sums.3.sum_ref, bf16[1,7168,256]{2,1,0:T(8,128)(2,1)} %gate_ref.1, ...), custom_call_target="tpu_custom_call" | custom-call | tf_op jit(solution)/shard_map/far_hidden/pallas_call | solution.py:110
  160.2 0.7 collective-permute-start.21
  160.9 2.0 %collective-permute-start.22 = (bf16[256,256]{1,0:T(8,128)(2,1)S(1)}, bf16[256,256]{1,0:T(8,128)(2,1)S(1)}, u32[]{:S(2)}, u32[]{:S(2)}) collective-permute-start(bf16[256,256]{1,0:T(8,128)(2,1)S(1)} %far_hidden.3.refs_0_), channel_id=1, source_target_pairs={{0,96},{32,0},{64,32},{96,64},{1,97},{33,1},{65,33},{97,65},{2,98}... | collective-permute-start | bytes 393224 | tf_op jit(solution)/shard_map/ppermute | solution.py:17
  162.9 1.1 collective-permute-start.23
  164.0 3.1 %collected.1.total_ref = bf16[320,1792]{1,0:T(8,128)(2,1)} custom-call(s32[320,1]{1,0:T(8,128)S(1)} %select_n.147.slot_ref, bf16[512,1792]{1,0:T(8,128)(2,1)} %bitcast.15.back_ref), custom_call_target="tpu_custom_call" | custom-call | flops 49999998976 | bytes 250000000 | tf_op jit(solution)/shard_map/collected/pallas_call | solution.py:201
  167.2 2.8 %collective-permute-done.23.refs_3_ = bf16[256,256]{1,0:T(8,128)(2,1)S(1)} collective-permute-done((bf16[256,256]{1,0:T(8,128)(2,1)S(1)}, bf16[256,256]{1,0:T(8,128)(2,1)S(1)}, u32[]{:S(2)}, u32[]{:S(2)}) %collective-permute-start.23) | collective-permute-done | bytes 131104 | tf_op jit(solution)/shard_map/ppermute | solution.py:17
  169.9 3.6 %projected.3 = bf16[256,1792]{1,0:T(8,128)(2,1)} custom-call(bf16[256,256]{1,0:T(8,128)(2,1)S(1)} %far_hidden.3.refs_0_, bf16[256,256]{1,0:T(8,128)(2,1)S(1)} %collective-permute-done.21.refs_1_, bf16[256,256]{1,0:T(8,128)(2,1)S(1)} %collective-permute-done.22.refs_2_, bf16[256,256]{1,0:T(8,128)(2,1)S(1)} %collective-permute-done.23.refs_3_, ...), custom_call_target="tpu_custom_call" | custom-call | tf_op jit(solution)/shard_map/projected/pallas_call | solution.py:156
  173.5 8.7 %all-to-all-start.3 = ((bf16[32,8,1792]{2,1,0:T(8,128)(2,1)}), bf16[32,8,1792]{2,1,0:T(8,128)(2,1)S(1)}, u32[]{:S(2)}, u32[]{:S(2)}) async-start(bf16[32,8,1792]{2,1,0:T(8,128)(2,1)} %bitcast.29), calls=%async_computation.3 | async-start | bytes 1835008 | tf_op jit(solution)/shard_map/all_to_all | solution.py:247
  182.2 4.4 %broadcast_select_fusion = bf16[1,256,7168]{2,1,0:T(8,128)(2,1)} fusion(bf16[1,256,7168]{2,1,0:T(8,128)(2,1)} %collective-permute-done.5, bf16[1,256,7168]{2,1,0:T(8,128)(2,1)} %param.13, pred[]{:T(512)S(6)} %ne.72), kind=kLoop, calls=%fused_computation | loop fusion | flops 1835008 | bytes 11010049 | tf_op jit(solution)/shard_map/jit(_where)/select_n | solution.py:348
  186.7 11.3 %all-to-all-done.3 = bf16[32,8,1792]{2,1,0:T(8,128)(2,1)S(1)} async-done(((bf16[32,8,1792]{2,1,0:T(8,128)(2,1)}), bf16[32,8,1792]{2,1,0:T(8,128)(2,1)S(1)}, u32[]{:S(2)}, u32[]{:S(2)}) %all-to-all-start.3) | async-done | bytes 917536 | tf_op jit(solution)/shard_map/all_to_all | solution.py:247
  198.0 1.8 mixed_rows.1
  (55 shorter events, 3.4 us)
Async XLA Ops:
  0.6 9.8 %copy-start = (bf16[320,1792]{1,0:T(8,128)(2,1)S(1)}, bf16[320,1792]{1,0:T(8,128)(2,1)}, u32[]{:S(2)}) copy-start(bf16[320,1792]{1,0:T(8,128)(2,1)} %param.7) | copy-start | bytes 3440644
  0.6 49.0 %collective-permute-start = (bf16[1,7168,256]{2,1,0:T(8,128)(2,1)}, bf16[1,7168,256]{2,1,0:T(8,128)(2,1)}, u32[]{:S(2)}, u32[]{:S(2)}) collective-permute-start(bf16[1,7168,256]{2,1,0:T(8,128)(2,1)} %gate_ref.1), channel_id=1, source_target_pairs={{0,1},{1,0},{2,3},{3,2},{4,5},{5,4},{6,7},{7,6},{8,9},{9,8},{10,11... | collective-permute-start | bytes 11010056 | tf_op jit(solution)/shard_map/ppermute | solution.py:21
  2.1 47.5 %collective-permute-start.1 = (bf16[1,7168,256]{2,1,0:T(8,128)(2,1)}, bf16[1,7168,256]{2,1,0:T(8,128)(2,1)}, u32[]{:S(2)}, u32[]{:S(2)}) collective-permute-start(bf16[1,7168,256]{2,1,0:T(8,128)(2,1)} %up_ref.1), channel_id=1, source_target_pairs={{0,1},{1,0},{2,3},{3,2},{4,5},{5,4},{6,7},{7,6},{8,9},{9,8},{10,11... | collective-permute-start | bytes 11010056 | tf_op jit(solution)/shard_map/ppermute | solution.py:21
  2.2 7.9 %copy-start.7 = (s32[320,8]{0,1:T(8,128)S(1)}, s32[320,8]{0,1:T(8,128)}, u32[]{:S(2)}) copy-start(s32[320,8]{0,1:T(8,128)} %param.8) | copy-start | bytes 30724
  5.9 23.0 %collective-permute-start.2 = (bf16[256,1792]{1,0:T(8,128)(2,1)}, bf16[256,1792]{1,0:T(8,128)(2,1)S(1)}, u32[]{:S(2)}, u32[]{:S(2)}) collective-permute-start(bf16[256,1792]{1,0:T(8,128)(2,1)} %get-tuple-element.96), channel_id=1, source_target_pairs={{0,32},{32,64},{64,96},{96,0},{1,33},{33,65},{65,97},{97,1},{2,34}... | collective-permute-start | bytes 2752520 | tf_op jit(solution)/shard_map/ppermute | solution.py:17
  7.2 21.8 %collective-permute-start.3 = (bf16[256,1792]{1,0:T(8,128)(2,1)}, bf16[256,1792]{1,0:T(8,128)(2,1)}, u32[]{:S(2)}, u32[]{:S(2)}) collective-permute-start(bf16[256,1792]{1,0:T(8,128)(2,1)} %get-tuple-element.95), channel_id=1, source_target_pairs={{0,96},{32,0},{64,32},{96,64},{1,97},{33,1},{65,33},{97,65},{2,98}... | collective-permute-start | bytes 2752520 | tf_op jit(solution)/shard_map/ppermute | solution.py:17
  8.5 41.1 %collective-permute-start.4 = (bf16[256,1792]{1,0:T(8,128)(2,1)}, bf16[256,1792]{1,0:T(8,128)(2,1)}, u32[]{:S(2)}, u32[]{:S(2)}) collective-permute-start(bf16[256,1792]{1,0:T(8,128)(2,1)} %get-tuple-element.94), channel_id=1, source_target_pairs={{0,64},{32,96},{64,0},{96,32},{1,65},{33,97},{65,1},{97,33},{2,66}... | collective-permute-start | bytes 2752520 | tf_op jit(solution)/shard_map/ppermute | solution.py:17
  12.7 36.9 %copy-start.8 = (f32[320,8]{0,1:T(8,128)S(1)}, f32[320,8]{0,1:T(8,128)}, u32[]{:S(2)}) copy-start(f32[320,8]{0,1:T(8,128)} %param.9) | copy-start | bytes 30724
  12.7 37.9 %all-to-all-start = ((bf16[32,16,1792]{2,1,0:T(8,128)(2,1)}), bf16[32,16,1792]{2,1,0:T(8,128)(2,1)}, u32[]{:S(2)}, u32[]{:S(2)}) async-start(bf16[32,16,1792]{2,1,0:T(8,128)(2,1)} %bitcast.31), calls=%async_computation | async-start | bytes 3670016 | tf_op jit(solution)/shard_map/all_to_all | solution.py:247
  28.9 21.1 %copy-start.3 = (bf16[256,1792]{1,0:T(8,128)(2,1)}, bf16[256,1792]{1,0:T(8,128)(2,1)S(1)}, u32[]{:S(2)}) copy-start(bf16[256,1792]{1,0:T(8,128)(2,1)S(1)} %collective-permute-done.2.refs_5_) | copy-start | bytes 2752516
  50.0 0.7 copy-start.5
  53.1 2.9 %copy-start.9 = (s32[32]{0:T(128)S(1)}, s32[32]{0:T(128)}, u32[]{:S(2)}) copy-start(s32[32]{0:T(128)} %param.10) | copy-start | bytes 388
  53.2 18.8 %collective-permute-start.6 = (bf16[192,1792]{1,0:T(8,128)(2,1)S(1)}, bf16[192,1792]{1,0:T(8,128)(2,1)}, u32[]{:S(2)}, u32[]{:S(2)}) collective-permute-start(bf16[192,1792]{1,0:T(8,128)(2,1)S(1)} %get-tuple-element.99.refs_0_), channel_id=1, source_target_pairs={{0,32},{32,64},{64,96},{96,0},{1,33},{33,65},{65,97},{97,1},{2,34}... | collective-permute-start | bytes 2064392 | tf_op jit(solution)/shard_map/ppermute | solution.py:17
  53.8 18.3 %collective-permute-start.8 = (bf16[192,1792]{1,0:T(8,128)(2,1)S(1)}, bf16[192,1792]{1,0:T(8,128)(2,1)}, u32[]{:S(2)}, u32[]{:S(2)}) collective-permute-start(bf16[192,1792]{1,0:T(8,128)(2,1)S(1)} %get-tuple-element.98.refs_1_), channel_id=1, source_target_pairs={{0,96},{32,0},{64,32},{96,64},{1,97},{33,1},{65,33},{97,65},{2,98}... | collective-permute-start | bytes 2064392 | tf_op jit(solution)/shard_map/ppermute | solution.py:17
  57.2 27.7 %collective-permute-start.10 = (bf16[192,1792]{1,0:T(8,128)(2,1)S(1)}, bf16[192,1792]{1,0:T(8,128)(2,1)}, u32[]{:S(2)}, u32[]{:S(2)}) collective-permute-start(bf16[192,1792]{1,0:T(8,128)(2,1)S(1)} %get-tuple-element.98.refs_1_), channel_id=1, source_target_pairs={{0,32},{32,64},{64,96},{96,0},{1,33},{33,65},{65,97},{97,1},{2,34}... | collective-permute-start | bytes 2064392 | tf_op jit(solution)/shard_map/ppermute | solution.py:17
  57.3 27.7 %collective-permute-start.11 = (bf16[192,1792]{1,0:T(8,128)(2,1)S(1)}, bf16[192,1792]{1,0:T(8,128)(2,1)}, u32[]{:S(2)}, u32[]{:S(2)}) collective-permute-start(bf16[192,1792]{1,0:T(8,128)(2,1)S(1)} %get-tuple-element.99.refs_0_), channel_id=1, source_target_pairs={{0,96},{32,0},{64,32},{96,64},{1,97},{33,1},{65,33},{97,65},{2,98}... | collective-permute-start | bytes 2064392 | tf_op jit(solution)/shard_map/ppermute | solution.py:17
  61.5 44.6 %all-to-all-start.1 = ((bf16[32,8,1792]{2,1,0:T(8,128)(2,1)}), bf16[32,8,1792]{2,1,0:T(8,128)(2,1)}, u32[]{:S(2)}, u32[]{:S(2)}) async-start(bf16[32,8,1792]{2,1,0:T(8,128)(2,1)} %fusion), calls=%async_computation.1 | async-start | bytes 1835008 | tf_op jit(solution)/shard_map/all_to_all | solution.py:247
  72.0 27.6 %collective-permute-start.7 = (bf16[192,1792]{1,0:T(8,128)(2,1)}, bf16[192,1792]{1,0:T(8,128)(2,1)S(1)}, u32[]{:S(2)}, u32[]{:S(2)}) collective-permute-start(bf16[192,1792]{1,0:T(8,128)(2,1)} %collective-permute-done.6.refs_2_), channel_id=1, source_target_pairs={{0,32},{32,64},{64,96},{96,0},{1,33},{33,65},{65,97},{97,1},{2,34}... | collective-permute-start | bytes 2064392 | tf_op jit(solution)/shard_map/ppermute | solution.py:17
  72.1 27.5 %collective-permute-start.9 = (bf16[192,1792]{1,0:T(8,128)(2,1)}, bf16[192,1792]{1,0:T(8,128)(2,1)S(1)}, u32[]{:S(2)}, u32[]{:S(2)}) collective-permute-start(bf16[192,1792]{1,0:T(8,128)(2,1)} %collective-permute-done.8.refs_5_), channel_id=1, source_target_pairs={{0,96},{32,0},{64,32},{96,64},{1,97},{33,1},{65,33},{97,65},{2,98}... | collective-permute-start | bytes 2064392 | tf_op jit(solution)/shard_map/ppermute | solution.py:17
  102.2 13.0 %copy-start.4 = (bf16[256,1792]{1,0:T(8,128)(2,1)S(1)}, bf16[256,1792]{1,0:T(8,128)(2,1)}, u32[]{:S(2)}) copy-start(bf16[256,1792]{1,0:T(8,128)(2,1)} %copy-done.3) | copy-start | bytes 2752516
  102.2 6.0 %collective-permute-start.12 = (bf16[384,256]{1,0:T(8,128)(2,1)S(1)}, bf16[384,256]{1,0:T(8,128)(2,1)S(1)}, u32[]{:S(2)}, u32[]{:S(2)}) collective-permute-start(bf16[384,256]{1,0:T(8,128)(2,1)S(1)} %far_hidden.2.refs_0_), channel_id=1, source_target_pairs={{0,32},{32,64},{64,96},{96,0},{1,33},{33,65},{65,97},{97,1},{2,34}... | collective-permute-start | bytes 589832 | tf_op jit(solution)/shard_map/ppermute | solution.py:17
  102.5 5.8 %collective-permute-start.13 = (bf16[384,256]{1,0:T(8,128)(2,1)S(1)}, bf16[384,256]{1,0:T(8,128)(2,1)S(1)}, u32[]{:S(2)}, u32[]{:S(2)}) collective-permute-start(bf16[384,256]{1,0:T(8,128)(2,1)S(1)} %far_hidden.2.refs_0_), channel_id=1, source_target_pairs={{0,96},{32,0},{64,32},{96,64},{1,97},{33,1},{65,33},{97,65},{2,98}... | collective-permute-start | bytes 589832 | tf_op jit(solution)/shard_map/ppermute | solution.py:17
  105.2 7.4 %collective-permute-start.14 = (bf16[384,256]{1,0:T(8,128)(2,1)S(1)}, bf16[384,256]{1,0:T(8,128)(2,1)}, u32[]{:S(2)}, u32[]{:S(2)}) collective-permute-start(bf16[384,256]{1,0:T(8,128)(2,1)S(1)} %far_hidden.2.refs_0_), channel_id=1, source_target_pairs={{0,64},{32,96},{64,0},{96,32},{1,65},{33,97},{65,1},{97,33},{2,66}... | collective-permute-start | bytes 589832 | tf_op jit(solution)/shard_map/ppermute | solution.py:17
  112.6 9.7 %collective-permute-start.15 = (bf16[128,1792]{1,0:T(8,128)(2,1)S(1)}, bf16[128,1792]{1,0:T(8,128)(2,1)}, u32[]{:S(2)}, u32[]{:S(2)}) collective-permute-start(bf16[128,1792]{1,0:T(8,128)(2,1)S(1)} %get-tuple-element.70.refs_0_), channel_id=1, source_target_pairs={{0,32},{32,64},{64,96},{96,0},{1,33},{33,65},{65,97},{97,1},{2,34}... | collective-permute-start | bytes 1376264 | tf_op jit(solution)/shard_map/ppermute | solution.py:17
  113.2 9.0 %collective-permute-start.16 = (bf16[128,1792]{1,0:T(8,128)(2,1)S(1)}, bf16[128,1792]{1,0:T(8,128)(2,1)}, u32[]{:S(2)}, u32[]{:S(2)}) collective-permute-start(bf16[128,1792]{1,0:T(8,128)(2,1)S(1)} %get-tuple-element.71.refs_1_), channel_id=1, source_target_pairs={{0,96},{32,0},{64,32},{96,64},{1,97},{33,1},{65,33},{97,65},{2,98}... | collective-permute-start | bytes 1376264 | tf_op jit(solution)/shard_map/ppermute | solution.py:17
  122.2 41.8 %all-to-all-start.2 = ((bf16[32,16,1792]{2,1,0:T(8,128)(2,1)}), bf16[32,16,1792]{2,1,0:T(8,128)(2,1)}, u32[]{:S(2)}, u32[]{:S(2)}) async-start(bf16[32,16,1792]{2,1,0:T(8,128)(2,1)} %bitcast.30), calls=%async_computation.2 | async-start | bytes 3670016 | tf_op jit(solution)/shard_map/all_to_all | solution.py:247
  135.0 13.2 %collective-permute-start.19 = (bf16[128,1792]{1,0:T(8,128)(2,1)S(1)}, bf16[128,1792]{1,0:T(8,128)(2,1)S(1)}, u32[]{:S(2)}, u32[]{:S(2)}) collective-permute-start(bf16[128,1792]{1,0:T(8,128)(2,1)S(1)} %get-tuple-element.71.refs_1_), channel_id=1, source_target_pairs={{0,32},{32,64},{64,96},{96,0},{1,33},{33,65},{65,97},{97,1},{2,34}... | collective-permute-start | bytes 1376264 | tf_op jit(solution)/shard_map/ppermute | solution.py:17
  135.5 12.6 %collective-permute-start.20 = (bf16[128,1792]{1,0:T(8,128)(2,1)S(1)}, bf16[128,1792]{1,0:T(8,128)(2,1)S(1)}, u32[]{:S(2)}, u32[]{:S(2)}) collective-permute-start(bf16[128,1792]{1,0:T(8,128)(2,1)S(1)} %get-tuple-element.70.refs_0_), channel_id=1, source_target_pairs={{0,96},{32,0},{64,32},{96,64},{1,97},{33,1},{65,33},{97,65},{2,98}... | collective-permute-start | bytes 1376264 | tf_op jit(solution)/shard_map/ppermute | solution.py:17
  137.8 20.1 %collective-permute-start.17 = (bf16[128,1792]{1,0:T(8,128)(2,1)}, bf16[128,1792]{1,0:T(8,128)(2,1)S(1)}, u32[]{:S(2)}, u32[]{:S(2)}) collective-permute-start(bf16[128,1792]{1,0:T(8,128)(2,1)} %collective-permute-done.15.refs_2_), channel_id=1, source_target_pairs={{0,32},{32,64},{64,96},{96,0},{1,33},{33,65},{65,97},{97,1},{2,34}... | collective-permute-start | bytes 1376264 | tf_op jit(solution)/shard_map/ppermute | solution.py:17
  137.8 20.1 %collective-permute-start.18 = (bf16[128,1792]{1,0:T(8,128)(2,1)}, bf16[128,1792]{1,0:T(8,128)(2,1)S(1)}, u32[]{:S(2)}, u32[]{:S(2)}) collective-permute-start(bf16[128,1792]{1,0:T(8,128)(2,1)} %collective-permute-done.16.refs_5_), channel_id=1, source_target_pairs={{0,96},{32,0},{64,32},{96,64},{1,97},{33,1},{65,33},{97,65},{2,98}... | collective-permute-start | bytes 1376264 | tf_op jit(solution)/shard_map/ppermute | solution.py:17
  140.7 32.8 %collective-permute-start.5 = (bf16[1,256,7168]{2,1,0:T(8,128)(2,1)}, bf16[1,256,7168]{2,1,0:T(8,128)(2,1)}, u32[]{:S(2)}, u32[]{:S(2)}) collective-permute-start(bf16[1,256,7168]{2,1,0:T(8,128)(2,1)} %param.13), channel_id=1, source_target_pairs={{0,1},{1,0},{2,3},{3,2},{4,5},{5,4},{6,7},{7,6},{8,9},{9,8},{10,11... | collective-permute-start | bytes 11010056 | tf_op jit(solution)/shard_map/ppermute | solution.py:21
  160.2 7.0 %collective-permute-start.21 = (bf16[256,256]{1,0:T(8,128)(2,1)S(1)}, bf16[256,256]{1,0:T(8,128)(2,1)S(1)}, u32[]{:S(2)}, u32[]{:S(2)}) collective-permute-start(bf16[256,256]{1,0:T(8,128)(2,1)S(1)} %far_hidden.3.refs_0_), channel_id=1, source_target_pairs={{0,32},{32,64},{64,96},{96,0},{1,33},{33,65},{65,97},{97,1},{2,34}... | collective-permute-start | bytes 393224 | tf_op jit(solution)/shard_map/ppermute | solution.py:17
  160.9 6.3 %collective-permute-start.22 = (bf16[256,256]{1,0:T(8,128)(2,1)S(1)}, bf16[256,256]{1,0:T(8,128)(2,1)S(1)}, u32[]{:S(2)}, u32[]{:S(2)}) collective-permute-start(bf16[256,256]{1,0:T(8,128)(2,1)S(1)} %far_hidden.3.refs_0_), channel_id=1, source_target_pairs={{0,96},{32,0},{64,32},{96,64},{1,97},{33,1},{65,33},{97,65},{2,98}... | collective-permute-start | bytes 393224 | tf_op jit(solution)/shard_map/ppermute | solution.py:17
  162.9 7.0 %collective-permute-start.23 = (bf16[256,256]{1,0:T(8,128)(2,1)S(1)}, bf16[256,256]{1,0:T(8,128)(2,1)S(1)}, u32[]{:S(2)}, u32[]{:S(2)}) collective-permute-start(bf16[256,256]{1,0:T(8,128)(2,1)S(1)} %far_hidden.3.refs_0_), channel_id=1, source_target_pairs={{0,64},{32,96},{64,0},{96,32},{1,65},{33,97},{65,1},{97,33},{2,66}... | collective-permute-start | bytes 393224 | tf_op jit(solution)/shard_map/ppermute | solution.py:17
  173.5 24.5 %all-to-all-start.3 = ((bf16[32,8,1792]{2,1,0:T(8,128)(2,1)}), bf16[32,8,1792]{2,1,0:T(8,128)(2,1)S(1)}, u32[]{:S(2)}, u32[]{:S(2)}) async-start(bf16[32,8,1792]{2,1,0:T(8,128)(2,1)} %bitcast.29), calls=%async_computation.3 | async-start | bytes 1835008 | tf_op jit(solution)/shard_map/all_to_all | solution.py:247
  182.2 15.8 %copy-start.2 = (bf16[320,1792]{1,0:T(8,128)(2,1)S(1)}, bf16[320,1792]{1,0:T(8,128)(2,1)}, u32[]{:S(2)}) copy-start(bf16[320,1792]{1,0:T(8,128)(2,1)} %collected.1.total_ref) | copy-start | bytes 3440644
  182.2 15.8 %copy-start.6 = (f32[320,1]{1,0:T(8,128)S(1)}, f32[320,1]{1,0:T(8,128)}, u32[]{:S(2)}) copy-start(f32[320,1]{1,0:T(8,128)} %copy-done.5) | copy-start | bytes 3844
  182.2 17.6 %copy-start.1 = (bf16[320,1792]{1,0:T(8,128)(2,1)S(1)}, bf16[320,1792]{1,0:T(8,128)(2,1)}, u32[]{:S(2)}) copy-start(bf16[320,1792]{1,0:T(8,128)(2,1)} %param.7) | copy-start | bytes 3440644

commit v5 on v4

--- a/solution.py
+++ b/solution.py
@@ -331,21 +331,20 @@
     def project(chunk, hidden, cost):
         return projected(hidden, down, chunk[1], chunk[2], cost)
 
-    placed = [jnp.where(moved, o, w) for o, w in zip(swaps, own)]
+    placed = [jnp.where(moved, o, w) for o, w in zip(swaps[:2], own)]
+    last = [jnp.where(moved, swapped(own[2]), own[2])]
     halves_a = split(live_rows(CHUNKS[0], got_a))
     hidden_a = activations(halves_a, first_step(halves_a), placed)
     halves_b = split(live_rows(CHUNKS[1], got_b))
     halves_b, hidden_a = tied(halves_b, hidden_a)
     near = first_step(halves_b)
     out_a = project(CHUNKS[0], hidden_a, LONG)
-    near, out_a = tied(near, out_a)
+    near, _ = tied(near, out_a)
     back_a = exchanged(out_a)
-    hidden_b = activations(halves_b, near, [])
-    other = swapped(own[2])
+    hidden_b = activations(halves_b, near, last)
     total, hidden_b = tied(collected(slot_a[:, None], back_a), hidden_b)
     out_b = project(CHUNKS[1], hidden_b, FREE)
-    other, out_b, last = tied(other, out_b, own[2])
-    placed.append(jnp.where(moved, other, last))
+    placed += last
     back_b = exchanged(out_b)
     mixed = mixed_rows(slot_b[:, None], back_b, total, gate_weight)
     return (mixed, *placed)

time: 201 us -> 194 us (0.965)
  starting transfers between devices: 72.8 us -> 66.9 us
  waiting for transfers between devices: 70.6 us -> 65.7 us
  local copies, waits for them, and re-layouts: 6.65 us -> 10.6 us
    ppermute x21, waiting for transfers between devices: 59.2 us -> 43.5 us  [shifted(): lax.ppermute(value, 'dp', [(i, (i + step) % size) for i in range(size)])]
    all_to_all x4, waiting for transfers between devices: 11.3 us -> 22.2 us  [exchanged(): lax.all_to_all(blocks, 'expert', split_axis=0, concat_axis=0, tiled=True)]
    all_to_all x4, starting transfers between devices: 41.5 us -> 36.7 us  [exchanged(): lax.all_to_all(blocks, 'expert', split_axis=0, concat_axis=0, tiled=True)]
    unnamed x21 -> x31, local copies, waits for them, and re-layouts: 0.83 us -> 4.06 us
    ppermute x21, starting transfers between devices: 28.3 us -> 26.2 us  [shifted(): lax.ppermute(value, 'dp', [(i, (i + step) % size) for i in range(size)])]
  transfers between devices with their start and end apart: 28 -> 28, of which waited for: 11 -> 10; matrix products, arithmetic and copies ran while one was open for 11% -> 11% of each run, Pallas kernels for 14% -> 13%
where the time goes in v5:
time: 194 us; the launch traced here: 193 us
  starting transfers between devices  66.9 us (34%)
  waiting for transfers between devices  65.7 us (34%)
  Pallas kernels  30.5 us (16%)
  other arithmetic  11.3 us (6%)
  local copies, waits for them, and re-layouts  10.6 us (5%)
  matrix products  6.51 us (3%)
    ppermute x21, waiting for transfers between devices, shifted(): lax.ppermute(value, 'dp', [(i, (i + step) % size) for i in range(size)])  43.5 us
    all_to_all x4, starting transfers between devices, exchanged(): lax.all_to_all(blocks, 'expert', split_axis=0, concat_axis=0, tiled=True)  36.7 us
    ppermute x21, starting transfers between devices, shifted(): lax.ppermute(value, 'dp', [(i, (i + step) % size) for i in range(size)])  26.2 us
    all_to_all x4, waiting for transfers between devices, exchanged(): lax.all_to_all(blocks, 'expert', split_axis=0, concat_axis=0, tiled=True)  22.2 us
    pallas_call x2, Pallas kernels, near_sums(): pl.pallas_call(kernel, out_shape=jax.ShapeDtypeStruct((count, 2 * units),...  11.4 us
    pallas_call x2, Pallas kernels, projected(): pl.pallas_call(kernel, out_shape=pltpu.HBM((slots, width), jnp.bfloat16),...  9.13 us
    select_n x1, other arithmetic, body(): placed = [jnp.where(moved, o, w) for o, w in zip(swaps[:2], own)]  6.91 us
    dot_general x4, matrix products, dot32(): return jnp.dot(left, right, preferred_element_type=jnp.float32)  6.51 us
  transfers between devices with their start and end apart: 28, of which 10 were waited for; matrix products, arithmetic and copies ran while one was open for 11% of the time, Pallas kernels for 13%

profile of v5, /device:TPU:1, one launch (start us, length us, event | category | flops | bytes accessed | tf_op | source)
XLA Modules:
  0.0 193.0 jit_solution(1465005983194253171)
XLA Ops:
  0.6 1.5 collective-permute-start
  2.2 3.6 %dynamic-slice_bitcast_fusion = (bf16[256,1792]{1,0:T(8,128)(2,1)}, bf16[256,1792]{1,0:T(8,128)(2,1)}, bf16[256,1792]{1,0:T(8,128)(2,1)}, bf16[256,1792]{1,0:T(8,128)(2,1)S(1)}) fusion(bf16[1,256,7168]{2,1,0:T(8,128)(2,1)} %param.13, s32[]{:T(128)S(6)} %select_n.137, s32[]{:T(128)S(6)} %select_n.135, s32[]{:T(128)S(6)} %select_n.133, s32[]{:T(128)S(6)} %select_n.131), kind=kLoop, calls=%fused_computation.9 | loop fusion | bytes 7340048 | tf_op jit(solution)/shard_map/dynamic_slice | solution.py:289
  5.9 1.3 collective-permute-start.2
  7.2 1.4 collective-permute-start.3
  8.5 1.6 collective-permute-start.4
  10.4 2.3 %convolution_convert_fusion = bf16[512,1792]{1,0:T(8,128)(2,1)} fusion(bf16[320,1792]{1,0:T(8,128)(2,1)S(1)} %copy-done, s32[320]{0:T(512)S(1)} %get-tuple-element.104), kind=kOutput, calls=%fused_computation.3 | convolution fusion | flops 588283904 | bytes 2983168 | tf_op jit(solution)/shard_map/dot_general | solution.py:25
  12.7 9.5 %all-to-all-start = ((bf16[32,16,1792]{2,1,0:T(8,128)(2,1)}), bf16[32,16,1792]{2,1,0:T(8,128)(2,1)}, u32[]{:S(2)}, u32[]{:S(2)}) async-start(bf16[32,16,1792]{2,1,0:T(8,128)(2,1)} %bitcast.31), calls=%async_computation | async-start | bytes 3670016 | tf_op jit(solution)/shard_map/all_to_all | solution.py:247
  22.4 6.5 %collective-permute-done.2.refs_5_ = bf16[256,1792]{1,0:T(8,128)(2,1)S(1)} collective-permute-done((bf16[256,1792]{1,0:T(8,128)(2,1)}, bf16[256,1792]{1,0:T(8,128)(2,1)S(1)}, u32[]{:S(2)}, u32[]{:S(2)}) %collective-permute-start.2) | collective-permute-done | bytes 917536 | tf_op jit(solution)/shard_map/ppermute | solution.py:17
  28.9 20.7 %collective-permute-done.4.refs_7_ = bf16[256,1792]{1,0:T(8,128)(2,1)} collective-permute-done((bf16[256,1792]{1,0:T(8,128)(2,1)}, bf16[256,1792]{1,0:T(8,128)(2,1)}, u32[]{:S(2)}, u32[]{:S(2)}) %collective-permute-start.4) | collective-permute-done | bytes 917536 | tf_op jit(solution)/shard_map/ppermute | solution.py:17
  50.0 0.7 copy-done.5
  50.6 2.4 %convolution_convert_fusion.1 = bf16[384,1792]{1,0:T(8,128)(2,1)S(1)} fusion(bf16[512,1792]{1,0:T(8,128)(2,1)} %bitcast.1, s32[384]{0:T(512)S(1)} %fusion.12), kind=kOutput, calls=%fused_computation.4 | convolution fusion | flops 705527808 | bytes 3212800 | tf_op jit(solution)/shard_map/dot_general | solution.py:25
  53.8 2.1 %collective-permute-start.7 = (bf16[192,1792]{1,0:T(8,128)(2,1)S(1)}, bf16[192,1792]{1,0:T(8,128)(2,1)}, u32[]{:S(2)}, u32[]{:S(2)}) collective-permute-start(bf16[192,1792]{1,0:T(8,128)(2,1)S(1)} %get-tuple-element.100.refs_1_), channel_id=1, source_target_pairs={{0,96},{32,0},{64,32},{96,64},{1,97},{33,1},{65,33},{97,65},{2,98}... | collective-permute-start | bytes 2064392 | tf_op jit(solution)/shard_map/ppermute | solution.py:17
  55.9 0.8 select_n.147.slot_ref
  58.1 1.5 collective-permute-start.9
  59.5 2.4 %collective-permute-start.20 = (bf16[1,256,7168]{2,1,0:T(8,128)(2,1)}, bf16[1,256,7168]{2,1,0:T(8,128)(2,1)}, u32[]{:S(2)}, u32[]{:S(2)}) collective-permute-start(bf16[1,256,7168]{2,1,0:T(8,128)(2,1)} %param.13), channel_id=1, source_target_pairs={{0,1},{1,0},{2,3},{3,2},{4,5},{5,4},{6,7},{7,6},{8,9},{9,8},{10,11... | collective-permute-start | bytes 11010056 | tf_op jit(solution)/shard_map/ppermute | solution.py:21
  61.9 1.5 fusion
  63.4 8.3 %all-to-all-start.1 = ((bf16[32,8,1792]{2,1,0:T(8,128)(2,1)}), bf16[32,8,1792]{2,1,0:T(8,128)(2,1)}, u32[]{:S(2)}, u32[]{:S(2)}) async-start(bf16[32,8,1792]{2,1,0:T(8,128)(2,1)} %fusion), calls=%async_computation.1 | async-start | bytes 1835008 | tf_op jit(solution)/shard_map/all_to_all | solution.py:247
  71.8 2.7 %collective-permute-start.8 = (bf16[192,1792]{1,0:T(8,128)(2,1)}, bf16[192,1792]{1,0:T(8,128)(2,1)S(1)}, u32[]{:S(2)}, u32[]{:S(2)}) collective-permute-start(bf16[192,1792]{1,0:T(8,128)(2,1)} %collective-permute-done.7.refs_5_), channel_id=1, source_target_pairs={{0,96},{32,0},{64,32},{96,64},{1,97},{33,1},{65,33},{97,65},{2,98}... | collective-permute-start | bytes 2064392 | tf_op jit(solution)/shard_map/ppermute | solution.py:17
  74.5 6.9 %broadcast_select_fusion.1 = (bf16[1,7168,256]{2,1,0:T(8,128)(2,1)}, bf16[1,7168,256]{2,1,0:T(8,128)(2,1)}) fusion(bf16[1,7168,256]{2,1,0:T(8,128)(2,1)} %collective-permute-done.1, bf16[1,7168,256]{2,1,0:T(8,128)(2,1)} %up_ref.1, pred[]{:T(512)S(6)} %ne.72, bf16[1,7168,256]{2,1,0:T(8,128)(2,1)} %collective-permute-done, bf16[1,7168,256]{2,1,0:T(8,128)(2,1)} %gate_ref.1), kind=kLoop, calls=%fused_computation.1 | loop fusion | flops 3670016 | bytes 22020096 | tf_op jit(solution)/shard_map/jit(_where)/select_n | solution.py:334
  81.4 2.5 %collective-permute-done.10.refs_4_ = bf16[192,1792]{1,0:T(8,128)(2,1)} collective-permute-done((bf16[192,1792]{1,0:T(8,128)(2,1)S(1)}, bf16[192,1792]{1,0:T(8,128)(2,1)}, u32[]{:S(2)}, u32[]{:S(2)}) %collective-permute-start.10) | collective-permute-done | bytes 688160 | tf_op jit(solution)/shard_map/ppermute | solution.py:17
  83.9 1.1 collective-permute-done.9.refs_3_
  85.0 6.1 %near_sums.2.sum_ref = f32[384,512]{1,0:T(8,128)S(1)} custom-call(s32[3]{0:T(128)S(1)} %pad_add_fusion.spot_ref, bf16[192,1792]{1,0:T(8,128)(2,1)S(1)} %get-tuple-element.101.refs_0_, bf16[192,1792]{1,0:T(8,128)(2,1)S(1)} %get-tuple-element.100.refs_1_, bf16[192,1792]{1,0:T(8,128)(2,1)} %collective-permute-done.5.refs_2_, ...), custom_call_target="tpu_custom_call" | custom-call | tf_op jit(solution)/shard_map/near_sums/pallas_call | solution.py:69
  91.1 8.5 %collective-permute-done.6.first_ref = bf16[192,1792]{1,0:T(8,128)(2,1)S(1)} collective-permute-done((bf16[192,1792]{1,0:T(8,128)(2,1)}, bf16[192,1792]{1,0:T(8,128)(2,1)S(1)}, u32[]{:S(2)}, u32[]{:S(2)}) %collective-permute-start.6) | collective-permute-done | bytes 688160 | tf_op jit(solution)/shard_map/ppermute | solution.py:17
  99.6 2.6 %far_hidden.2.refs_0_ = bf16[384,256]{1,0:T(8,128)(2,1)S(1)} custom-call(s32[1]{0:T(128)} %bitcast.9.spot_ref, bf16[192,1792]{1,0:T(8,128)(2,1)S(1)} %collective-permute-done.6.first_ref, bf16[192,1792]{1,0:T(8,128)(2,1)S(1)} %collective-permute-done.8.second_ref, f32[384,512]{1,0:T(8,128)S(1)} %near_sums.2.sum_ref, bf16[1,7168,256]{2,1,0:T(8,128)(2,1)} %gate_ref.1, ...), custom_call_target="tpu_custom_call" | custom-call | tf_op jit(solution)/shard_map/far_hidden/pallas_call | solution.py:110
  102.3 2.7 %collective-permute-start.12 = (bf16[384,256]{1,0:T(8,128)(2,1)S(1)}, bf16[384,256]{1,0:T(8,128)(2,1)S(1)}, u32[]{:S(2)}, u32[]{:S(2)}) collective-permute-start(bf16[384,256]{1,0:T(8,128)(2,1)S(1)} %far_hidden.2.refs_0_), channel_id=1, source_target_pairs={{0,96},{32,0},{64,32},{96,64},{1,97},{33,1},{65,33},{97,65},{2,98}... | collective-permute-start | bytes 589832 | tf_op jit(solution)/shard_map/ppermute | solution.py:17
  105.0 0.9 collective-permute-start.13
  105.9 1.2 slice_bitcast_fusion
  107.1 0.9 collective-permute-done.11.refs_1_
  108.7 0.7 copy-done.10
  109.4 3.0 %collective-permute-done.13.refs_3_ = bf16[384,256]{1,0:T(8,128)(2,1)} collective-permute-done((bf16[384,256]{1,0:T(8,128)(2,1)S(1)}, bf16[384,256]{1,0:T(8,128)(2,1)}, u32[]{:S(2)}, u32[]{:S(2)}) %collective-permute-start.13) | collective-permute-done | bytes 196640 | tf_op jit(solution)/shard_map/ppermute | solution.py:17
  112.4 2.3 %collective-permute-start.15 = (bf16[128,1792]{1,0:T(8,128)(2,1)S(1)}, bf16[128,1792]{1,0:T(8,128)(2,1)S(1)}, u32[]{:S(2)}, u32[]{:S(2)}) collective-permute-start(bf16[128,1792]{1,0:T(8,128)(2,1)S(1)} %get-tuple-element.79.refs_1_), channel_id=1, source_target_pairs={{0,96},{32,0},{64,32},{96,64},{1,97},{33,1},{65,33},{97,65},{2,98}... | collective-permute-start | bytes 1376264 | tf_op jit(solution)/shard_map/ppermute | solution.py:17
  114.7 2.7 %collective-permute-start.19 = (bf16[128,1792]{1,0:T(8,128)(2,1)S(1)}, bf16[128,1792]{1,0:T(8,128)(2,1)}, u32[]{:S(2)}, u32[]{:S(2)}) collective-permute-start(bf16[128,1792]{1,0:T(8,128)(2,1)S(1)} %get-tuple-element.78.refs_0_), channel_id=1, source_target_pairs={{0,96},{32,0},{64,32},{96,64},{1,97},{33,1},{65,33},{97,65},{2,98}... | collective-permute-start | bytes 1376264 | tf_op jit(solution)/shard_map/ppermute | solution.py:17
  117.4 0.9 copy-done.9
  118.4 0.9 copy-done.11
  119.3 5.5 %projected.2 = bf16[512,1792]{1,0:T(8,128)(2,1)} custom-call(bf16[384,256]{1,0:T(8,128)(2,1)S(1)} %far_hidden.2.refs_0_, bf16[384,256]{1,0:T(8,128)(2,1)S(1)} %copy-done.9, bf16[384,256]{1,0:T(8,128)(2,1)S(1)} %copy-done.11, bf16[384,256]{1,0:T(8,128)(2,1)} %collective-permute-done.13.refs_3_, bf16[256,1792]{1,0:T(8,128)(2,1)S(1)} %get-tuple-element.74.refs_4_, ...), custom_call_target="tpu_custom_call" | custom-call | flops 49999998976 | bytes 250000000 | tf_op jit(solution)/shard_map/projected/pallas_call | solution.py:156
  124.8 12.8 %all-to-all-start.2 = ((bf16[32,16,1792]{2,1,0:T(8,128)(2,1)}), bf16[32,16,1792]{2,1,0:T(8,128)(2,1)}, u32[]{:S(2)}, u32[]{:S(2)}) async-start(bf16[32,16,1792]{2,1,0:T(8,128)(2,1)} %bitcast.30), calls=%async_computation.2 | async-start | bytes 3670016 | tf_op jit(solution)/shard_map/all_to_all | solution.py:247
  137.7 2.7 %collective-permute-start.17 = (bf16[128,1792]{1,0:T(8,128)(2,1)S(1)}, bf16[128,1792]{1,0:T(8,128)(2,1)S(1)}, u32[]{:S(2)}, u32[]{:S(2)}) collective-permute-start(bf16[128,1792]{1,0:T(8,128)(2,1)S(1)} %collective-permute-done.15.refs_5_), channel_id=1, source_target_pairs={{0,96},{32,0},{64,32},{96,64},{1,97},{33,1},{65,33},{97,65},{2,98}... | collective-permute-start | bytes 1376264 | tf_op jit(solution)/shard_map/ppermute | solution.py:17
  140.4 4.3 %broadcast_select_fusion = bf16[1,256,7168]{2,1,0:T(8,128)(2,1)} fusion(bf16[1,256,7168]{2,1,0:T(8,128)(2,1)} %collective-permute-done.20, bf16[1,256,7168]{2,1,0:T(8,128)(2,1)} %param.13, pred[]{:T(512)S(6)} %ne.72), kind=kLoop, calls=%fused_computation | loop fusion | flops 1835008 | bytes 11010049 | tf_op jit(solution)/shard_map/jit(_where)/select_n | solution.py:335
  144.6 5.2 %near_sums.3.sum_ref = f32[256,512]{1,0:T(8,128)S(1)} custom-call(s32[3]{0:T(128)S(1)} %pad_add_fusion.spot_ref, bf16[128,1792]{1,0:T(8,128)(2,1)S(1)} %get-tuple-element.78.refs_0_, bf16[128,1792]{1,0:T(8,128)(2,1)S(1)} %get-tuple-element.79.refs_1_, bf16[128,1792]{1,0:T(8,128)(2,1)} %collective-permute-done.14.refs_2_, ...), custom_call_target="tpu_custom_call" | custom-call | tf_op jit(solution)/shard_map/near_sums/pallas_call | solution.py:69
  150.1 2.3 %far_hidden.3.refs_0_ = bf16[256,256]{1,0:T(8,128)(2,1)S(1)} custom-call(s32[1]{0:T(128)} %bitcast.9.spot_ref, bf16[128,1792]{1,0:T(8,128)(2,1)S(1)} %collective-permute-done.16.first_ref, bf16[128,1792]{1,0:T(8,128)(2,1)S(1)} %collective-permute-done.17.second_ref, f32[256,512]{1,0:T(8,128)S(1)} %near_sums.3.sum_ref, bf16[1,7168,256]{2,1,0:T(8,128)(2,1)} %gate_ref.1, ...), custom_call_target="tpu_custom_call" | custom-call | tf_op jit(solution)/shard_map/far_hidden/pallas_call | solution.py:110
  153.1 2.1 %collective-permute-start.22 = (bf16[256,256]{1,0:T(8,128)(2,1)S(1)}, bf16[256,256]{1,0:T(8,128)(2,1)S(1)}, u32[]{:S(2)}, u32[]{:S(2)}) collective-permute-start(bf16[256,256]{1,0:T(8,128)(2,1)S(1)} %far_hidden.3.refs_0_), channel_id=1, source_target_pairs={{0,96},{32,0},{64,32},{96,64},{1,97},{33,1},{65,33},{97,65},{2,98}... | collective-permute-start | bytes 393224 | tf_op jit(solution)/shard_map/ppermute | solution.py:17
  155.2 0.8 collective-permute-start.23
  156.0 6.6 %all-to-all-done.2 = bf16[32,16,1792]{2,1,0:T(8,128)(2,1)} async-done(((bf16[32,16,1792]{2,1,0:T(8,128)(2,1)}), bf16[32,16,1792]{2,1,0:T(8,128)(2,1)}, u32[]{:S(2)}, u32[]{:S(2)}) %all-to-all-start.2) | async-done | bytes 1835040 | tf_op jit(solution)/shard_map/all_to_all | solution.py:247
  162.6 3.1 %collected.1.total_ref = bf16[320,1792]{1,0:T(8,128)(2,1)} custom-call(s32[320,1]{1,0:T(8,128)S(1)} %copy-done.7, bf16[512,1792]{1,0:T(8,128)(2,1)} %bitcast.15.back_ref), custom_call_target="tpu_custom_call" | custom-call | flops 49999998976 | bytes 250000000 | tf_op jit(solution)/shard_map/collected/pallas_call | solution.py:201
  165.7 3.6 %projected.3 = bf16[256,1792]{1,0:T(8,128)(2,1)} custom-call(bf16[256,256]{1,0:T(8,128)(2,1)S(1)} %far_hidden.3.refs_0_, bf16[256,256]{1,0:T(8,128)(2,1)S(1)} %collective-permute-done.21.refs_1_, bf16[256,256]{1,0:T(8,128)(2,1)S(1)} %collective-permute-done.22.refs_2_, bf16[256,256]{1,0:T(8,128)(2,1)S(1)} %collective-permute-done.23.refs_3_, ...), custom_call_target="tpu_custom_call" | custom-call | tf_op jit(solution)/shard_map/projected/pallas_call | solution.py:156
  169.3 6.1 %all-to-all-start.3 = ((bf16[32,8,1792]{2,1,0:T(8,128)(2,1)}), bf16[32,8,1792]{2,1,0:T(8,128)(2,1)S(1)}, u32[]{:S(2)}, u32[]{:S(2)}) async-start(bf16[32,8,1792]{2,1,0:T(8,128)(2,1)} %bitcast.29), calls=%async_computation.3 | async-start | bytes 1835008 | tf_op jit(solution)/shard_map/all_to_all | solution.py:247
  175.6 15.6 %all-to-all-done.3 = bf16[32,8,1792]{2,1,0:T(8,128)(2,1)S(1)} async-done(((bf16[32,8,1792]{2,1,0:T(8,128)(2,1)}), bf16[32,8,1792]{2,1,0:T(8,128)(2,1)S(1)}, u32[]{:S(2)}, u32[]{:S(2)}) %all-to-all-start.3) | async-done | bytes 917536 | tf_op jit(solution)/shard_map/all_to_all | solution.py:247
  191.2 1.8 mixed_rows.1
  (65 shorter events, 4.1 us)
Async XLA Ops:
  0.6 9.8 %copy-start = (bf16[320,1792]{1,0:T(8,128)(2,1)S(1)}, bf16[320,1792]{1,0:T(8,128)(2,1)}, u32[]{:S(2)}) copy-start(bf16[320,1792]{1,0:T(8,128)(2,1)} %param.7) | copy-start | bytes 3440644
  0.6 49.0 %collective-permute-start = (bf16[1,7168,256]{2,1,0:T(8,128)(2,1)}, bf16[1,7168,256]{2,1,0:T(8,128)(2,1)}, u32[]{:S(2)}, u32[]{:S(2)}) collective-permute-start(bf16[1,7168,256]{2,1,0:T(8,128)(2,1)} %gate_ref.1), channel_id=1, source_target_pairs={{0,1},{1,0},{2,3},{3,2},{4,5},{5,4},{6,7},{7,6},{8,9},{9,8},{10,11... | collective-permute-start | bytes 11010056 | tf_op jit(solution)/shard_map/ppermute | solution.py:21
  2.1 47.5 %collective-permute-start.1 = (bf16[1,7168,256]{2,1,0:T(8,128)(2,1)}, bf16[1,7168,256]{2,1,0:T(8,128)(2,1)}, u32[]{:S(2)}, u32[]{:S(2)}) collective-permute-start(bf16[1,7168,256]{2,1,0:T(8,128)(2,1)} %up_ref.1), channel_id=1, source_target_pairs={{0,1},{1,0},{2,3},{3,2},{4,5},{5,4},{6,7},{7,6},{8,9},{9,8},{10,11... | collective-permute-start | bytes 11010056 | tf_op jit(solution)/shard_map/ppermute | solution.py:21
  2.2 7.9 %copy-start.12 = (s32[320,8]{0,1:T(8,128)S(1)}, s32[320,8]{0,1:T(8,128)}, u32[]{:S(2)}) copy-start(s32[320,8]{0,1:T(8,128)} %param.8) | copy-start | bytes 30724
  5.9 23.0 %collective-permute-start.2 = (bf16[256,1792]{1,0:T(8,128)(2,1)}, bf16[256,1792]{1,0:T(8,128)(2,1)S(1)}, u32[]{:S(2)}, u32[]{:S(2)}) collective-permute-start(bf16[256,1792]{1,0:T(8,128)(2,1)} %get-tuple-element.98), channel_id=1, source_target_pairs={{0,32},{32,64},{64,96},{96,0},{1,33},{33,65},{65,97},{97,1},{2,34}... | collective-permute-start | bytes 2752520 | tf_op jit(solution)/shard_map/ppermute | solution.py:17
  7.2 21.8 %collective-permute-start.3 = (bf16[256,1792]{1,0:T(8,128)(2,1)}, bf16[256,1792]{1,0:T(8,128)(2,1)}, u32[]{:S(2)}, u32[]{:S(2)}) collective-permute-start(bf16[256,1792]{1,0:T(8,128)(2,1)} %get-tuple-element.97), channel_id=1, source_target_pairs={{0,96},{32,0},{64,32},{96,64},{1,97},{33,1},{65,33},{97,65},{2,98}... | collective-permute-start | bytes 2752520 | tf_op jit(solution)/shard_map/ppermute | solution.py:17
  8.5 41.1 %collective-permute-start.4 = (bf16[256,1792]{1,0:T(8,128)(2,1)}, bf16[256,1792]{1,0:T(8,128)(2,1)}, u32[]{:S(2)}, u32[]{:S(2)}) collective-permute-start(bf16[256,1792]{1,0:T(8,128)(2,1)} %get-tuple-element.96), channel_id=1, source_target_pairs={{0,64},{32,96},{64,0},{96,32},{1,65},{33,97},{65,1},{97,33},{2,66}... | collective-permute-start | bytes 2752520 | tf_op jit(solution)/shard_map/ppermute | solution.py:17
  12.7 36.9 %copy-start.13 = (f32[320,8]{0,1:T(8,128)S(1)}, f32[320,8]{0,1:T(8,128)}, u32[]{:S(2)}) copy-start(f32[320,8]{0,1:T(8,128)} %param.9) | copy-start | bytes 30724
  12.7 37.9 %all-to-all-start = ((bf16[32,16,1792]{2,1,0:T(8,128)(2,1)}), bf16[32,16,1792]{2,1,0:T(8,128)(2,1)}, u32[]{:S(2)}, u32[]{:S(2)}) async-start(bf16[32,16,1792]{2,1,0:T(8,128)(2,1)} %bitcast.31), calls=%async_computation | async-start | bytes 3670016 | tf_op jit(solution)/shard_map/all_to_all | solution.py:247
  28.9 21.1 %copy-start.3 = (bf16[256,1792]{1,0:T(8,128)(2,1)}, bf16[256,1792]{1,0:T(8,128)(2,1)S(1)}, u32[]{:S(2)}) copy-start(bf16[256,1792]{1,0:T(8,128)(2,1)S(1)} %collective-permute-done.2.refs_5_) | copy-start | bytes 2752516
  50.0 0.7 copy-start.5
  53.1 3.6 %copy-start.14 = (s32[32]{0:T(128)S(1)}, s32[32]{0:T(128)}, u32[]{:S(2)}) copy-start(s32[32]{0:T(128)} %param.10) | copy-start | bytes 388
  53.2 18.5 %collective-permute-start.5 = (bf16[192,1792]{1,0:T(8,128)(2,1)S(1)}, bf16[192,1792]{1,0:T(8,128)(2,1)}, u32[]{:S(2)}, u32[]{:S(2)}) collective-permute-start(bf16[192,1792]{1,0:T(8,128)(2,1)S(1)} %get-tuple-element.101.refs_0_), channel_id=1, source_target_pairs={{0,32},{32,64},{64,96},{96,0},{1,33},{33,65},{65,97},{97,1},{2,34}... | collective-permute-start | bytes 2064392 | tf_op jit(solution)/shard_map/ppermute | solution.py:17
  53.8 18.0 %collective-permute-start.7 = (bf16[192,1792]{1,0:T(8,128)(2,1)S(1)}, bf16[192,1792]{1,0:T(8,128)(2,1)}, u32[]{:S(2)}, u32[]{:S(2)}) collective-permute-start(bf16[192,1792]{1,0:T(8,128)(2,1)S(1)} %get-tuple-element.100.refs_1_), channel_id=1, source_target_pairs={{0,96},{32,0},{64,32},{96,64},{1,97},{33,1},{65,33},{97,65},{2,98}... | collective-permute-start | bytes 2064392 | tf_op jit(solution)/shard_map/ppermute | solution.py:17
  58.0 25.8 %collective-permute-start.10 = (bf16[192,1792]{1,0:T(8,128)(2,1)S(1)}, bf16[192,1792]{1,0:T(8,128)(2,1)}, u32[]{:S(2)}, u32[]{:S(2)}) collective-permute-start(bf16[192,1792]{1,0:T(8,128)(2,1)S(1)} %get-tuple-element.101.refs_0_), channel_id=1, source_target_pairs={{0,96},{32,0},{64,32},{96,64},{1,97},{33,1},{65,33},{97,65},{2,98}... | collective-permute-start | bytes 2064392 | tf_op jit(solution)/shard_map/ppermute | solution.py:17
  58.1 26.9 %collective-permute-start.9 = (bf16[192,1792]{1,0:T(8,128)(2,1)S(1)}, bf16[192,1792]{1,0:T(8,128)(2,1)}, u32[]{:S(2)}, u32[]{:S(2)}) collective-permute-start(bf16[192,1792]{1,0:T(8,128)(2,1)S(1)} %get-tuple-element.100.refs_1_), channel_id=1, source_target_pairs={{0,32},{32,64},{64,96},{96,0},{1,33},{33,65},{65,97},{97,1},{2,34}... | collective-permute-start | bytes 2064392 | tf_op jit(solution)/shard_map/ppermute | solution.py:17
  59.5 80.9 %collective-permute-start.20 = (bf16[1,256,7168]{2,1,0:T(8,128)(2,1)}, bf16[1,256,7168]{2,1,0:T(8,128)(2,1)}, u32[]{:S(2)}, u32[]{:S(2)}) collective-permute-start(bf16[1,256,7168]{2,1,0:T(8,128)(2,1)} %param.13), channel_id=1, source_target_pairs={{0,1},{1,0},{2,3},{3,2},{4,5},{5,4},{6,7},{7,6},{8,9},{9,8},{10,11... | collective-permute-start | bytes 11010056 | tf_op jit(solution)/shard_map/ppermute | solution.py:21
  63.4 42.5 %all-to-all-start.1 = ((bf16[32,8,1792]{2,1,0:T(8,128)(2,1)}), bf16[32,8,1792]{2,1,0:T(8,128)(2,1)}, u32[]{:S(2)}, u32[]{:S(2)}) async-start(bf16[32,8,1792]{2,1,0:T(8,128)(2,1)} %fusion), calls=%async_computation.1 | async-start | bytes 1835008 | tf_op jit(solution)/shard_map/all_to_all | solution.py:247
  71.7 27.9 %collective-permute-start.6 = (bf16[192,1792]{1,0:T(8,128)(2,1)}, bf16[192,1792]{1,0:T(8,128)(2,1)S(1)}, u32[]{:S(2)}, u32[]{:S(2)}) collective-permute-start(bf16[192,1792]{1,0:T(8,128)(2,1)} %collective-permute-done.5.refs_2_), channel_id=1, source_target_pairs={{0,32},{32,64},{64,96},{96,0},{1,33},{33,65},{65,97},{97,1},{2,34}... | collective-permute-start | bytes 2064392 | tf_op jit(solution)/shard_map/ppermute | solution.py:17
  71.8 27.8 %collective-permute-start.8 = (bf16[192,1792]{1,0:T(8,128)(2,1)}, bf16[192,1792]{1,0:T(8,128)(2,1)S(1)}, u32[]{:S(2)}, u32[]{:S(2)}) collective-permute-start(bf16[192,1792]{1,0:T(8,128)(2,1)} %collective-permute-done.7.refs_5_), channel_id=1, source_target_pairs={{0,96},{32,0},{64,32},{96,64},{1,97},{33,1},{65,33},{97,65},{2,98}... | collective-permute-start | bytes 2064392 | tf_op jit(solution)/shard_map/ppermute | solution.py:17
  102.2 15.2 %copy-start.4 = (bf16[256,1792]{1,0:T(8,128)(2,1)S(1)}, bf16[256,1792]{1,0:T(8,128)(2,1)}, u32[]{:S(2)}) copy-start(bf16[256,1792]{1,0:T(8,128)(2,1)} %copy-done.3) | copy-start | bytes 2752516
  102.3 5.8 %collective-permute-start.11 = (bf16[384,256]{1,0:T(8,128)(2,1)S(1)}, bf16[384,256]{1,0:T(8,128)(2,1)S(1)}, u32[]{:S(2)}, u32[]{:S(2)}) collective-permute-start(bf16[384,256]{1,0:T(8,128)(2,1)S(1)} %far_hidden.2.refs_0_), channel_id=1, source_target_pairs={{0,32},{32,64},{64,96},{96,0},{1,33},{33,65},{65,97},{97,1},{2,34}... | collective-permute-start | bytes 589832 | tf_op jit(solution)/shard_map/ppermute | solution.py:17
  102.3 6.4 %collective-permute-start.12 = (bf16[384,256]{1,0:T(8,128)(2,1)S(1)}, bf16[384,256]{1,0:T(8,128)(2,1)S(1)}, u32[]{:S(2)}, u32[]{:S(2)}) collective-permute-start(bf16[384,256]{1,0:T(8,128)(2,1)S(1)} %far_hidden.2.refs_0_), channel_id=1, source_target_pairs={{0,96},{32,0},{64,32},{96,64},{1,97},{33,1},{65,33},{97,65},{2,98}... | collective-permute-start | bytes 589832 | tf_op jit(solution)/shard_map/ppermute | solution.py:17
  105.0 7.4 %collective-permute-start.13 = (bf16[384,256]{1,0:T(8,128)(2,1)S(1)}, bf16[384,256]{1,0:T(8,128)(2,1)}, u32[]{:S(2)}, u32[]{:S(2)}) collective-permute-start(bf16[384,256]{1,0:T(8,128)(2,1)S(1)} %far_hidden.2.refs_0_), channel_id=1, source_target_pairs={{0,64},{32,96},{64,0},{96,32},{1,65},{33,97},{65,1},{97,33},{2,66}... | collective-permute-start | bytes 589832 | tf_op jit(solution)/shard_map/ppermute | solution.py:17
  108.1 0.7 copy-start.8
  108.7 0.7 copy-start.10
  112.4 25.2 %collective-permute-start.15 = (bf16[128,1792]{1,0:T(8,128)(2,1)S(1)}, bf16[128,1792]{1,0:T(8,128)(2,1)S(1)}, u32[]{:S(2)}, u32[]{:S(2)}) collective-permute-start(bf16[128,1792]{1,0:T(8,128)(2,1)S(1)} %get-tuple-element.79.refs_1_), channel_id=1, source_target_pairs={{0,96},{32,0},{64,32},{96,64},{1,97},{33,1},{65,33},{97,65},{2,98}... | collective-permute-start | bytes 1376264 | tf_op jit(solution)/shard_map/ppermute | solution.py:17
  114.7 29.9 %collective-permute-start.18 = (bf16[128,1792]{1,0:T(8,128)(2,1)S(1)}, bf16[128,1792]{1,0:T(8,128)(2,1)}, u32[]{:S(2)}, u32[]{:S(2)}) collective-permute-start(bf16[128,1792]{1,0:T(8,128)(2,1)S(1)} %get-tuple-element.79.refs_1_), channel_id=1, source_target_pairs={{0,32},{32,64},{64,96},{96,0},{1,33},{33,65},{65,97},{97,1},{2,34}... | collective-permute-start | bytes 1376264 | tf_op jit(solution)/shard_map/ppermute | solution.py:17
  114.7 22.9 %collective-permute-start.14 = (bf16[128,1792]{1,0:T(8,128)(2,1)S(1)}, bf16[128,1792]{1,0:T(8,128)(2,1)}, u32[]{:S(2)}, u32[]{:S(2)}) collective-permute-start(bf16[128,1792]{1,0:T(8,128)(2,1)S(1)} %get-tuple-element.78.refs_0_), channel_id=1, source_target_pairs={{0,32},{32,64},{64,96},{96,0},{1,33},{33,65},{65,97},{97,1},{2,34}... | collective-permute-start | bytes 1376264 | tf_op jit(solution)/shard_map/ppermute | solution.py:17
  114.7 29.9 %collective-permute-start.19 = (bf16[128,1792]{1,0:T(8,128)(2,1)S(1)}, bf16[128,1792]{1,0:T(8,128)(2,1)}, u32[]{:S(2)}, u32[]{:S(2)}) collective-permute-start(bf16[128,1792]{1,0:T(8,128)(2,1)S(1)} %get-tuple-element.78.refs_0_), channel_id=1, source_target_pairs={{0,96},{32,0},{64,32},{96,64},{1,97},{33,1},{65,33},{97,65},{2,98}... | collective-permute-start | bytes 1376264 | tf_op jit(solution)/shard_map/ppermute | solution.py:17
  117.4 0.9 copy-start.9
  118.4 0.9 copy-start.11
  124.8 37.8 %all-to-all-start.2 = ((bf16[32,16,1792]{2,1,0:T(8,128)(2,1)}), bf16[32,16,1792]{2,1,0:T(8,128)(2,1)}, u32[]{:S(2)}, u32[]{:S(2)}) async-start(bf16[32,16,1792]{2,1,0:T(8,128)(2,1)} %bitcast.30), calls=%async_computation.2 | async-start | bytes 3670016 | tf_op jit(solution)/shard_map/all_to_all | solution.py:247
  137.6 12.5 %collective-permute-start.16 = (bf16[128,1792]{1,0:T(8,128)(2,1)}, bf16[128,1792]{1,0:T(8,128)(2,1)S(1)}, u32[]{:S(2)}, u32[]{:S(2)}) collective-permute-start(bf16[128,1792]{1,0:T(8,128)(2,1)} %collective-permute-done.14.refs_2_), channel_id=1, source_target_pairs={{0,32},{32,64},{64,96},{96,0},{1,33},{33,65},{65,97},{97,1},{2,34}... | collective-permute-start | bytes 1376264 | tf_op jit(solution)/shard_map/ppermute | solution.py:17
  137.7 12.4 %collective-permute-start.17 = (bf16[128,1792]{1,0:T(8,128)(2,1)S(1)}, bf16[128,1792]{1,0:T(8,128)(2,1)S(1)}, u32[]{:S(2)}, u32[]{:S(2)}) collective-permute-start(bf16[128,1792]{1,0:T(8,128)(2,1)S(1)} %collective-permute-done.15.refs_5_), channel_id=1, source_target_pairs={{0,96},{32,0},{64,32},{96,64},{1,97},{33,1},{65,33},{97,65},{2,98}... | collective-permute-start | bytes 1376264 | tf_op jit(solution)/shard_map/ppermute | solution.py:17
  149.9 12.7 %copy-start.7 = (s32[320,1]{1,0:T(8,128)S(1)}, s32[320,1]{1,0:T(8,128)}, u32[]{:S(2)}) copy-start(s32[320,1]{1,0:T(8,128)} %select_n.147.slot_ref) | copy-start | bytes 3844
  152.4 13.3 %collective-permute-start.21 = (bf16[256,256]{1,0:T(8,128)(2,1)S(1)}, bf16[256,256]{1,0:T(8,128)(2,1)S(1)}, u32[]{:S(2)}, u32[]{:S(2)}) collective-permute-start(bf16[256,256]{1,0:T(8,128)(2,1)S(1)} %far_hidden.3.refs_0_), channel_id=1, source_target_pairs={{0,32},{32,64},{64,96},{96,0},{1,33},{33,65},{65,97},{97,1},{2,34}... | collective-permute-start | bytes 393224 | tf_op jit(solution)/shard_map/ppermute | solution.py:17
  153.1 12.7 %collective-permute-start.22 = (bf16[256,256]{1,0:T(8,128)(2,1)S(1)}, bf16[256,256]{1,0:T(8,128)(2,1)S(1)}, u32[]{:S(2)}, u32[]{:S(2)}) collective-permute-start(bf16[256,256]{1,0:T(8,128)(2,1)S(1)} %far_hidden.3.refs_0_), channel_id=1, source_target_pairs={{0,96},{32,0},{64,32},{96,64},{1,97},{33,1},{65,33},{97,65},{2,98}... | collective-permute-start | bytes 393224 | tf_op jit(solution)/shard_map/ppermute | solution.py:17
  155.2 10.6 %collective-permute-start.23 = (bf16[256,256]{1,0:T(8,128)(2,1)S(1)}, bf16[256,256]{1,0:T(8,128)(2,1)S(1)}, u32[]{:S(2)}, u32[]{:S(2)}) collective-permute-start(bf16[256,256]{1,0:T(8,128)(2,1)S(1)} %far_hidden.3.refs_0_), channel_id=1, source_target_pairs={{0,64},{32,96},{64,0},{96,32},{1,65},{33,97},{65,1},{97,33},{2,66}... | collective-permute-start | bytes 393224 | tf_op jit(solution)/shard_map/ppermute | solution.py:17
  169.3 21.9 %copy-start.2 = (bf16[320,1792]{1,0:T(8,128)(2,1)S(1)}, bf16[320,1792]{1,0:T(8,128)(2,1)}, u32[]{:S(2)}) copy-start(bf16[320,1792]{1,0:T(8,128)(2,1)} %collected.1.total_ref) | copy-start | bytes 3440644
  169.3 21.9 %copy-start.6 = (f32[320,1]{1,0:T(8,128)S(1)}, f32[320,1]{1,0:T(8,128)}, u32[]{:S(2)}) copy-start(f32[320,1]{1,0:T(8,128)} %copy-done.5) | copy-start | bytes 3844
  169.3 21.9 %all-to-all-start.3 = ((bf16[32,8,1792]{2,1,0:T(8,128)(2,1)}), bf16[32,8,1792]{2,1,0:T(8,128)(2,1)S(1)}, u32[]{:S(2)}, u32[]{:S(2)}) async-start(bf16[32,8,1792]{2,1,0:T(8,128)(2,1)} %bitcast.29), calls=%async_computation.3 | async-start | bytes 1835008 | tf_op jit(solution)/shard_map/all_to_all | solution.py:247
  175.5 17.6 %copy-start.1 = (bf16[320,1792]{1,0:T(8,128)(2,1)S(1)}, bf16[320,1792]{1,0:T(8,128)(2,1)}, u32[]{:S(2)}) copy-start(bf16[320,1792]{1,0:T(8,128)(2,1)} %param.7) | copy-start | bytes 3440644
